TPU v7x, 32 devices: a whole 2x2x4 slice. The times are simulated.
32 devices in a mesh: rel: 2 (over core), ent: 16 (over z, y, x).
Axes of the slice: x: 2, y: 2, z: 4, core: 2. Of those that a mesh axis runs over, the one named last changes fastest.
Arguments:
- facts: bfloat16 [16, 2048, 2048], P('rel', 'ent'), may hold values from -6 to 6
- observed: int32 [16, 2048, 158], P('rel', 'ent'), may hold values from 0 to 8191
- factors: bfloat16 [2048, 128], P('ent'), may hold values from -0.59765625 to 0.59765625
- cores: bfloat16 [16, 128, 128], P('rel'), may hold values from -6 to 6
Outputs:
- grad_factors: float32 [2048, 128], P('ent')
- grad_cores: float32 [16, 128, 128], P('rel')
All inputs are finite; a program needn't handle non-finite values.
Results may differ from a plain program's by a relative error of at most 0.0008.
Values may be sent and summed in bfloat16 or wider, within the bound.
No kernel may reach another device: no remote copies, remote signals or barrier semaphores. Data moves between devices by JAX's collectives and lax.ppermute only.
A program may use at most 128 MiB of HBM per device.

v0:
```python
import jax
import jax.numpy as jnp
from jax import lax
from jax.sharding import PartitionSpec as P


def unpack(words, count):
    shifts = jnp.arange(13, dtype=jnp.int32)
    bits = jnp.bitwise_and(jnp.right_shift(words[..., None], shifts), 1)
    flat = bits.reshape(words.shape[:-1] + (words.shape[-1] * 13,))
    return flat[..., :count].astype(jnp.bfloat16)


def per_device(facts, observed, factors, cores):
    n_all = facts.shape[2]
    rel_loc, ent_loc, rank = (cores.shape[0], factors.shape[0], factors.shape[1])
    n_rel = rel_loc * lax.axis_size("rel")
    mask = unpack(observed, n_all)
    left = jnp.einsum("ir,krs->kis", factors, cores, preferred_element_type=jnp.float32).astype(
        jnp.bfloat16
    )
    piece = lax.all_gather(factors, "ent", axis=0, tiled=True)
    right = jnp.einsum("js,krs->kjr", piece, cores, preferred_element_type=jnp.float32).astype(
        jnp.bfloat16
    )
    model = jnp.einsum("kis,js->kij", left, piece, preferred_element_type=jnp.float32)
    data = facts.astype(jnp.float32)
    marks = mask.astype(jnp.float32)
    err = (marks * (model - data)).astype(jnp.bfloat16)
    own_rows = jnp.einsum("kij,kjr->ir", err, right, preferred_element_type=jnp.float32)
    block = jnp.einsum("kij,kis->js", err, left, preferred_element_type=jnp.float32)
    all_rows = block
    pull_sum = jnp.einsum("kij,js->kis", err, piece, preferred_element_type=jnp.float32)
    own_rows, all_rows, pull_sum = (own_rows, all_rows, pull_sum)
    offset = lax.axis_index("ent") * ent_loc
    mine = lax.dynamic_slice_in_dim(all_rows, offset, ent_loc, 0)
    partial_value = lax.dynamic_update_slice_in_dim(all_rows, mine + own_rows, offset, 0)
    rel_count = lax.axis_size("rel")
    ent_count = lax.axis_size("ent")
    sub_rows = ent_loc // rel_count
    arranged = (
        partial_value.reshape(ent_count, rel_count, sub_rows, rank)
        .transpose(1, 0, 2, 3)
        .reshape(n_all, rank)
    )
    share_rows = lax.psum_scatter(arranged, ("rel", "ent"), scatter_dimension=0, tiled=True)
    owned = lax.all_gather(share_rows, "rel", axis=0, tiled=True)
    grad_factors = owned / jnp.sqrt(jnp.float32(n_all * n_rel))
    pull = pull_sum.astype(jnp.bfloat16)
    core_part = jnp.einsum("ir,kis->krs", factors, pull, preferred_element_type=jnp.float32)
    core_grad = lax.psum(core_part, "ent")
    grad_cores = core_grad * (rank / n_all)
    return (grad_factors, grad_cores)


def solution(mesh):
    return jax.shard_map(
        per_device,
        mesh=mesh,
        in_specs=(
            P("rel", "ent", None),
            P("rel", "ent", None),
            P("ent", None),
            P("rel", None, None),
        ),
        out_specs=(P("ent", None), P("rel", None, None)),
        check_vma=False,
    )
```

profile of v0, /device:TPU:0, one launch (start us, length us, event | category | flops | bytes accessed | tf_op | source)
XLA Modules:
  0.0 265.3 jit_solution(4294253816372640306)
XLA Ops:
  8.0 0.0 copy-start
  8.0 0.0 all-reduce.2.cloned.1.call-start
  8.1 45.7 %all_gather.6 = bf16[2048,128]{1,0:T(8,128)(2,1)S(1)} all-gather(bf16[128,128]{1,0:T(8,128)(2,1)} %param.6), channel_id=1, replica_groups=mesh['rel'=2,'ent'=16] {'ent'}, dimensions={0}, use_global_device_ids=true | all-gather | bytes 557056 | tf_op jit(solution)/shard_map/all_gather | solution.py:22
  53.7 0.0 copy-done
  53.7 1.0 fusion.2
  54.8 4.5 %fusion.8 = f32[8,128,2048]{2,1,0:T(8,128)} fusion(bf16[8,128,128]{1,2,0:T(8,128)(2,1)S(1)} %fusion.2, bf16[2048,128]{1,0:T(8,128)(2,1)S(1)} %all_gather.6), kind=kOutput, calls=%fused_computation.15 | convolution fusion | flops 536870912 | bytes 9175040 | tf_op jit(solution)/shard_map/kis,js->kij/dot_general | solution.py:26
  59.3 9.3 %copy.23 = f32[8,128,2048]{1,0,2:T(8,128)} copy(f32[8,128,2048]{2,1,0:T(8,128)} %fusion.8) | data formatting | bytes 16777216 | tf_op jit(solution)/shard_map/kis,js->kij/dot_general | solution.py:26
  68.6 0.0 copy-start.2
  68.6 6.7 %copy.22 = bf16[8,128,2048]{1,0,2:T(8,128)(2,1)} copy(bf16[8,128,2048]{2,1,0:T(8,128)(2,1)} %param.4) | data formatting | bytes 8388608 | tf_op args[0]
  75.3 0.2 shift_right_arithmetic.23
  75.5 0.0 copy-done.2
  75.5 0.0 copy-start.1
  75.5 0.5 shift_right_arithmetic.20
  76.1 2.8 %copy-done.1 = f32[8,128,2048]{1,0,2:T(8,128)S(1)} copy-done((f32[8,128,2048]{1,0,2:T(8,128)S(1)}, f32[8,128,2048]{1,0,2:T(8,128)}, u32[]{:S(2)}) %copy-start.1) | copy-done | bytes 8388632
  78.9 8.5 %multiply_convert_fusion = bf16[8,128,2048]{1,0,2:T(8,128)(2,1)} fusion(f32[8,128,2048]{1,0,2:T(8,128)S(1)} %copy-done.1, bf16[8,128,2048]{1,0,2:T(8,128)(2,1)} %copy.22, s32[8,128,2054]{1,0,2:T(8,128)S(1)} %bitcast.40, s32[2048]{0:T(1024)S(1)} %slice.6), kind=kLoop, calls=%fused_computation.3 | loop fusion | flops 16777216 | bytes 25174016 | tf_op jit(solution)/shard_map/convert_element_type | solution.py:29
  87.4 0.0 copy-start.3
  87.4 6.7 %copy.29 = bf16[8,128,2048]{2,1,0:T(8,128)(2,1)} copy(bf16[8,128,2048]{1,0,2:T(8,128)(2,1)} %multiply_convert_fusion) | data formatting | bytes 8388608 | tf_op jit(solution)/shard_map/convert_element_type | solution.py:29
  94.1 0.0 copy-done.3
  94.1 4.5 %convolution_bitcast_fusion.1 = f32[8,128,128]{1,2,0:T(8,128)} fusion(bf16[8,128,2048]{2,1,0:T(8,128)(2,1)} %copy.29, bf16[2048,128]{1,0:T(8,128)(2,1)S(1)} %all_gather.6, bf16[128,128]{1,0:T(8,128)(2,1)S(1)} %copy-done.3), kind=kOutput, calls=%fused_computation.6 | convolution fusion | flops 570556416 | bytes 5275648 | tf_op jit(solution)/shard_map/ir,kis->krs/dot_general | solution.py:50
  98.6 0.0 all-reduce.2.cloned.1.call-update
  98.6 0.0 reduce-scatter.2.cloned.1.call-start
  98.7 3.6 %convolution_bitcast_fusion = f32[2048,128]{1,0:T(8,128)S(1)} fusion(bf16[8,128,2048]{2,1,0:T(8,128)(2,1)} %copy.29, bf16[8,128,128]{1,2,0:T(8,128)(2,1)S(1)} %fusion.2), kind=kOutput, calls=%fused_computation.5 | convolution fusion | flops 536870912 | bytes 5505024 | tf_op jit(solution)/shard_map/kij,kis->js/dot_general | solution.py:31
  102.3 3.2 %convert_bitcast_fusion = bf16[8,2048,128]{1,2,0:T(8,128)(2,1)} fusion(bf16[8,128,128]{2,1,0:T(8,128)(2,1)S(1)} %copy-done, bf16[2048,128]{1,0:T(8,128)(2,1)S(1)} %all_gather.6), kind=kOutput, calls=%fused_computation.4 | convolution fusion | flops 538968064 | bytes 4980736 | tf_op jit(solution)/shard_map/js,krs->kjr/dot_general | solution.py:23
  105.5 6.8 %copy.36 = bf16[8,2048,128]{2,0,1:T(8,128)(2,1)} copy(bf16[8,2048,128]{1,2,0:T(8,128)(2,1)} %convert_bitcast_fusion) | data formatting | bytes 8388608 | tf_op jit(solution)/shard_map/convert_element_type | solution.py:23
  112.3 4.8 %fusion.4 = f32[2048,128]{1,0:T(8,128)S(1)} fusion(f32[2048,128]{1,0:T(8,128)S(1)} %convolution_bitcast_fusion, s32[]{:T(128)S(6)} %select_n.4, bf16[8,128,2048]{1,0,2:T(8,128)(2,1)} %multiply_convert_fusion, bf16[8,2048,128]{2,0,1:T(8,128)(2,1)} %copy.36), kind=kOutput, calls=%fused_computation.12 | convolution fusion | flops 536887296 | bytes 8519684 | tf_op jit(solution)/shard_map/kij,kjr->ir/dot_general | solution.py:30
  117.1 1.0 copy.28
  118.2 0.0 reduce-scatter.2.cloned.1.call-update
  118.2 85.7 %all-reduce.2.cloned.1.call-done = f32[8,128,128]{1,2,0:T(8,128)} async-done(((f32[8,128,128]{1,2,0:T(8,128)}), f32[8,128,128]{1,2,0:T(8,128)}) %all-reduce.2.cloned.1.call-update) | async-done | bytes 524304 | tf_op jit(solution)/shard_map/psum | solution.py:51
  203.9 1.1 broadcast_multiply_fusion
  205.0 1.0 copy.31
  206.0 49.2 %reduce-scatter.2.cloned.1.call-done = f32[64,128]{1,0:T(8,128)} async-done(((f32[2048,128]{1,0:T(8,128)}), f32[64,128]{1,0:T(8,128)}) %reduce-scatter.2.cloned.1.call-update) | async-done | bytes 32784 | tf_op jit(solution)/shard_map/reduce_scatter | solution.py:46
  255.1 2.1 all_gather.7
  257.2 0.6 broadcast_multiply_fusion.1
  (2 shorter events, 0.0 us)
Async XLA Ops:
  8.0 45.8 %copy-start = (bf16[8,128,128]{2,1,0:T(8,128)(2,1)S(1)}, bf16[8,128,128]{2,1,0:T(8,128)(2,1)}, u32[]{:S(2)}) copy-start(bf16[8,128,128]{2,1,0:T(8,128)(2,1)} %param.7) | copy-start | bytes 786436
  8.0 195.9 %all-reduce.2.cloned.1.call-start = ((), (), s32[]{:S(2)}) async-start(), calls=%async_computation.2 | async-start | bytes 1048576 | tf_op jit(solution)/shard_map/psum | solution.py:51
  68.6 7.0 %copy-start.2 = (s32[8,128,158]{1,0,2:T(8,128)S(1)}, s32[8,128,158]{1,0,2:T(8,128)}, u32[]{:S(2)}) copy-start(s32[8,128,158]{1,0,2:T(8,128)} %param.5) | copy-start | bytes 1941508
  75.5 3.4 %copy-start.1 = (f32[8,128,2048]{1,0,2:T(8,128)S(1)}, f32[8,128,2048]{1,0,2:T(8,128)}, u32[]{:S(2)}) copy-start(f32[8,128,2048]{1,0,2:T(8,128)} %copy.23) | copy-start | bytes 25165828
  87.4 6.7 %copy-start.3 = (bf16[128,128]{1,0:T(8,128)(2,1)S(1)}, bf16[128,128]{1,0:T(8,128)(2,1)}, u32[]{:S(2)}) copy-start(bf16[128,128]{1,0:T(8,128)(2,1)} %param.6) | copy-start | bytes 98308
  98.6 156.5 %reduce-scatter.2.cloned.1.call-start = ((), (), s32[]{:S(2)}) async-start(), calls=%async_computation.1 | async-start | bytes 1081344 | tf_op jit(solution)/shard_map/reduce_scatter | solution.py:46
Sparse Core Ops, SparseCore 0:
  98.7 105.1 all-reduce.1
Sparse Core Ops, SparseCore 1:
  118.3 136.8 reduce-scatter.1
where the time goes:
time: 266 us; the launch traced here: 265 us
  waiting for transfers between devices  135 us (51%)
  blocking collectives  47.8 us (18%)
  local copies, waits for them, and re-layouts  35.1 us (13%)
  matrix products  21.7 us (8%)
  between operations  15.6 us (6%)
  other arithmetic  10.2 us (4%)
    psum x1, waiting for transfers between devices, per_device(): core_grad = lax.psum(core_part, 'ent')  85.7 us
    reduce_scatter x1, waiting for transfers between devices, per_device(): lax.psum_scatter(arranged, ('rel', 'ent'), scatter_dimension=0, tiled=True)  49.2 us
    all_gather x1, blocking collectives, per_device(): piece = lax.all_gather(factors, 'ent', axis=0, tiled=True)  45.7 us
    unnamed x10, local copies, waits for them, and re-layouts  10.6 us
    dot_general x1, local copies, waits for them, and re-layouts, per_device(): jnp.einsum('kis,js->kij', left, piece, preferred_element_type=jnp.float32)  9.29 us
    convert_element_type x1, other arithmetic, per_device(): err = (marks * (model - data)).astype(jnp.bfloat16)  8.5 us
    convert_element_type x1, local copies, waits for them, and re-layouts, per_device(): jnp.einsum('js,krs->kjr', piece, cores, preferred_element_type=jnp.float32)  6.78 us
    convert_element_type x1, local copies, waits for them, and re-layouts, per_device(): err = (marks * (model - data)).astype(jnp.bfloat16)  6.69 us
  transfers between devices with their start and end apart: 2, of which 2 were waited for; matrix products, arithmetic and copies ran while one was open for 8% of the time, Pallas kernels for 0%

commit v1 on v0

v1 whole, which is shorter than its diff:
```python
import functools

import jax
import jax.numpy as jnp
from jax import lax
from jax.experimental import pallas as pl
from jax.experimental.pallas import tpu as pltpu
from jax.sharding import PartitionSpec as P


BITS = 13
LANES = 128
F32 = jnp.float32
BF16 = jnp.bfloat16
MIB = 1 << 20


def swap(x, axis, size, distance):
    return lax.ppermute(x, axis, [(i, i ^ distance) for i in range(size)])


def nt(a, b):
    return lax.dot_general(a, b, (((1,), (1,)), ((), ())), preferred_element_type=F32)


def tn(a, b):
    return lax.dot_general(a, b, (((0,), (0,)), ((), ())), preferred_element_type=F32)


def nn(a, b):
    return jnp.dot(a, b, preferred_element_type=F32)


def chip_of(me, slot, low, high):
    return jnp.bitwise_xor(me, (slot % high) * low + slot // high)


def take_pair(pieces, pair, scratch, size):
    inside = pieces[0].shape[0] // size
    for p, piece in enumerate(pieces):
        for i in range(inside):

            @pl.when(pair == p * inside + i)
            def _():
                scratch[...] = piece[i * size : (i + 1) * size, :]


def add_err(pair, me, low, high, left_ref, piece, words_ref, facts, err_ref, acc_ref):
    relations, half = words_ref.shape[0], words_ref.shape[1]
    rows, width = 2 * half, piece.shape[0] // 2
    lane = lax.broadcasted_iota(jnp.int32, (half, LANES), 1)
    words, bits, blocks = [], [], []
    for s in range(2):
        chip = chip_of(me, 2 * pair + s, low, high)
        column = lax.rem(chip, BITS) * LANES + lane
        word = jnp.right_shift(column * 5042, 16)
        words.append(word)
        bits.append(jnp.left_shift(1, column - word * BITS))
        blocks.append(pl.multiple_of(lax.div(chip, BITS) * LANES, LANES))
    for k in range(relations):
        at = slice(k * rows, (k + 1) * rows)
        model = nt(left_ref[at, :], piece)
        tiles = []
        for s in range(2):
            marks = jnp.take_along_axis(
                words_ref[k, :, pl.ds(blocks[s], LANES)], words[s], axis=1
            )
            data = facts[s][k].astype(F32)
            diff = model[:, s * width : (s + 1) * width] - data
            top = jnp.where((marks & bits[s]) != 0, diff[:half], 0.0)
            low_bits = jnp.left_shift(bits[s], 16)
            bottom = jnp.where((marks & low_bits) != 0, diff[half:], 0.0)
            tiles.append(jnp.concatenate([top, bottom], axis=0).astype(BF16))
        err = jnp.concatenate(tiles, axis=1)
        err_ref[0, at, :] = err
        acc_ref[at, :] += nn(err, piece)


def early_kernel(
    low, high, me_ref, words_ref, facts0_ref, facts1_ref, own_ref, cores_ref, column_ref,
    err_ref, left_ref, acc_ref,
):
    pair = pl.program_id(0)
    rows = own_ref.shape[0]

    @pl.when(pair == 0)
    def _():
        acc_ref[...] = jnp.zeros_like(acc_ref)
        for k in range(cores_ref.shape[0]):
            left_ref[k * rows : (k + 1) * rows, :] = nn(own_ref[...], cores_ref[k]).astype(BF16)

    add_err(
        pair, me_ref[0], low, high, left_ref, column_ref[...], words_ref,
        (facts0_ref, facts1_ref), err_ref, acc_ref,
    )


def late_kernel(
    low, high, first, me_ref, words_ref, facts0_ref, facts1_ref, left_ref, part_ref, _, *rest
):
    pieces, (err_ref, *pulls) = rest[: low - 1], rest[low - 1 : -2]
    piece_ref, acc_ref = rest[-2:]
    step = pl.program_id(0)

    @pl.when(step == 0)
    def _():
        acc_ref[...] = part_ref[...]

    take_pair(pieces, step, piece_ref, piece_ref.shape[0])
    add_err(
        step + first, me_ref[0], low, high, left_ref, piece_ref[...], words_ref,
        (facts0_ref, facts1_ref), err_ref, acc_ref,
    )

    @pl.when(step == pl.num_programs(0) - 1)
    def _():
        size = pulls[0].shape[0]
        far = me_ref[0] // low
        for d in range(high):
            at = pl.multiple_of(jnp.bitwise_xor(far, d) * size, size)
            pulls[d][...] = acc_ref[pl.ds(at, size), :].astype(BF16)


def rows_kernel(low, rel, me_ref, err_ref, left_ref, cores_ref, *rest):
    pieces, outs = rest[:low], rest[low : low + rel]
    piece_ref, _, total_ref, own_ref = rest[low + rel :]
    mine = me_ref[1]
    step, pairs = pl.program_id(0), pl.num_programs(0)
    pair = lax.rem(step + 1, pairs)

    @pl.when(step == 0)
    def _():
        own_ref[...] = jnp.zeros_like(own_ref)

    take_pair(pieces, pair, piece_ref, piece_ref.shape[0])
    rank = left_ref.shape[1]
    rows = piece_ref.shape[0] // 2
    relations = cores_ref.shape[0] // rank
    total_ref[...] = tn(err_ref[0], left_ref[...])
    own = own_ref[...]
    for k in range(relations):
        span = slice(k * rank, (k + 1) * rank)
        right = nt(piece_ref[...], cores_ref[span, :]).astype(BF16)
        own = own + nn(err_ref[0, k * rows : (k + 1) * rows, :], right)
    own_ref[...] = own

    @pl.when(step == pairs - 1)
    def _():
        total_ref[:rows, :] += own_ref[...]

    sub = rows // rel
    for h in range(rel):
        piece = jnp.bitwise_xor(mine, h) * sub
        for s in range(2):
            src = pl.multiple_of(piece + s * rows, sub)
            dst = pl.multiple_of((2 * pair + s) * sub, sub)
            outs[h][pl.ds(dst, sub), :] = total_ref[pl.ds(src, sub), :]


def merge_kernel(low, high, rel, me_ref, column_ref, *rest):
    pulls, shares, outs = rest[:high], rest[high : high + rel], rest[high + rel : -1]
    total_ref = rest[-1]
    rank = column_ref.shape[1]
    rows = column_ref.shape[0] // high
    near = jnp.bitwise_and(me_ref[0], low - 1)
    for k in range(pulls[0].shape[0] // rows):
        acc = tn(column_ref[:rows, :], pulls[0][k * rows : (k + 1) * rows, :])
        for d in range(1, high):
            acc = acc + tn(
                column_ref[d * rows : (d + 1) * rows, :], pulls[d][k * rows : (k + 1) * rows, :]
            )
        total_ref[k * rank : (k + 1) * rank, :] = acc
    size = total_ref.shape[0] // low
    block = shares[0].shape[0] // low
    for q in range(low):
        part = shares[0][q * block : (q + 1) * block, :]
        for h in range(1, rel):
            part = part + shares[h][q * block : (q + 1) * block, :]
        outs[q][:block, :] = part
        src = pl.multiple_of(jnp.bitwise_xor(near, q) * size, size)
        outs[q][block:, :] = total_ref[pl.ds(src, size), :]


def near_kernel(low, high, scale, *rest):
    parts, outs = rest[:low], rest[low:]
    total = parts[0][...]
    for q in range(1, low):
        total = total + parts[q][...]
    size = total.shape[0] - outs[0].shape[0]
    sub = size // (high - 1)
    core = total[high * sub :, :] * scale
    for d in range(high):
        outs[d][:sub, :] = total[d * sub : (d + 1) * sub, :]
        outs[d][sub:, :] = core


def far_kernel(low, high, root, me_ref, *rest):
    parts, (owned_ref, column_ref) = rest[:high], rest[high:]
    sub, size = owned_ref.shape[0], column_ref.shape[0] // high
    far = me_ref[0] // low
    total = parts[0][:sub, :]
    for d in range(1, high):
        total = total + parts[d][:sub, :]
    owned_ref[...] = total / jnp.sqrt(F32(root))
    for d in range(high):
        at = pl.multiple_of(jnp.bitwise_xor(far, d) * size, size)
        column_ref[pl.ds(at, size), :] = parts[d][sub:, :]


def gradients(facts, observed, factors, cores):
    relations, rows, n_all = facts.shape
    rank = factors.shape[1]
    rel, ent = lax.axis_size("rel"), lax.axis_size("ent")
    low = 1 << ((ent.bit_length() - 1) // 2)
    high = ent // low
    per = relations // high
    here = lax.axis_index("rel")
    me = jnp.stack([lax.axis_index("ent"), here]).astype(jnp.int32)

    def near_swap(x, d):
        return swap(x, "ent", ent, d)

    def far_swap(x, d):
        return swap(x, "ent", ent, d * low)

    column = jnp.concatenate([factors] + [far_swap(factors, d) for d in range(1, high)])
    nears = [near_swap(column, q) for q in range(1, low)]

    half = rows // 2
    packed = observed[:, :half] | jnp.left_shift(observed[:, half:], 16)
    spare = -packed.shape[2] % LANES
    packed = jnp.pad(packed, ((0, 0), (0, 0), (0, spare)))

    def whole(shape):
        return pl.BlockSpec(shape, lambda t, me: (0,) * len(shape))

    def facts_block(first, s):
        return pl.BlockSpec(
            (relations, rows, rows),
            lambda t, me: (0, 0, chip_of(me[0], 2 * (t + first) + s, low, high)),
        )

    stack, pairs, first = relations * rows, ent // 2, high // 2
    wide = 2 * rows
    shape = jax.ShapeDtypeStruct
    cost = lambda share: pl.CostEstimate(
        flops=int(4 * stack * n_all * rank * share),
        bytes_accessed=int(4 * stack * n_all * share),
        transcendentals=0,
    )
    err, left, part = pl.pallas_call(
        functools.partial(early_kernel, low, high),
        grid_spec=pltpu.PrefetchScalarGridSpec(
            num_scalar_prefetch=1,
            grid=(first,),
            in_specs=[
                whole(packed.shape),
                facts_block(0, 0),
                facts_block(0, 1),
                whole((rows, rank)),
                whole(cores.shape),
                pl.BlockSpec((wide, rank), lambda t, me: (t, 0)),
            ],
            out_specs=[
                pl.BlockSpec((1, stack, wide), lambda t, me: (t, 0, 0)),
                whole((stack, rank)),
                whole((stack, rank)),
            ],
        ),
        out_shape=[
            shape((pairs, stack, wide), BF16),
            shape((stack, rank), BF16),
            shape((stack, rank), F32),
        ],
        cost_estimate=cost(first / pairs),
        compiler_params=pltpu.CompilerParams(vmem_limit_bytes=16 * MIB),
        name="early_kernel",
    )(me, packed, facts, facts, factors, cores, column)

    err, *pulls = pl.pallas_call(
        functools.partial(late_kernel, low, high, first),
        grid_spec=pltpu.PrefetchScalarGridSpec(
            num_scalar_prefetch=1,
            grid=(pairs - first,),
            in_specs=[
                whole(packed.shape),
                facts_block(first, 0),
                facts_block(first, 1),
                whole((stack, rank)),
                whole((stack, rank)),
                pl.BlockSpec(memory_space=pl.ANY),
            ]
            + [whole(column.shape)] * (low - 1),
            out_specs=[pl.BlockSpec((1, stack, wide), lambda t, me: (t + first, 0, 0))]
            + [whole((per * rows, rank))] * high,
            scratch_shapes=[pltpu.VMEM((wide, rank), BF16), pltpu.VMEM((stack, rank), F32)],
        ),
        out_shape=[shape(err.shape, BF16)] + [shape((per * rows, rank), BF16)] * high,
        input_output_aliases={6: 0},
        cost_estimate=cost(1 - first / pairs),
        compiler_params=pltpu.CompilerParams(vmem_limit_bytes=16 * MIB),
        name="late_kernel",
    )(me, packed, facts, facts, left, part, err, *nears)

    for d in range(1, high):
        pulls[d] = far_swap(pulls[d], d)

    sub = rows // rel
    rows_call = pl.pallas_call(
        functools.partial(rows_kernel, low, rel),
        grid_spec=pltpu.PrefetchScalarGridSpec(
            num_scalar_prefetch=1,
            grid=(pairs,),
            in_specs=[
                pl.BlockSpec((1, stack, wide), lambda t, me: ((t + 1) % pairs, 0, 0)),
                whole((stack, rank)),
                whole((relations * rank, rank)),
            ]
            + [whole(column.shape)] * low,
            out_specs=[whole((ent * sub, rank))] * rel,
            scratch_shapes=[
                pltpu.VMEM((wide, rank), BF16),
                pltpu.VMEM((wide, relations * rank), BF16),
                pltpu.VMEM((wide, rank), F32),
                pltpu.VMEM((rows, rank), F32),
            ],
        ),
        out_shape=[shape((ent * sub, rank), F32)] * rel,
        cost_estimate=cost(1.5),
        compiler_params=pltpu.CompilerParams(vmem_limit_bytes=16 * MIB),
        name="rows_kernel",
    )
    shares = rows_call(me, err, left, cores.reshape(relations * rank, rank), column, *nears)
    shares = [shares[0]] + [swap(shares[h], "rel", rel, h) for h in range(1, rel)]

    size = per * rank // low
    merged = pl.pallas_call(
        functools.partial(merge_kernel, low, high, rel),
        in_specs=[pl.BlockSpec(memory_space=pltpu.SMEM)]
        + [pl.BlockSpec(memory_space=pltpu.VMEM)] * (1 + high + rel),
        out_shape=[shape((high * sub + size, rank), F32)] * low,
        scratch_shapes=[pltpu.VMEM((per * rank, rank), F32)],
        compiler_params=pltpu.CompilerParams(vmem_limit_bytes=8 * MIB),
        name="merge_kernel",
    )(me, column, *pulls, *shares)
    merged = [merged[0]] + [near_swap(merged[q], q) for q in range(1, low)]

    parts = pl.pallas_call(
        functools.partial(near_kernel, low, high, rank / n_all),
        out_shape=[shape((sub + size, rank), F32)] * high,
        compiler_params=pltpu.CompilerParams(vmem_limit_bytes=6 * MIB),
        name="near_kernel",
    )(*merged)
    parts = [parts[0]] + [far_swap(parts[d], d) for d in range(1, high)]

    owned, core_column = pl.pallas_call(
        functools.partial(far_kernel, low, high, n_all * relations * rel),
        in_specs=[pl.BlockSpec(memory_space=pltpu.SMEM)]
        + [pl.BlockSpec(memory_space=pltpu.VMEM)] * high,
        out_shape=[shape((sub, rank), F32), shape((high * size, rank), F32)],
        compiler_params=pltpu.CompilerParams(vmem_limit_bytes=4 * MIB),
        name="far_kernel",
    )(me, *parts)

    grad_factors = jnp.zeros((rel, sub, rank), F32)
    for h in range(rel):
        piece = owned if h == 0 else swap(owned, "rel", rel, h)
        grad_factors = lax.dynamic_update_index_in_dim(grad_factors, piece, here ^ h, 0)
    grad_factors = grad_factors.reshape(rows, rank)

    grad_cores = jnp.zeros((high, low, size, rank), F32)
    near = lax.axis_index("ent") & (low - 1)
    core_column = core_column.reshape(high, size, rank)
    for q in range(low):
        piece = core_column if q == 0 else near_swap(core_column, q)
        grad_cores = lax.dynamic_update_index_in_dim(grad_cores, piece, near ^ q, 1)
    return grad_factors, grad_cores.reshape(relations, rank, rank)


def solution(mesh):
    return jax.shard_map(
        gradients,
        mesh=mesh,
        in_specs=(
            P("rel", "ent", None),
            P("rel", "ent", None),
            P("ent", None),
            P("rel", None, None),
        ),
        out_specs=(P("ent", None), P("rel", None, None)),
        check_vma=False,
    )
```

time: 266 us -> 71.3 us (0.27)
  waiting for transfers between devices: 135 us -> 22.5 us
  blocking collectives: 47.8 us -> 0 us
  local copies, waits for them, and re-layouts: 35.1 us -> 5.39 us
  starting transfers between devices: 0.08 us -> 25.3 us
  matrix products: 21.7 us -> 0 us
  Pallas kernels: 0 us -> 16.9 us
  between operations: 15.6 us -> 0.86 us
  other arithmetic: 10.2 us -> 0.17 us
    psum x1 -> x0, waiting for transfers between devices: 85.7 us -> none  [per_device(): core_grad = lax.psum(core_part, 'ent')]
    reduce_scatter x1 -> x0, waiting for transfers between devices: 49.2 us -> none  [per_device(): lax.psum_scatter(arranged, ('rel', 'ent'), scatter_dimension=0, tiled=True)]
    all_gather x2 -> x0, blocking collectives: 47.8 us -> none  [the longest x1 45.7 us: per_device(): piece = lax.all_gather(factors, 'ent', axis=0, tiled=True)]
    ppermute x0 -> x20, starting transfers between devices: none -> 25.3 us  [swap(): return lax.ppermute(x, axis, [(i, i ^ distance) for i in range(size)])]
    ppermute x0 -> x20, waiting for transfers between devices: none -> 22.5 us  [swap(): return lax.ppermute(x, axis, [(i, i ^ distance) for i in range(size)])]
    dot_general x6 -> x0, matrix products: 21.7 us -> none  [the longest x1 4.83 us: per_device(): jnp.einsum('kij,kjr->ir', err, right, preferred_element_type=jnp.float32)]
    pallas_call x0 -> x6, Pallas kernels: none -> 16.9 us  [the longest x1 6.95 us: gradients(): rows_call(me, err, left, cores.reshape(relations * rank, rank), column, *...]
    convert_element_type x2 -> x0, local copies, waits for them, and re-layouts: 13.5 us -> none  [the longest x1 6.78 us: per_device(): jnp.einsum('js,krs->kjr', piece, cores, preferred_element_type=jnp.float32)]
  transfers between devices with their start and end apart: 2 -> 20, of which waited for: 2 -> 13; matrix products, arithmetic and copies ran while one was open for 8% -> 4% of each run, Pallas kernels for 0% -> 4%
where the time goes in v1:
time: 71.3 us; the launch traced here: 71.1 us
  starting transfers between devices  25.3 us (35%)
  waiting for transfers between devices  22.5 us (32%)
  Pallas kernels  16.9 us (24%)
  local copies, waits for them, and re-layouts  5.39 us (8%)
  between operations  0.86 us (1%)
    ppermute x20, starting transfers between devices, swap(): return lax.ppermute(x, axis, [(i, i ^ distance) for i in range(size)])  25.3 us
    ppermute x20, waiting for transfers between devices, swap(): return lax.ppermute(x, axis, [(i, i ^ distance) for i in range(size)])  22.5 us
    pallas_call x1, Pallas kernels, gradients(): rows_call(me, err, left, cores.reshape(relations * rank, rank), column, *...  6.95 us
    pallas_call x1, Pallas kernels, gradients(): pl.pallas_call(functools.partial(late_kernel, low, high, first), grid_spe...  5.99 us
    unnamed x15, local copies, waits for them, and re-layouts  3.71 us
    pallas_call x1, Pallas kernels, gradients(): pl.pallas_call(functools.partial(early_kernel, low, high), grid_spec=pltp...  2.55 us
    slice x1, local copies, waits for them, and re-layouts, gradients(): packed = observed[:, :half] | jnp.left_shift(observed[:, half:], 16)  1.53 us
  transfers between devices with their start and end apart: 20, of which 13 were waited for; matrix products, arithmetic and copies ran while one was open for 4% of the time, Pallas kernels for 4%

profile of v1, /device:TPU:0, one launch (start us, length us, event | category | flops | bytes accessed | tf_op | source)
XLA Modules:
  0.0 71.1 jit_solution(6444565805112413687)
XLA Ops:
  0.7 3.1 %collective-permute-start = (bf16[128,128]{1,0:T(8,128)(2,1)}, bf16[128,128]{1,0:T(8,128)(2,1)S(1)}, u32[]{:S(2)}, u32[]{:S(2)}) collective-permute-start(bf16[128,128]{1,0:T(8,128)(2,1)} %own_ref.1), channel_id=1, source_target_pairs={{0,4},{1,5},{2,6},{3,7},{4,0},{5,1},{6,2},{7,3},{8,12},{9,13},{10,... | collective-permute-start | bytes 98312 | tf_op jit(solution)/shard_map/ppermute | solution.py:19
  3.8 2.6 %collective-permute-start.1 = (bf16[128,128]{1,0:T(8,128)(2,1)}, bf16[128,128]{1,0:T(8,128)(2,1)S(1)}, u32[]{:S(2)}, u32[]{:S(2)}) collective-permute-start(bf16[128,128]{1,0:T(8,128)(2,1)} %own_ref.1), channel_id=1, source_target_pairs={{0,8},{1,9},{2,10},{3,11},{4,12},{5,13},{6,14},{7,15},{8,0},{9,1},... | collective-permute-start | bytes 98312 | tf_op jit(solution)/shard_map/ppermute | solution.py:19
  6.4 1.5 %fusion = (s32[8,64,158]{1,0,2:T(8,128)S(1)}, s32[8,64,158]{1,0,2:T(8,128)S(1)}) fusion(s32[8,128,158]{1,0,2:T(8,128)} %param.5), kind=kLoop, calls=%fused_computation.12 | loop fusion | bytes 1294336 | tf_op jit(solution)/shard_map/slice | solution.py:230
  7.9 0.4 copy.13
  8.2 0.3 copy.14
  8.6 0.1 shift-left_or_fusion
  8.8 0.0 collective-permute-done
  8.8 0.6 collective-permute-done.1
  9.4 2.9 %collective-permute-done.2 = bf16[128,128]{1,0:T(8,128)(2,1)S(1)} collective-permute-done((bf16[128,128]{1,0:T(8,128)(2,1)}, bf16[128,128]{1,0:T(8,128)(2,1)S(1)}, u32[]{:S(2)}, u32[]{:S(2)}) %collective-permute-start.2) | collective-permute-done | bytes 32800 | tf_op jit(solution)/shard_map/ppermute | solution.py:19
  12.3 1.5 %collective-permute-start.3 = (bf16[512,128]{1,0:T(8,128)(2,1)S(1)}, bf16[512,128]{1,0:T(8,128)(2,1)S(1)}, u32[]{:S(2)}, u32[]{:S(2)}) collective-permute-start(bf16[512,128]{1,0:T(8,128)(2,1)S(1)} %constant_dynamic-update-slice_fusion.column_ref.rest_0_), channel_id=1, source_target_pairs={{0,1},{1,0},{2,3},{3,2},{4,5},{5,4},{6,7},{7,6},{8,9},{9,8},{10,11... | collective-permute-start | bytes 393224 | tf_op jit(solution)/shard_map/ppermute | solution.py:19
  13.8 1.5 %collective-permute-start.4 = (bf16[512,128]{1,0:T(8,128)(2,1)S(1)}, bf16[512,128]{1,0:T(8,128)(2,1)S(1)}, u32[]{:S(2)}, u32[]{:S(2)}) collective-permute-start(bf16[512,128]{1,0:T(8,128)(2,1)S(1)} %constant_dynamic-update-slice_fusion.column_ref.rest_0_), channel_id=1, source_target_pairs={{0,2},{1,3},{2,0},{3,1},{4,6},{5,7},{6,4},{7,5},{8,10},{9,11},{10,... | collective-permute-start | bytes 393224 | tf_op jit(solution)/shard_map/ppermute | solution.py:19
  15.3 0.5 collective-permute-start.5
  15.8 0.1 pad_add_fusion.me_ref
  15.9 2.2 %copy-done = bf16[8,128,2048]{2,1,0:T(8,128)(2,1)S(1)} copy-done((bf16[8,128,2048]{2,1,0:T(8,128)(2,1)S(1)}, bf16[8,128,2048]{2,1,0:T(8,128)(2,1)}, u32[]{:S(2)}) %copy-start) | copy-done | bytes 4194328
  18.0 2.5 %early_kernel.1 = (bf16[8,1024,256]{2,1,0:T(8,128)(2,1)S(1)}, bf16[1024,128]{1,0:T(8,128)(2,1)S(1)}, f32[1024,128]{1,0:T(8,128)S(1)}) custom-call(s32[2]{0:T(128)S(1)} %pad_add_fusion.me_ref, s32[8,64,256]{2,1,0:T(8,128)S(1)} %pad.4.words_ref, bf16[8,128,2048]{2,1,0:T(8,128)(2,1)S(1)} %copy-done, bf16[8,128,2048]{2,1,0:T(8,128)(2,1)S(1)} %copy-done, ...), custom_call_target="tpu_custom_call" | custom-call | flops 268435456 | bytes 2097152 | tf_op jit(solution)/shard_map/early_kernel/pallas_call | solution.py:251
  20.6 0.0 collective-permute-done.3.rest_0_.rest_1_
  20.6 0.0 collective-permute-done.4.rest_1_.rest_2_
  20.6 0.5 collective-permute-done.5.rest_2_.rest_3_
  21.2 6.0 %late_kernel.1 = (bf16[8,1024,256]{2,1,0:T(8,128)(2,1)S(1)}, bf16[256,128]{1,0:T(8,128)(2,1)S(1)}, bf16[256,128]{1,0:T(8,128)(2,1)S(1)}, bf16[256,128]{1,0:T(8,128)(2,1)S(1)}, bf16[256,128]{1,0:T(8,128)(2,1)S(1)}) custom-call(s32[2]{0:T(128)S(1)} %pad_add_fusion.me_ref, s32[8,64,256]{2,1,0:T(8,128)S(1)} %pad.4.words_ref, ...), custom_call_target="tpu_custom_call", output_to_operand_aliasing={{0}: (6, {})} | custom-call | flops 805306368 | bytes 6291456 | tf_op jit(solution)/shard_map/late_kernel/pallas_call | solution.py:280
  27.2 7.0 %rows_kernel.1 = (f32[1024,128]{1,0:T(8,128)S(1)}, f32[1024,128]{1,0:T(8,128)S(1)}) custom-call(s32[2]{0:T(128)S(1)} %pad_add_fusion.me_ref, bf16[8,1024,256]{2,1,0:T(8,128)(2,1)S(1)} %get-tuple-element.29.err_ref, bf16[1024,128]{1,0:T(8,128)(2,1)S(1)} %get-tuple-element.22.left_ref, bf16[1024,128]{1,0:T(8,128)(2,1)S(1)} %bitcast.25, ...), custom_call_target="tpu_custom_call" | custom-call | flops 1610612736 | bytes 12582912 | tf_op jit(solution)/shard_map/rows_kernel/pallas_call | solution.py:333
  34.1 0.1 collective-permute-start.9
  34.2 0.1 collective-permute-start.6
  34.3 1.3 %collective-permute-start.7 = (bf16[256,128]{1,0:T(8,128)(2,1)S(1)}, bf16[256,128]{1,0:T(8,128)(2,1)S(1)}, u32[]{:S(2)}, u32[]{:S(2)}) collective-permute-start(bf16[256,128]{1,0:T(8,128)(2,1)S(1)} %get-tuple-element.27), channel_id=1, source_target_pairs={{0,8},{1,9},{2,10},{3,11},{4,12},{5,13},{6,14},{7,15},{8,0},{9,1},... | collective-permute-start | bytes 196616 | tf_op jit(solution)/shard_map/ppermute | solution.py:19
  35.6 3.0 %collective-permute-start.8 = (bf16[256,128]{1,0:T(8,128)(2,1)S(1)}, bf16[256,128]{1,0:T(8,128)(2,1)S(1)}, u32[]{:S(2)}, u32[]{:S(2)}) collective-permute-start(bf16[256,128]{1,0:T(8,128)(2,1)S(1)} %get-tuple-element.28), channel_id=1, source_target_pairs={{0,12},{1,13},{2,14},{3,15},{4,8},{5,9},{6,10},{7,11},{8,4},{9,5},... | collective-permute-start | bytes 196616 | tf_op jit(solution)/shard_map/ppermute | solution.py:19
  38.7 1.1 %collective-permute-done.6.rest_1_ = bf16[256,128]{1,0:T(8,128)(2,1)S(1)} collective-permute-done((bf16[256,128]{1,0:T(8,128)(2,1)S(1)}, bf16[256,128]{1,0:T(8,128)(2,1)S(1)}, u32[]{:S(2)}, u32[]{:S(2)}) %collective-permute-start.6) | collective-permute-done | bytes 65568 | tf_op jit(solution)/shard_map/ppermute | solution.py:19
  39.7 3.3 %collective-permute-done.7.rest_2_ = bf16[256,128]{1,0:T(8,128)(2,1)S(1)} collective-permute-done((bf16[256,128]{1,0:T(8,128)(2,1)S(1)}, bf16[256,128]{1,0:T(8,128)(2,1)S(1)}, u32[]{:S(2)}, u32[]{:S(2)}) %collective-permute-start.7) | collective-permute-done | bytes 65568 | tf_op jit(solution)/shard_map/ppermute | solution.py:19
  43.0 0.8 %merge_kernel.1 = (f32[320,128]{1,0:T(8,128)S(1)}, f32[320,128]{1,0:T(8,128)S(1)}, f32[320,128]{1,0:T(8,128)S(1)}, f32[320,128]{1,0:T(8,128)S(1)}) custom-call(s32[2]{0:T(128)S(1)} %pad_add_fusion.me_ref, bf16[512,128]{1,0:T(8,128)(2,1)S(1)} %constant_dynamic-update-slice_fusion.column_ref.rest_0_, bf16[256,128]{1,0:T(8,128)(2,1)S(1)} %get-tuple-element.25.rest_0_, ...), custom_call_target="tpu_custom_call" | custom-call | tf_op jit(solution)/shard_map/merge_kernel/pallas_call | solution.py:337
  43.9 1.0 %collective-permute-start.10 = (f32[320,128]{1,0:T(8,128)S(1)}, f32[320,128]{1,0:T(8,128)S(1)}, u32[]{:S(2)}, u32[]{:S(2)}) collective-permute-start(f32[320,128]{1,0:T(8,128)S(1)} %get-tuple-element.33), channel_id=1, source_target_pairs={{0,1},{1,0},{2,3},{3,2},{4,5},{5,4},{6,7},{7,6},{8,9},{9,8},{10,11... | collective-permute-start | bytes 491528 | tf_op jit(solution)/shard_map/ppermute | solution.py:19
  44.9 1.5 %collective-permute-start.11 = (f32[320,128]{1,0:T(8,128)S(1)}, f32[320,128]{1,0:T(8,128)S(1)}, u32[]{:S(2)}, u32[]{:S(2)}) collective-permute-start(f32[320,128]{1,0:T(8,128)S(1)} %get-tuple-element.34), channel_id=1, source_target_pairs={{0,2},{1,3},{2,0},{3,1},{4,6},{5,7},{6,4},{7,5},{8,10},{9,11},{10,... | collective-permute-start | bytes 491528 | tf_op jit(solution)/shard_map/ppermute | solution.py:19
  46.4 1.0 %collective-permute-start.12 = (f32[320,128]{1,0:T(8,128)S(1)}, f32[320,128]{1,0:T(8,128)S(1)}, u32[]{:S(2)}, u32[]{:S(2)}) collective-permute-start(f32[320,128]{1,0:T(8,128)S(1)} %get-tuple-element.35), channel_id=1, source_target_pairs={{0,3},{1,2},{2,1},{3,0},{4,7},{5,6},{6,5},{7,4},{8,11},{9,10},{10,... | collective-permute-start | bytes 491528 | tf_op jit(solution)/shard_map/ppermute | solution.py:19
  47.4 2.7 %collective-permute-done.10.rest_1_ = f32[320,128]{1,0:T(8,128)S(1)} collective-permute-done((f32[320,128]{1,0:T(8,128)S(1)}, f32[320,128]{1,0:T(8,128)S(1)}, u32[]{:S(2)}, u32[]{:S(2)}) %collective-permute-start.10) | collective-permute-done | bytes 163872 | tf_op jit(solution)/shard_map/ppermute | solution.py:19
  50.2 3.0 %collective-permute-done.11.rest_2_ = f32[320,128]{1,0:T(8,128)S(1)} collective-permute-done((f32[320,128]{1,0:T(8,128)S(1)}, f32[320,128]{1,0:T(8,128)S(1)}, u32[]{:S(2)}, u32[]{:S(2)}) %collective-permute-start.11) | collective-permute-done | bytes 163872 | tf_op jit(solution)/shard_map/ppermute | solution.py:19
  53.2 2.0 %collective-permute-start.13 = (f32[128,128]{1,0:T(8,128)S(1)}, f32[128,128]{1,0:T(8,128)S(1)}, u32[]{:S(2)}, u32[]{:S(2)}) collective-permute-start(f32[128,128]{1,0:T(8,128)S(1)} %get-tuple-element.37), channel_id=1, source_target_pairs={{0,4},{1,5},{2,6},{3,7},{4,0},{5,1},{6,2},{7,3},{8,12},{9,13},{10,... | collective-permute-start | bytes 196616 | tf_op jit(solution)/shard_map/ppermute | solution.py:19
  55.2 0.8 %collective-permute-start.14 = (f32[128,128]{1,0:T(8,128)S(1)}, f32[128,128]{1,0:T(8,128)S(1)}, u32[]{:S(2)}, u32[]{:S(2)}) collective-permute-start(f32[128,128]{1,0:T(8,128)S(1)} %get-tuple-element.38), channel_id=1, source_target_pairs={{0,8},{1,9},{2,10},{3,11},{4,12},{5,13},{6,14},{7,15},{8,0},{9,1},... | collective-permute-start | bytes 196616 | tf_op jit(solution)/shard_map/ppermute | solution.py:19
  55.9 1.7 %collective-permute-start.15 = (f32[128,128]{1,0:T(8,128)S(1)}, f32[128,128]{1,0:T(8,128)S(1)}, u32[]{:S(2)}, u32[]{:S(2)}) collective-permute-start(f32[128,128]{1,0:T(8,128)S(1)} %get-tuple-element.39), channel_id=1, source_target_pairs={{0,12},{1,13},{2,14},{3,15},{4,8},{5,9},{6,10},{7,11},{8,4},{9,5},... | collective-permute-start | bytes 196616 | tf_op jit(solution)/shard_map/ppermute | solution.py:19
  57.6 0.0 collective-permute-done.13.rest_1_
  57.7 3.5 %collective-permute-done.14.rest_2_ = f32[128,128]{1,0:T(8,128)S(1)} collective-permute-done((f32[128,128]{1,0:T(8,128)S(1)}, f32[128,128]{1,0:T(8,128)S(1)}, u32[]{:S(2)}, u32[]{:S(2)}) %collective-permute-start.14) | collective-permute-done | bytes 65568 | tf_op jit(solution)/shard_map/ppermute | solution.py:19
  61.2 0.9 %collective-permute-done.15.rest_3_ = f32[128,128]{1,0:T(8,128)S(1)} collective-permute-done((f32[128,128]{1,0:T(8,128)S(1)}, f32[128,128]{1,0:T(8,128)S(1)}, u32[]{:S(2)}, u32[]{:S(2)}) %collective-permute-start.15) | collective-permute-done | bytes 65568 | tf_op jit(solution)/shard_map/ppermute | solution.py:19
  62.1 0.6 far_kernel.1
  62.7 1.1 %collective-permute-start.17 = (f32[4,64,128]{2,1,0:T(8,128)S(1)}, f32[4,64,128]{2,1,0:T(8,128)S(1)}, u32[]{:S(2)}, u32[]{:S(2)}) collective-permute-start(f32[4,64,128]{2,1,0:T(8,128)S(1)} %bitcast.26), channel_id=1, source_target_pairs={{0,1},{1,0},{2,3},{3,2},{4,5},{5,4},{6,7},{7,6},{8,9},{9,8},{10,11... | collective-permute-start | bytes 393224 | tf_op jit(solution)/shard_map/ppermute | solution.py:19
  63.8 0.7 collective-permute-start.18
  64.5 1.8 %collective-permute-start.19 = (f32[4,64,128]{2,1,0:T(8,128)S(1)}, f32[4,64,128]{2,1,0:T(8,128)S(1)}, u32[]{:S(2)}, u32[]{:S(2)}) collective-permute-start(f32[4,64,128]{2,1,0:T(8,128)S(1)} %bitcast.28), channel_id=1, source_target_pairs={{0,3},{1,2},{2,1},{3,0},{4,7},{5,6},{6,5},{7,4},{8,11},{9,10},{10,... | collective-permute-start | bytes 393224 | tf_op jit(solution)/shard_map/ppermute | solution.py:19
  66.3 1.1 %collective-permute-done.16 = f32[64,128]{1,0:T(8,128)S(1)} collective-permute-done((f32[64,128]{1,0:T(8,128)S(1)}, f32[64,128]{1,0:T(8,128)S(1)}, u32[]{:S(2)}, u32[]{:S(2)}) %collective-permute-start.16) | collective-permute-done | bytes 32800 | tf_op jit(solution)/shard_map/ppermute | solution.py:19
  67.5 0.5 collective-permute-done.17
  68.0 0.8 %collective-permute-done.18 = f32[4,64,128]{2,1,0:T(8,128)S(1)} collective-permute-done((f32[4,64,128]{2,1,0:T(8,128)S(1)}, f32[4,64,128]{2,1,0:T(8,128)S(1)}, u32[]{:S(2)}, u32[]{:S(2)}) %collective-permute-start.18) | collective-permute-done | bytes 131104 | tf_op jit(solution)/shard_map/ppermute | solution.py:19
  68.8 1.5 %collective-permute-done.19 = f32[4,64,128]{2,1,0:T(8,128)S(1)} collective-permute-done((f32[4,64,128]{2,1,0:T(8,128)S(1)}, f32[4,64,128]{2,1,0:T(8,128)S(1)}, u32[]{:S(2)}, u32[]{:S(2)}) %collective-permute-start.19) | collective-permute-done | bytes 131104 | tf_op jit(solution)/shard_map/ppermute | solution.py:19
  70.3 0.0 copy-start.3
  70.4 0.8 %copy-done.3 = f32[4,4,64,128]{3,2,1,0:T(8,128)} copy-done((f32[4,4,64,128]{3,2,1,0:T(8,128)}, f32[4,4,64,128]{3,2,1,0:T(8,128)S(1)}, u32[]{:S(2)}) %copy-start.3) | copy-done | bytes 524312
  (26 shorter events, 0.2 us)
Async XLA Ops:
  0.6 8.1 %copy-start.2 = (bf16[128,128]{1,0:T(8,128)(2,1)S(1)}, bf16[128,128]{1,0:T(8,128)(2,1)}, u32[]{:S(2)}) copy-start(bf16[128,128]{1,0:T(8,128)(2,1)} %own_ref.1) | copy-start | bytes 98308
  0.6 15.2 %copy-start.1 = (bf16[8,128,128]{2,1,0:T(8,128)(2,1)S(1)}, bf16[8,128,128]{2,1,0:T(8,128)(2,1)}, u32[]{:S(2)}) copy-start(bf16[8,128,128]{2,1,0:T(8,128)(2,1)} %cores_ref.1) | copy-start | bytes 786436
  0.7 8.1 %collective-permute-start = (bf16[128,128]{1,0:T(8,128)(2,1)}, bf16[128,128]{1,0:T(8,128)(2,1)S(1)}, u32[]{:S(2)}, u32[]{:S(2)}) collective-permute-start(bf16[128,128]{1,0:T(8,128)(2,1)} %own_ref.1), channel_id=1, source_target_pairs={{0,4},{1,5},{2,6},{3,7},{4,0},{5,1},{6,2},{7,3},{8,12},{9,13},{10,... | collective-permute-start | bytes 98312 | tf_op jit(solution)/shard_map/ppermute | solution.py:19
  3.8 5.6 %collective-permute-start.1 = (bf16[128,128]{1,0:T(8,128)(2,1)}, bf16[128,128]{1,0:T(8,128)(2,1)S(1)}, u32[]{:S(2)}, u32[]{:S(2)}) collective-permute-start(bf16[128,128]{1,0:T(8,128)(2,1)} %own_ref.1), channel_id=1, source_target_pairs={{0,8},{1,9},{2,10},{3,11},{4,12},{5,13},{6,14},{7,15},{8,0},{9,1},... | collective-permute-start | bytes 98312 | tf_op jit(solution)/shard_map/ppermute | solution.py:19
  6.4 5.9 %collective-permute-start.2 = (bf16[128,128]{1,0:T(8,128)(2,1)}, bf16[128,128]{1,0:T(8,128)(2,1)S(1)}, u32[]{:S(2)}, u32[]{:S(2)}) collective-permute-start(bf16[128,128]{1,0:T(8,128)(2,1)} %own_ref.1), channel_id=1, source_target_pairs={{0,12},{1,13},{2,14},{3,15},{4,8},{5,9},{6,10},{7,11},{8,4},{9,5},... | collective-permute-start | bytes 98312 | tf_op jit(solution)/shard_map/ppermute | solution.py:19
  12.3 8.3 %collective-permute-start.3 = (bf16[512,128]{1,0:T(8,128)(2,1)S(1)}, bf16[512,128]{1,0:T(8,128)(2,1)S(1)}, u32[]{:S(2)}, u32[]{:S(2)}) collective-permute-start(bf16[512,128]{1,0:T(8,128)(2,1)S(1)} %constant_dynamic-update-slice_fusion.column_ref.rest_0_), channel_id=1, source_target_pairs={{0,1},{1,0},{2,3},{3,2},{4,5},{5,4},{6,7},{7,6},{8,9},{9,8},{10,11... | collective-permute-start | bytes 393224 | tf_op jit(solution)/shard_map/ppermute | solution.py:19
  13.8 6.8 %collective-permute-start.4 = (bf16[512,128]{1,0:T(8,128)(2,1)S(1)}, bf16[512,128]{1,0:T(8,128)(2,1)S(1)}, u32[]{:S(2)}, u32[]{:S(2)}) collective-permute-start(bf16[512,128]{1,0:T(8,128)(2,1)S(1)} %constant_dynamic-update-slice_fusion.column_ref.rest_0_), channel_id=1, source_target_pairs={{0,2},{1,3},{2,0},{3,1},{4,6},{5,7},{6,4},{7,5},{8,10},{9,11},{10,... | collective-permute-start | bytes 393224 | tf_op jit(solution)/shard_map/ppermute | solution.py:19
  15.3 5.9 %collective-permute-start.5 = (bf16[512,128]{1,0:T(8,128)(2,1)S(1)}, bf16[512,128]{1,0:T(8,128)(2,1)S(1)}, u32[]{:S(2)}, u32[]{:S(2)}) collective-permute-start(bf16[512,128]{1,0:T(8,128)(2,1)S(1)} %constant_dynamic-update-slice_fusion.column_ref.rest_0_), channel_id=1, source_target_pairs={{0,3},{1,2},{2,1},{3,0},{4,7},{5,6},{6,5},{7,4},{8,11},{9,10},{10,... | collective-permute-start | bytes 393224 | tf_op jit(solution)/shard_map/ppermute | solution.py:19
  15.9 2.2 %copy-start = (bf16[8,128,2048]{2,1,0:T(8,128)(2,1)S(1)}, bf16[8,128,2048]{2,1,0:T(8,128)(2,1)}, u32[]{:S(2)}) copy-start(bf16[8,128,2048]{2,1,0:T(8,128)(2,1)} %facts1_ref.3) | copy-start | bytes 12582916
  34.1 8.9 %collective-permute-start.9 = (f32[1024,128]{1,0:T(8,128)S(1)}, f32[1024,128]{1,0:T(8,128)S(1)}, u32[]{:S(2)}, u32[]{:S(2)}) collective-permute-start(f32[1024,128]{1,0:T(8,128)S(1)} %get-tuple-element.31), channel_id=1, source_target_pairs={{0,16},{16,0},{1,17},{17,1},{2,18},{18,2},{3,19},{19,3},{4,20},{20... | collective-permute-start | bytes 1572872 | tf_op jit(solution)/shard_map/ppermute | solution.py:19
  34.2 5.5 %collective-permute-start.6 = (bf16[256,128]{1,0:T(8,128)(2,1)S(1)}, bf16[256,128]{1,0:T(8,128)(2,1)S(1)}, u32[]{:S(2)}, u32[]{:S(2)}) collective-permute-start(bf16[256,128]{1,0:T(8,128)(2,1)S(1)} %get-tuple-element.26), channel_id=1, source_target_pairs={{0,4},{1,5},{2,6},{3,7},{4,0},{5,1},{6,2},{7,3},{8,12},{9,13},{10,... | collective-permute-start | bytes 196616 | tf_op jit(solution)/shard_map/ppermute | solution.py:19
  34.3 8.7 %collective-permute-start.7 = (bf16[256,128]{1,0:T(8,128)(2,1)S(1)}, bf16[256,128]{1,0:T(8,128)(2,1)S(1)}, u32[]{:S(2)}, u32[]{:S(2)}) collective-permute-start(bf16[256,128]{1,0:T(8,128)(2,1)S(1)} %get-tuple-element.27), channel_id=1, source_target_pairs={{0,8},{1,9},{2,10},{3,11},{4,12},{5,13},{6,14},{7,15},{8,0},{9,1},... | collective-permute-start | bytes 196616 | tf_op jit(solution)/shard_map/ppermute | solution.py:19
  35.6 7.4 %collective-permute-start.8 = (bf16[256,128]{1,0:T(8,128)(2,1)S(1)}, bf16[256,128]{1,0:T(8,128)(2,1)S(1)}, u32[]{:S(2)}, u32[]{:S(2)}) collective-permute-start(bf16[256,128]{1,0:T(8,128)(2,1)S(1)} %get-tuple-element.28), channel_id=1, source_target_pairs={{0,12},{1,13},{2,14},{3,15},{4,8},{5,9},{6,10},{7,11},{8,4},{9,5},... | collective-permute-start | bytes 196616 | tf_op jit(solution)/shard_map/ppermute | solution.py:19
  43.9 6.3 %collective-permute-start.10 = (f32[320,128]{1,0:T(8,128)S(1)}, f32[320,128]{1,0:T(8,128)S(1)}, u32[]{:S(2)}, u32[]{:S(2)}) collective-permute-start(f32[320,128]{1,0:T(8,128)S(1)} %get-tuple-element.33), channel_id=1, source_target_pairs={{0,1},{1,0},{2,3},{3,2},{4,5},{5,4},{6,7},{7,6},{8,9},{9,8},{10,11... | collective-permute-start | bytes 491528 | tf_op jit(solution)/shard_map/ppermute | solution.py:19
  44.9 8.2 %collective-permute-start.11 = (f32[320,128]{1,0:T(8,128)S(1)}, f32[320,128]{1,0:T(8,128)S(1)}, u32[]{:S(2)}, u32[]{:S(2)}) collective-permute-start(f32[320,128]{1,0:T(8,128)S(1)} %get-tuple-element.34), channel_id=1, source_target_pairs={{0,2},{1,3},{2,0},{3,1},{4,6},{5,7},{6,4},{7,5},{8,10},{9,11},{10,... | collective-permute-start | bytes 491528 | tf_op jit(solution)/shard_map/ppermute | solution.py:19
  46.4 6.7 %collective-permute-start.12 = (f32[320,128]{1,0:T(8,128)S(1)}, f32[320,128]{1,0:T(8,128)S(1)}, u32[]{:S(2)}, u32[]{:S(2)}) collective-permute-start(f32[320,128]{1,0:T(8,128)S(1)} %get-tuple-element.35), channel_id=1, source_target_pairs={{0,3},{1,2},{2,1},{3,0},{4,7},{5,6},{6,5},{7,4},{8,11},{9,10},{10,... | collective-permute-start | bytes 491528 | tf_op jit(solution)/shard_map/ppermute | solution.py:19
  53.2 4.5 %collective-permute-start.13 = (f32[128,128]{1,0:T(8,128)S(1)}, f32[128,128]{1,0:T(8,128)S(1)}, u32[]{:S(2)}, u32[]{:S(2)}) collective-permute-start(f32[128,128]{1,0:T(8,128)S(1)} %get-tuple-element.37), channel_id=1, source_target_pairs={{0,4},{1,5},{2,6},{3,7},{4,0},{5,1},{6,2},{7,3},{8,12},{9,13},{10,... | collective-permute-start | bytes 196616 | tf_op jit(solution)/shard_map/ppermute | solution.py:19
  55.2 6.0 %collective-permute-start.14 = (f32[128,128]{1,0:T(8,128)S(1)}, f32[128,128]{1,0:T(8,128)S(1)}, u32[]{:S(2)}, u32[]{:S(2)}) collective-permute-start(f32[128,128]{1,0:T(8,128)S(1)} %get-tuple-element.38), channel_id=1, source_target_pairs={{0,8},{1,9},{2,10},{3,11},{4,12},{5,13},{6,14},{7,15},{8,0},{9,1},... | collective-permute-start | bytes 196616 | tf_op jit(solution)/shard_map/ppermute | solution.py:19
  55.9 6.2 %collective-permute-start.15 = (f32[128,128]{1,0:T(8,128)S(1)}, f32[128,128]{1,0:T(8,128)S(1)}, u32[]{:S(2)}, u32[]{:S(2)}) collective-permute-start(f32[128,128]{1,0:T(8,128)S(1)} %get-tuple-element.39), channel_id=1, source_target_pairs={{0,12},{1,13},{2,14},{3,15},{4,8},{5,9},{6,10},{7,11},{8,4},{9,5},... | collective-permute-start | bytes 196616 | tf_op jit(solution)/shard_map/ppermute | solution.py:19
  62.7 5.3 %collective-permute-start.17 = (f32[4,64,128]{2,1,0:T(8,128)S(1)}, f32[4,64,128]{2,1,0:T(8,128)S(1)}, u32[]{:S(2)}, u32[]{:S(2)}) collective-permute-start(f32[4,64,128]{2,1,0:T(8,128)S(1)} %bitcast.26), channel_id=1, source_target_pairs={{0,1},{1,0},{2,3},{3,2},{4,5},{5,4},{6,7},{7,6},{8,9},{9,8},{10,11... | collective-permute-start | bytes 393224 | tf_op jit(solution)/shard_map/ppermute | solution.py:19
  63.8 5.0 %collective-permute-start.18 = (f32[4,64,128]{2,1,0:T(8,128)S(1)}, f32[4,64,128]{2,1,0:T(8,128)S(1)}, u32[]{:S(2)}, u32[]{:S(2)}) collective-permute-start(f32[4,64,128]{2,1,0:T(8,128)S(1)} %bitcast.27), channel_id=1, source_target_pairs={{0,2},{1,3},{2,0},{3,1},{4,6},{5,7},{6,4},{7,5},{8,10},{9,11},{10,... | collective-permute-start | bytes 393224 | tf_op jit(solution)/shard_map/ppermute | solution.py:19
  64.5 5.9 %collective-permute-start.19 = (f32[4,64,128]{2,1,0:T(8,128)S(1)}, f32[4,64,128]{2,1,0:T(8,128)S(1)}, u32[]{:S(2)}, u32[]{:S(2)}) collective-permute-start(f32[4,64,128]{2,1,0:T(8,128)S(1)} %bitcast.28), channel_id=1, source_target_pairs={{0,3},{1,2},{2,1},{3,0},{4,7},{5,6},{6,5},{7,4},{8,11},{9,10},{10,... | collective-permute-start | bytes 393224 | tf_op jit(solution)/shard_map/ppermute | solution.py:19
  66.2 1.2 %collective-permute-start.16 = (f32[64,128]{1,0:T(8,128)S(1)}, f32[64,128]{1,0:T(8,128)S(1)}, u32[]{:S(2)}, u32[]{:S(2)}) collective-permute-start(f32[64,128]{1,0:T(8,128)S(1)} %get-tuple-element.40), channel_id=1, source_target_pairs={{0,16},{16,0},{1,17},{17,1},{2,18},{18,2},{3,19},{19,3},{4,20},{20... | collective-permute-start | bytes 98312 | tf_op jit(solution)/shard_map/ppermute | solution.py:19
  67.4 2.9 %copy-start.4 = (f32[2,64,128]{2,1,0:T(8,128)}, f32[2,64,128]{2,1,0:T(8,128)S(1)}, u32[]{:S(2)}) copy-start(f32[2,64,128]{2,1,0:T(8,128)S(1)} %bitcast_dynamic-update-slice_fusion.3) | copy-start | bytes 196612
  70.3 0.8 %copy-start.3 = (f32[4,4,64,128]{3,2,1,0:T(8,128)}, f32[4,4,64,128]{3,2,1,0:T(8,128)S(1)}, u32[]{:S(2)}) copy-start(f32[4,4,64,128]{3,2,1,0:T(8,128)S(1)} %bitcast_dynamic-update-slice_fusion) | copy-start | bytes 1572868

commit v2 on v1

--- a/solution.py
+++ b/solution.py
@@ -17,6 +17,13 @@
 
 def swap(x, axis, size, distance):
     return lax.ppermute(x, axis, [(i, i ^ distance) for i in range(size)])
+
+
+def from_partners(own, size, send):
+    got = [own]
+    for d in range(1, size):
+        got.append(send(d))
+    return got
 
 
 def nt(a, b):
@@ -57,9 +64,14 @@
         words.append(word)
         bits.append(jnp.left_shift(1, column - word * BITS))
         blocks.append(pl.multiple_of(lax.div(chip, BITS) * LANES, LANES))
+
+    def at(k):
+        return slice(k * rows, (k + 1) * rows)
+
+    whole_model = nt(left_ref[...], piece)
+    errs = []
     for k in range(relations):
-        at = slice(k * rows, (k + 1) * rows)
-        model = nt(left_ref[at, :], piece)
+        model = whole_model[at(k), :]
         tiles = []
         for s in range(2):
             marks = jnp.take_along_axis(
@@ -72,8 +84,9 @@
             bottom = jnp.where((marks & low_bits) != 0, diff[half:], 0.0)
             tiles.append(jnp.concatenate([top, bottom], axis=0).astype(BF16))
         err = jnp.concatenate(tiles, axis=1)
-        err_ref[0, at, :] = err
-        acc_ref[at, :] += nn(err, piece)
+        err_ref[0, at(k), :] = err
+        errs.append(err)
+    acc_ref[...] += nn(jnp.concatenate(errs, axis=0), piece)
 
 
 def early_kernel(
@@ -136,12 +149,13 @@
     rank = left_ref.shape[1]
     rows = piece_ref.shape[0] // 2
     relations = cores_ref.shape[0] // rank
+    own = own_ref[...]
+    right_all = nt(piece_ref[...], cores_ref[...]).astype(BF16)
     total_ref[...] = tn(err_ref[0], left_ref[...])
-    own = own_ref[...]
-    for k in range(relations):
-        span = slice(k * rank, (k + 1) * rank)
-        right = nt(piece_ref[...], cores_ref[span, :]).astype(BF16)
-        own = own + nn(err_ref[0, k * rows : (k + 1) * rows, :], right)
+    for p in range(relations):
+        own = own + nn(
+            err_ref[0, p * rows : (p + 1) * rows, :], right_all[:, p * rank : (p + 1) * rank]
+        )
     own_ref[...] = own
 
     @pl.when(step == pairs - 1)
@@ -223,8 +237,8 @@
     def far_swap(x, d):
         return swap(x, "ent", ent, d * low)
 
-    column = jnp.concatenate([factors] + [far_swap(factors, d) for d in range(1, high)])
-    nears = [near_swap(column, q) for q in range(1, low)]
+    column = jnp.concatenate(from_partners(factors, high, lambda d: far_swap(factors, d)))
+    nears = from_partners(column, low, lambda q: near_swap(column, q))[1:]
 
     half = rows // 2
     packed = observed[:, :half] | jnp.left_shift(observed[:, half:], 16)
@@ -302,8 +316,7 @@
         name="late_kernel",
     )(me, packed, facts, facts, left, part, err, *nears)
 
-    for d in range(1, high):
-        pulls[d] = far_swap(pulls[d], d)
+    pulls = from_partners(pulls[0], high, lambda d: far_swap(pulls[d], d))
 
     sub = rows // rel
     rows_call = pl.pallas_call(
@@ -343,7 +356,7 @@
         compiler_params=pltpu.CompilerParams(vmem_limit_bytes=8 * MIB),
         name="merge_kernel",
     )(me, column, *pulls, *shares)
-    merged = [merged[0]] + [near_swap(merged[q], q) for q in range(1, low)]
+    merged = from_partners(merged[0], low, lambda q: near_swap(merged[q], q))
 
     parts = pl.pallas_call(
         functools.partial(near_kernel, low, high, rank / n_all),
@@ -351,7 +364,7 @@
         compiler_params=pltpu.CompilerParams(vmem_limit_bytes=6 * MIB),
         name="near_kernel",
     )(*merged)
-    parts = [parts[0]] + [far_swap(parts[d], d) for d in range(1, high)]
+    parts = from_partners(parts[0], high, lambda d: far_swap(parts[d], d))
 
     owned, core_column = pl.pallas_call(
         functools.partial(far_kernel, low, high, n_all * relations * rel),
@@ -371,8 +384,7 @@
     grad_cores = jnp.zeros((high, low, size, rank), F32)
     near = lax.axis_index("ent") & (low - 1)
     core_column = core_column.reshape(high, size, rank)
-    for q in range(low):
-        piece = core_column if q == 0 else near_swap(core_column, q)
+    for q, piece in enumerate(from_partners(core_column, low, lambda q: near_swap(core_column, q))):
         grad_cores = lax.dynamic_update_index_in_dim(grad_cores, piece, near ^ q, 1)
     return grad_factors, grad_cores.reshape(relations, rank, rank)
 

time: 71.3 us -> 69.4 us (0.973)
  Pallas kernels: 16.9 us -> 14.7 us
    pallas_call x1, Pallas kernels: 6.95 us -> 5.78 us  [gradients(): rows_call(me, err, left, cores.reshape(relations * rank, rank), column, *...]
    pallas_call x1, Pallas kernels: 5.99 us -> 5.21 us  [gradients(): pl.pallas_call(functools.partial(late_kernel, low, high, first), grid_spe...]
  transfers between devices with their start and end apart: 20 -> 20, of which waited for: 13 -> 13; matrix products, arithmetic and copies ran while one was open for 4% -> 4% of each run, Pallas kernels for 4% -> 3%
where the time goes in v2:
time: 69.4 us; the launch traced here: 69.2 us
  starting transfers between devices  25.3 us (36%)
  waiting for transfers between devices  22.8 us (33%)
  Pallas kernels  14.7 us (21%)
  local copies, waits for them, and re-layouts  5.39 us (8%)
  between operations  0.86 us (1%)
    ppermute x20, starting transfers between devices, swap(): return lax.ppermute(x, axis, [(i, i ^ distance) for i in range(size)])  25.3 us
    ppermute x20, waiting for transfers between devices, swap(): return lax.ppermute(x, axis, [(i, i ^ distance) for i in range(size)])  22.8 us
    pallas_call x1, Pallas kernels, gradients(): rows_call(me, err, left, cores.reshape(relations * rank, rank), column, *...  5.78 us
    pallas_call x1, Pallas kernels, gradients(): pl.pallas_call(functools.partial(late_kernel, low, high, first), grid_spe...  5.21 us
    unnamed x15, local copies, waits for them, and re-layouts  3.71 us
    pallas_call x1, Pallas kernels, gradients(): pl.pallas_call(functools.partial(early_kernel, low, high), grid_spec=pltp...  2.29 us
    slice x1, local copies, waits for them, and re-layouts, gradients(): packed = observed[:, :half] | jnp.left_shift(observed[:, half:], 16)  1.53 us
  transfers between devices with their start and end apart: 20, of which 13 were waited for; matrix products, arithmetic and copies ran while one was open for 4% of the time, Pallas kernels for 3%

profile of v2, /device:TPU:0, one launch (start us, length us, event | category | flops | bytes accessed | tf_op | source)
XLA Modules:
  0.0 69.2 jit_solution(952734113576812068)
XLA Ops:
  0.7 3.1 %collective-permute-start = (bf16[128,128]{1,0:T(8,128)(2,1)}, bf16[128,128]{1,0:T(8,128)(2,1)S(1)}, u32[]{:S(2)}, u32[]{:S(2)}) collective-permute-start(bf16[128,128]{1,0:T(8,128)(2,1)} %own_ref.1), channel_id=1, source_target_pairs={{0,4},{1,5},{2,6},{3,7},{4,0},{5,1},{6,2},{7,3},{8,12},{9,13},{10,... | collective-permute-start | bytes 98312 | tf_op jit(solution)/shard_map/ppermute | solution.py:19
  3.8 2.6 %collective-permute-start.1 = (bf16[128,128]{1,0:T(8,128)(2,1)}, bf16[128,128]{1,0:T(8,128)(2,1)S(1)}, u32[]{:S(2)}, u32[]{:S(2)}) collective-permute-start(bf16[128,128]{1,0:T(8,128)(2,1)} %own_ref.1), channel_id=1, source_target_pairs={{0,8},{1,9},{2,10},{3,11},{4,12},{5,13},{6,14},{7,15},{8,0},{9,1},... | collective-permute-start | bytes 98312 | tf_op jit(solution)/shard_map/ppermute | solution.py:19
  6.4 1.5 %fusion = (s32[8,64,158]{1,0,2:T(8,128)S(1)}, s32[8,64,158]{1,0,2:T(8,128)S(1)}) fusion(s32[8,128,158]{1,0,2:T(8,128)} %param.5), kind=kLoop, calls=%fused_computation.12 | loop fusion | bytes 1294336 | tf_op jit(solution)/shard_map/slice | solution.py:244
  7.9 0.4 copy.13
  8.2 0.3 copy.14
  8.6 0.1 shift-left_or_fusion
  8.8 0.0 collective-permute-done
  8.8 0.6 collective-permute-done.1
  9.4 2.9 %collective-permute-done.2 = bf16[128,128]{1,0:T(8,128)(2,1)S(1)} collective-permute-done((bf16[128,128]{1,0:T(8,128)(2,1)}, bf16[128,128]{1,0:T(8,128)(2,1)S(1)}, u32[]{:S(2)}, u32[]{:S(2)}) %collective-permute-start.2) | collective-permute-done | bytes 32800 | tf_op jit(solution)/shard_map/ppermute | solution.py:19
  12.3 1.5 %collective-permute-start.3 = (bf16[512,128]{1,0:T(8,128)(2,1)S(1)}, bf16[512,128]{1,0:T(8,128)(2,1)S(1)}, u32[]{:S(2)}, u32[]{:S(2)}) collective-permute-start(bf16[512,128]{1,0:T(8,128)(2,1)S(1)} %constant_dynamic-update-slice_fusion.column_ref.rest_0_), channel_id=1, source_target_pairs={{0,1},{1,0},{2,3},{3,2},{4,5},{5,4},{6,7},{7,6},{8,9},{9,8},{10,11... | collective-permute-start | bytes 393224 | tf_op jit(solution)/shard_map/ppermute | solution.py:19
  13.8 1.5 %collective-permute-start.4 = (bf16[512,128]{1,0:T(8,128)(2,1)S(1)}, bf16[512,128]{1,0:T(8,128)(2,1)S(1)}, u32[]{:S(2)}, u32[]{:S(2)}) collective-permute-start(bf16[512,128]{1,0:T(8,128)(2,1)S(1)} %constant_dynamic-update-slice_fusion.column_ref.rest_0_), channel_id=1, source_target_pairs={{0,2},{1,3},{2,0},{3,1},{4,6},{5,7},{6,4},{7,5},{8,10},{9,11},{10,... | collective-permute-start | bytes 393224 | tf_op jit(solution)/shard_map/ppermute | solution.py:19
  15.3 0.5 collective-permute-start.5
  15.8 0.1 pad_add_fusion.me_ref
  15.9 2.2 %copy-done = bf16[8,128,2048]{2,1,0:T(8,128)(2,1)S(1)} copy-done((bf16[8,128,2048]{2,1,0:T(8,128)(2,1)S(1)}, bf16[8,128,2048]{2,1,0:T(8,128)(2,1)}, u32[]{:S(2)}) %copy-start) | copy-done | bytes 4194328
  18.0 2.3 %early_kernel.1 = (bf16[8,1024,256]{2,1,0:T(8,128)(2,1)S(1)}, bf16[1024,128]{1,0:T(8,128)(2,1)S(1)}, f32[1024,128]{1,0:T(8,128)S(1)}) custom-call(s32[2]{0:T(128)S(1)} %pad_add_fusion.me_ref, s32[8,64,256]{2,1,0:T(8,128)S(1)} %pad.4.words_ref, bf16[8,128,2048]{2,1,0:T(8,128)(2,1)S(1)} %copy-done, bf16[8,128,2048]{2,1,0:T(8,128)(2,1)S(1)} %copy-done, ...), custom_call_target="tpu_custom_call" | custom-call | flops 268435456 | bytes 2097152 | tf_op jit(solution)/shard_map/early_kernel/pallas_call | solution.py:265
  20.3 0.0 collective-permute-done.3.rest_0_.rest_1_
  20.4 0.8 %collective-permute-done.5.rest_2_.rest_3_ = bf16[512,128]{1,0:T(8,128)(2,1)S(1)} collective-permute-done((bf16[512,128]{1,0:T(8,128)(2,1)S(1)}, bf16[512,128]{1,0:T(8,128)(2,1)S(1)}, u32[]{:S(2)}, u32[]{:S(2)}) %collective-permute-start.5) | collective-permute-done | bytes 131104 | tf_op jit(solution)/shard_map/ppermute | solution.py:19
  21.2 5.2 %late_kernel.1 = (bf16[8,1024,256]{2,1,0:T(8,128)(2,1)S(1)}, bf16[256,128]{1,0:T(8,128)(2,1)S(1)}, bf16[256,128]{1,0:T(8,128)(2,1)S(1)}, bf16[256,128]{1,0:T(8,128)(2,1)S(1)}, bf16[256,128]{1,0:T(8,128)(2,1)S(1)}) custom-call(s32[2]{0:T(128)S(1)} %pad_add_fusion.me_ref, s32[8,64,256]{2,1,0:T(8,128)S(1)} %pad.4.words_ref, ...), custom_call_target="tpu_custom_call", output_to_operand_aliasing={{0}: (6, {})} | custom-call | flops 805306368 | bytes 6291456 | tf_op jit(solution)/shard_map/late_kernel/pallas_call | solution.py:294
  26.4 5.8 %rows_kernel.1 = (f32[1024,128]{1,0:T(8,128)S(1)}, f32[1024,128]{1,0:T(8,128)S(1)}) custom-call(s32[2]{0:T(128)S(1)} %pad_add_fusion.me_ref, bf16[8,1024,256]{2,1,0:T(8,128)(2,1)S(1)} %get-tuple-element.29.err_ref, bf16[1024,128]{1,0:T(8,128)(2,1)S(1)} %get-tuple-element.22.left_ref, bf16[1024,128]{1,0:T(8,128)(2,1)S(1)} %bitcast.25, ...), custom_call_target="tpu_custom_call" | custom-call | flops 1610612736 | bytes 12582912 | tf_op jit(solution)/shard_map/rows_kernel/pallas_call | solution.py:346
  32.2 0.1 collective-permute-start.9
  32.3 0.1 collective-permute-start.6
  32.3 1.3 %collective-permute-start.7 = (bf16[256,128]{1,0:T(8,128)(2,1)S(1)}, bf16[256,128]{1,0:T(8,128)(2,1)S(1)}, u32[]{:S(2)}, u32[]{:S(2)}) collective-permute-start(bf16[256,128]{1,0:T(8,128)(2,1)S(1)} %get-tuple-element.27), channel_id=1, source_target_pairs={{0,8},{1,9},{2,10},{3,11},{4,12},{5,13},{6,14},{7,15},{8,0},{9,1},... | collective-permute-start | bytes 196616 | tf_op jit(solution)/shard_map/ppermute | solution.py:19
  33.7 3.0 %collective-permute-start.8 = (bf16[256,128]{1,0:T(8,128)(2,1)S(1)}, bf16[256,128]{1,0:T(8,128)(2,1)S(1)}, u32[]{:S(2)}, u32[]{:S(2)}) collective-permute-start(bf16[256,128]{1,0:T(8,128)(2,1)S(1)} %get-tuple-element.28), channel_id=1, source_target_pairs={{0,12},{1,13},{2,14},{3,15},{4,8},{5,9},{6,10},{7,11},{8,4},{9,5},... | collective-permute-start | bytes 196616 | tf_op jit(solution)/shard_map/ppermute | solution.py:19
  36.7 1.1 %collective-permute-done.6.rest_1_ = bf16[256,128]{1,0:T(8,128)(2,1)S(1)} collective-permute-done((bf16[256,128]{1,0:T(8,128)(2,1)S(1)}, bf16[256,128]{1,0:T(8,128)(2,1)S(1)}, u32[]{:S(2)}, u32[]{:S(2)}) %collective-permute-start.6) | collective-permute-done | bytes 65568 | tf_op jit(solution)/shard_map/ppermute | solution.py:19
  37.8 3.3 %collective-permute-done.7.rest_2_ = bf16[256,128]{1,0:T(8,128)(2,1)S(1)} collective-permute-done((bf16[256,128]{1,0:T(8,128)(2,1)S(1)}, bf16[256,128]{1,0:T(8,128)(2,1)S(1)}, u32[]{:S(2)}, u32[]{:S(2)}) %collective-permute-start.7) | collective-permute-done | bytes 65568 | tf_op jit(solution)/shard_map/ppermute | solution.py:19
  41.1 0.0 collective-permute-done.8.rest_3_
  41.1 0.8 %merge_kernel.1 = (f32[320,128]{1,0:T(8,128)S(1)}, f32[320,128]{1,0:T(8,128)S(1)}, f32[320,128]{1,0:T(8,128)S(1)}, f32[320,128]{1,0:T(8,128)S(1)}) custom-call(s32[2]{0:T(128)S(1)} %pad_add_fusion.me_ref, bf16[512,128]{1,0:T(8,128)(2,1)S(1)} %constant_dynamic-update-slice_fusion.column_ref.rest_0_, bf16[256,128]{1,0:T(8,128)(2,1)S(1)} %get-tuple-element.25.rest_0_, ...), custom_call_target="tpu_custom_call" | custom-call | tf_op jit(solution)/shard_map/merge_kernel/pallas_call | solution.py:350
  41.9 0.8 %collective-permute-start.10 = (f32[320,128]{1,0:T(8,128)S(1)}, f32[320,128]{1,0:T(8,128)S(1)}, u32[]{:S(2)}, u32[]{:S(2)}) collective-permute-start(f32[320,128]{1,0:T(8,128)S(1)} %get-tuple-element.33), channel_id=1, source_target_pairs={{0,1},{1,0},{2,3},{3,2},{4,5},{5,4},{6,7},{7,6},{8,9},{9,8},{10,11... | collective-permute-start | bytes 491528 | tf_op jit(solution)/shard_map/ppermute | solution.py:19
  42.7 1.5 %collective-permute-start.11 = (f32[320,128]{1,0:T(8,128)S(1)}, f32[320,128]{1,0:T(8,128)S(1)}, u32[]{:S(2)}, u32[]{:S(2)}) collective-permute-start(f32[320,128]{1,0:T(8,128)S(1)} %get-tuple-element.34), channel_id=1, source_target_pairs={{0,2},{1,3},{2,0},{3,1},{4,6},{5,7},{6,4},{7,5},{8,10},{9,11},{10,... | collective-permute-start | bytes 491528 | tf_op jit(solution)/shard_map/ppermute | solution.py:19
  44.2 1.2 %collective-permute-start.12 = (f32[320,128]{1,0:T(8,128)S(1)}, f32[320,128]{1,0:T(8,128)S(1)}, u32[]{:S(2)}, u32[]{:S(2)}) collective-permute-start(f32[320,128]{1,0:T(8,128)S(1)} %get-tuple-element.35), channel_id=1, source_target_pairs={{0,3},{1,2},{2,1},{3,0},{4,7},{5,6},{6,5},{7,4},{8,11},{9,10},{10,... | collective-permute-start | bytes 491528 | tf_op jit(solution)/shard_map/ppermute | solution.py:19
  45.5 2.7 %collective-permute-done.10.rest_1_ = f32[320,128]{1,0:T(8,128)S(1)} collective-permute-done((f32[320,128]{1,0:T(8,128)S(1)}, f32[320,128]{1,0:T(8,128)S(1)}, u32[]{:S(2)}, u32[]{:S(2)}) %collective-permute-start.10) | collective-permute-done | bytes 163872 | tf_op jit(solution)/shard_map/ppermute | solution.py:19
  48.1 2.8 %collective-permute-done.11.rest_2_ = f32[320,128]{1,0:T(8,128)S(1)} collective-permute-done((f32[320,128]{1,0:T(8,128)S(1)}, f32[320,128]{1,0:T(8,128)S(1)}, u32[]{:S(2)}, u32[]{:S(2)}) %collective-permute-start.11) | collective-permute-done | bytes 163872 | tf_op jit(solution)/shard_map/ppermute | solution.py:19
  51.0 2.0 %collective-permute-start.13 = (f32[128,128]{1,0:T(8,128)S(1)}, f32[128,128]{1,0:T(8,128)S(1)}, u32[]{:S(2)}, u32[]{:S(2)}) collective-permute-start(f32[128,128]{1,0:T(8,128)S(1)} %get-tuple-element.37), channel_id=1, source_target_pairs={{0,4},{1,5},{2,6},{3,7},{4,0},{5,1},{6,2},{7,3},{8,12},{9,13},{10,... | collective-permute-start | bytes 196616 | tf_op jit(solution)/shard_map/ppermute | solution.py:19
  53.0 0.8 %collective-permute-start.14 = (f32[128,128]{1,0:T(8,128)S(1)}, f32[128,128]{1,0:T(8,128)S(1)}, u32[]{:S(2)}, u32[]{:S(2)}) collective-permute-start(f32[128,128]{1,0:T(8,128)S(1)} %get-tuple-element.38), channel_id=1, source_target_pairs={{0,8},{1,9},{2,10},{3,11},{4,12},{5,13},{6,14},{7,15},{8,0},{9,1},... | collective-permute-start | bytes 196616 | tf_op jit(solution)/shard_map/ppermute | solution.py:19
  53.7 1.7 %collective-permute-start.15 = (f32[128,128]{1,0:T(8,128)S(1)}, f32[128,128]{1,0:T(8,128)S(1)}, u32[]{:S(2)}, u32[]{:S(2)}) collective-permute-start(f32[128,128]{1,0:T(8,128)S(1)} %get-tuple-element.39), channel_id=1, source_target_pairs={{0,12},{1,13},{2,14},{3,15},{4,8},{5,9},{6,10},{7,11},{8,4},{9,5},... | collective-permute-start | bytes 196616 | tf_op jit(solution)/shard_map/ppermute | solution.py:19
  55.4 0.0 collective-permute-done.13.rest_1_
  55.5 3.5 %collective-permute-done.14.rest_2_ = f32[128,128]{1,0:T(8,128)S(1)} collective-permute-done((f32[128,128]{1,0:T(8,128)S(1)}, f32[128,128]{1,0:T(8,128)S(1)}, u32[]{:S(2)}, u32[]{:S(2)}) %collective-permute-start.14) | collective-permute-done | bytes 65568 | tf_op jit(solution)/shard_map/ppermute | solution.py:19
  59.0 0.9 %collective-permute-done.15.rest_3_ = f32[128,128]{1,0:T(8,128)S(1)} collective-permute-done((f32[128,128]{1,0:T(8,128)S(1)}, f32[128,128]{1,0:T(8,128)S(1)}, u32[]{:S(2)}, u32[]{:S(2)}) %collective-permute-start.15) | collective-permute-done | bytes 65568 | tf_op jit(solution)/shard_map/ppermute | solution.py:19
  59.9 0.6 far_kernel.1
  60.5 1.1 %collective-permute-start.17 = (f32[4,64,128]{2,1,0:T(8,128)S(1)}, f32[4,64,128]{2,1,0:T(8,128)S(1)}, u32[]{:S(2)}, u32[]{:S(2)}) collective-permute-start(f32[4,64,128]{2,1,0:T(8,128)S(1)} %bitcast.26), channel_id=1, source_target_pairs={{0,1},{1,0},{2,3},{3,2},{4,5},{5,4},{6,7},{7,6},{8,9},{9,8},{10,11... | collective-permute-start | bytes 393224 | tf_op jit(solution)/shard_map/ppermute | solution.py:19
  61.6 0.9 %collective-permute-start.18 = (f32[4,64,128]{2,1,0:T(8,128)S(1)}, f32[4,64,128]{2,1,0:T(8,128)S(1)}, u32[]{:S(2)}, u32[]{:S(2)}) collective-permute-start(f32[4,64,128]{2,1,0:T(8,128)S(1)} %bitcast.27), channel_id=1, source_target_pairs={{0,2},{1,3},{2,0},{3,1},{4,6},{5,7},{6,4},{7,5},{8,10},{9,11},{10,... | collective-permute-start | bytes 393224 | tf_op jit(solution)/shard_map/ppermute | solution.py:19
  62.5 1.5 %collective-permute-start.19 = (f32[4,64,128]{2,1,0:T(8,128)S(1)}, f32[4,64,128]{2,1,0:T(8,128)S(1)}, u32[]{:S(2)}, u32[]{:S(2)}) collective-permute-start(f32[4,64,128]{2,1,0:T(8,128)S(1)} %bitcast.28), channel_id=1, source_target_pairs={{0,3},{1,2},{2,1},{3,0},{4,7},{5,6},{6,5},{7,4},{8,11},{9,10},{10,... | collective-permute-start | bytes 393224 | tf_op jit(solution)/shard_map/ppermute | solution.py:19
  64.1 1.1 %collective-permute-done.16 = f32[64,128]{1,0:T(8,128)S(1)} collective-permute-done((f32[64,128]{1,0:T(8,128)S(1)}, f32[64,128]{1,0:T(8,128)S(1)}, u32[]{:S(2)}, u32[]{:S(2)}) %collective-permute-start.16) | collective-permute-done | bytes 32800 | tf_op jit(solution)/shard_map/ppermute | solution.py:19
  65.2 0.5 collective-permute-done.17
  65.8 0.8 %collective-permute-done.18 = f32[4,64,128]{2,1,0:T(8,128)S(1)} collective-permute-done((f32[4,64,128]{2,1,0:T(8,128)S(1)}, f32[4,64,128]{2,1,0:T(8,128)S(1)}, u32[]{:S(2)}, u32[]{:S(2)}) %collective-permute-start.18) | collective-permute-done | bytes 131104 | tf_op jit(solution)/shard_map/ppermute | solution.py:19
  66.6 1.8 %collective-permute-done.19 = f32[4,64,128]{2,1,0:T(8,128)S(1)} collective-permute-done((f32[4,64,128]{2,1,0:T(8,128)S(1)}, f32[4,64,128]{2,1,0:T(8,128)S(1)}, u32[]{:S(2)}, u32[]{:S(2)}) %collective-permute-start.19) | collective-permute-done | bytes 131104 | tf_op jit(solution)/shard_map/ppermute | solution.py:19
  68.4 0.0 copy-start.3
  68.4 0.8 %copy-done.3 = f32[4,4,64,128]{3,2,1,0:T(8,128)} copy-done((f32[4,4,64,128]{3,2,1,0:T(8,128)}, f32[4,4,64,128]{3,2,1,0:T(8,128)S(1)}, u32[]{:S(2)}) %copy-start.3) | copy-done | bytes 524312
  (26 shorter events, 0.2 us)
Async XLA Ops:
  0.6 8.1 %copy-start.2 = (bf16[128,128]{1,0:T(8,128)(2,1)S(1)}, bf16[128,128]{1,0:T(8,128)(2,1)}, u32[]{:S(2)}) copy-start(bf16[128,128]{1,0:T(8,128)(2,1)} %own_ref.1) | copy-start | bytes 98308
  0.6 15.2 %copy-start.1 = (bf16[8,128,128]{2,1,0:T(8,128)(2,1)S(1)}, bf16[8,128,128]{2,1,0:T(8,128)(2,1)}, u32[]{:S(2)}) copy-start(bf16[8,128,128]{2,1,0:T(8,128)(2,1)} %cores_ref.1) | copy-start | bytes 786436
  0.7 8.1 %collective-permute-start = (bf16[128,128]{1,0:T(8,128)(2,1)}, bf16[128,128]{1,0:T(8,128)(2,1)S(1)}, u32[]{:S(2)}, u32[]{:S(2)}) collective-permute-start(bf16[128,128]{1,0:T(8,128)(2,1)} %own_ref.1), channel_id=1, source_target_pairs={{0,4},{1,5},{2,6},{3,7},{4,0},{5,1},{6,2},{7,3},{8,12},{9,13},{10,... | collective-permute-start | bytes 98312 | tf_op jit(solution)/shard_map/ppermute | solution.py:19
  3.8 5.6 %collective-permute-start.1 = (bf16[128,128]{1,0:T(8,128)(2,1)}, bf16[128,128]{1,0:T(8,128)(2,1)S(1)}, u32[]{:S(2)}, u32[]{:S(2)}) collective-permute-start(bf16[128,128]{1,0:T(8,128)(2,1)} %own_ref.1), channel_id=1, source_target_pairs={{0,8},{1,9},{2,10},{3,11},{4,12},{5,13},{6,14},{7,15},{8,0},{9,1},... | collective-permute-start | bytes 98312 | tf_op jit(solution)/shard_map/ppermute | solution.py:19
  6.4 5.9 %collective-permute-start.2 = (bf16[128,128]{1,0:T(8,128)(2,1)}, bf16[128,128]{1,0:T(8,128)(2,1)S(1)}, u32[]{:S(2)}, u32[]{:S(2)}) collective-permute-start(bf16[128,128]{1,0:T(8,128)(2,1)} %own_ref.1), channel_id=1, source_target_pairs={{0,12},{1,13},{2,14},{3,15},{4,8},{5,9},{6,10},{7,11},{8,4},{9,5},... | collective-permute-start | bytes 98312 | tf_op jit(solution)/shard_map/ppermute | solution.py:19
  12.3 8.1 %collective-permute-start.3 = (bf16[512,128]{1,0:T(8,128)(2,1)S(1)}, bf16[512,128]{1,0:T(8,128)(2,1)S(1)}, u32[]{:S(2)}, u32[]{:S(2)}) collective-permute-start(bf16[512,128]{1,0:T(8,128)(2,1)S(1)} %constant_dynamic-update-slice_fusion.column_ref.rest_0_), channel_id=1, source_target_pairs={{0,1},{1,0},{2,3},{3,2},{4,5},{5,4},{6,7},{7,6},{8,9},{9,8},{10,11... | collective-permute-start | bytes 393224 | tf_op jit(solution)/shard_map/ppermute | solution.py:19
  13.8 6.6 %collective-permute-start.4 = (bf16[512,128]{1,0:T(8,128)(2,1)S(1)}, bf16[512,128]{1,0:T(8,128)(2,1)S(1)}, u32[]{:S(2)}, u32[]{:S(2)}) collective-permute-start(bf16[512,128]{1,0:T(8,128)(2,1)S(1)} %constant_dynamic-update-slice_fusion.column_ref.rest_0_), channel_id=1, source_target_pairs={{0,2},{1,3},{2,0},{3,1},{4,6},{5,7},{6,4},{7,5},{8,10},{9,11},{10,... | collective-permute-start | bytes 393224 | tf_op jit(solution)/shard_map/ppermute | solution.py:19
  15.3 5.9 %collective-permute-start.5 = (bf16[512,128]{1,0:T(8,128)(2,1)S(1)}, bf16[512,128]{1,0:T(8,128)(2,1)S(1)}, u32[]{:S(2)}, u32[]{:S(2)}) collective-permute-start(bf16[512,128]{1,0:T(8,128)(2,1)S(1)} %constant_dynamic-update-slice_fusion.column_ref.rest_0_), channel_id=1, source_target_pairs={{0,3},{1,2},{2,1},{3,0},{4,7},{5,6},{6,5},{7,4},{8,11},{9,10},{10,... | collective-permute-start | bytes 393224 | tf_op jit(solution)/shard_map/ppermute | solution.py:19
  15.9 2.2 %copy-start = (bf16[8,128,2048]{2,1,0:T(8,128)(2,1)S(1)}, bf16[8,128,2048]{2,1,0:T(8,128)(2,1)}, u32[]{:S(2)}) copy-start(bf16[8,128,2048]{2,1,0:T(8,128)(2,1)} %facts1_ref.3) | copy-start | bytes 12582916
  32.2 8.9 %collective-permute-start.9 = (f32[1024,128]{1,0:T(8,128)S(1)}, f32[1024,128]{1,0:T(8,128)S(1)}, u32[]{:S(2)}, u32[]{:S(2)}) collective-permute-start(f32[1024,128]{1,0:T(8,128)S(1)} %get-tuple-element.31), channel_id=1, source_target_pairs={{0,16},{16,0},{1,17},{17,1},{2,18},{18,2},{3,19},{19,3},{4,20},{20... | collective-permute-start | bytes 1572872 | tf_op jit(solution)/shard_map/ppermute | solution.py:19
  32.3 5.5 %collective-permute-start.6 = (bf16[256,128]{1,0:T(8,128)(2,1)S(1)}, bf16[256,128]{1,0:T(8,128)(2,1)S(1)}, u32[]{:S(2)}, u32[]{:S(2)}) collective-permute-start(bf16[256,128]{1,0:T(8,128)(2,1)S(1)} %get-tuple-element.26), channel_id=1, source_target_pairs={{0,4},{1,5},{2,6},{3,7},{4,0},{5,1},{6,2},{7,3},{8,12},{9,13},{10,... | collective-permute-start | bytes 196616 | tf_op jit(solution)/shard_map/ppermute | solution.py:19
  32.3 8.7 %collective-permute-start.7 = (bf16[256,128]{1,0:T(8,128)(2,1)S(1)}, bf16[256,128]{1,0:T(8,128)(2,1)S(1)}, u32[]{:S(2)}, u32[]{:S(2)}) collective-permute-start(bf16[256,128]{1,0:T(8,128)(2,1)S(1)} %get-tuple-element.27), channel_id=1, source_target_pairs={{0,8},{1,9},{2,10},{3,11},{4,12},{5,13},{6,14},{7,15},{8,0},{9,1},... | collective-permute-start | bytes 196616 | tf_op jit(solution)/shard_map/ppermute | solution.py:19
  33.7 7.4 %collective-permute-start.8 = (bf16[256,128]{1,0:T(8,128)(2,1)S(1)}, bf16[256,128]{1,0:T(8,128)(2,1)S(1)}, u32[]{:S(2)}, u32[]{:S(2)}) collective-permute-start(bf16[256,128]{1,0:T(8,128)(2,1)S(1)} %get-tuple-element.28), channel_id=1, source_target_pairs={{0,12},{1,13},{2,14},{3,15},{4,8},{5,9},{6,10},{7,11},{8,4},{9,5},... | collective-permute-start | bytes 196616 | tf_op jit(solution)/shard_map/ppermute | solution.py:19
  41.9 6.2 %collective-permute-start.10 = (f32[320,128]{1,0:T(8,128)S(1)}, f32[320,128]{1,0:T(8,128)S(1)}, u32[]{:S(2)}, u32[]{:S(2)}) collective-permute-start(f32[320,128]{1,0:T(8,128)S(1)} %get-tuple-element.33), channel_id=1, source_target_pairs={{0,1},{1,0},{2,3},{3,2},{4,5},{5,4},{6,7},{7,6},{8,9},{9,8},{10,11... | collective-permute-start | bytes 491528 | tf_op jit(solution)/shard_map/ppermute | solution.py:19
  42.7 8.2 %collective-permute-start.11 = (f32[320,128]{1,0:T(8,128)S(1)}, f32[320,128]{1,0:T(8,128)S(1)}, u32[]{:S(2)}, u32[]{:S(2)}) collective-permute-start(f32[320,128]{1,0:T(8,128)S(1)} %get-tuple-element.34), channel_id=1, source_target_pairs={{0,2},{1,3},{2,0},{3,1},{4,6},{5,7},{6,4},{7,5},{8,10},{9,11},{10,... | collective-permute-start | bytes 491528 | tf_op jit(solution)/shard_map/ppermute | solution.py:19
  44.2 6.7 %collective-permute-start.12 = (f32[320,128]{1,0:T(8,128)S(1)}, f32[320,128]{1,0:T(8,128)S(1)}, u32[]{:S(2)}, u32[]{:S(2)}) collective-permute-start(f32[320,128]{1,0:T(8,128)S(1)} %get-tuple-element.35), channel_id=1, source_target_pairs={{0,3},{1,2},{2,1},{3,0},{4,7},{5,6},{6,5},{7,4},{8,11},{9,10},{10,... | collective-permute-start | bytes 491528 | tf_op jit(solution)/shard_map/ppermute | solution.py:19
  51.0 4.5 %collective-permute-start.13 = (f32[128,128]{1,0:T(8,128)S(1)}, f32[128,128]{1,0:T(8,128)S(1)}, u32[]{:S(2)}, u32[]{:S(2)}) collective-permute-start(f32[128,128]{1,0:T(8,128)S(1)} %get-tuple-element.37), channel_id=1, source_target_pairs={{0,4},{1,5},{2,6},{3,7},{4,0},{5,1},{6,2},{7,3},{8,12},{9,13},{10,... | collective-permute-start | bytes 196616 | tf_op jit(solution)/shard_map/ppermute | solution.py:19
  53.0 6.0 %collective-permute-start.14 = (f32[128,128]{1,0:T(8,128)S(1)}, f32[128,128]{1,0:T(8,128)S(1)}, u32[]{:S(2)}, u32[]{:S(2)}) collective-permute-start(f32[128,128]{1,0:T(8,128)S(1)} %get-tuple-element.38), channel_id=1, source_target_pairs={{0,8},{1,9},{2,10},{3,11},{4,12},{5,13},{6,14},{7,15},{8,0},{9,1},... | collective-permute-start | bytes 196616 | tf_op jit(solution)/shard_map/ppermute | solution.py:19
  53.7 6.2 %collective-permute-start.15 = (f32[128,128]{1,0:T(8,128)S(1)}, f32[128,128]{1,0:T(8,128)S(1)}, u32[]{:S(2)}, u32[]{:S(2)}) collective-permute-start(f32[128,128]{1,0:T(8,128)S(1)} %get-tuple-element.39), channel_id=1, source_target_pairs={{0,12},{1,13},{2,14},{3,15},{4,8},{5,9},{6,10},{7,11},{8,4},{9,5},... | collective-permute-start | bytes 196616 | tf_op jit(solution)/shard_map/ppermute | solution.py:19
  60.5 5.3 %collective-permute-start.17 = (f32[4,64,128]{2,1,0:T(8,128)S(1)}, f32[4,64,128]{2,1,0:T(8,128)S(1)}, u32[]{:S(2)}, u32[]{:S(2)}) collective-permute-start(f32[4,64,128]{2,1,0:T(8,128)S(1)} %bitcast.26), channel_id=1, source_target_pairs={{0,1},{1,0},{2,3},{3,2},{4,5},{5,4},{6,7},{7,6},{8,9},{9,8},{10,11... | collective-permute-start | bytes 393224 | tf_op jit(solution)/shard_map/ppermute | solution.py:19
  61.6 5.0 %collective-permute-start.18 = (f32[4,64,128]{2,1,0:T(8,128)S(1)}, f32[4,64,128]{2,1,0:T(8,128)S(1)}, u32[]{:S(2)}, u32[]{:S(2)}) collective-permute-start(f32[4,64,128]{2,1,0:T(8,128)S(1)} %bitcast.27), channel_id=1, source_target_pairs={{0,2},{1,3},{2,0},{3,1},{4,6},{5,7},{6,4},{7,5},{8,10},{9,11},{10,... | collective-permute-start | bytes 393224 | tf_op jit(solution)/shard_map/ppermute | solution.py:19
  62.5 5.9 %collective-permute-start.19 = (f32[4,64,128]{2,1,0:T(8,128)S(1)}, f32[4,64,128]{2,1,0:T(8,128)S(1)}, u32[]{:S(2)}, u32[]{:S(2)}) collective-permute-start(f32[4,64,128]{2,1,0:T(8,128)S(1)} %bitcast.28), channel_id=1, source_target_pairs={{0,3},{1,2},{2,1},{3,0},{4,7},{5,6},{6,5},{7,4},{8,11},{9,10},{10,... | collective-permute-start | bytes 393224 | tf_op jit(solution)/shard_map/ppermute | solution.py:19
  64.0 1.2 %collective-permute-start.16 = (f32[64,128]{1,0:T(8,128)S(1)}, f32[64,128]{1,0:T(8,128)S(1)}, u32[]{:S(2)}, u32[]{:S(2)}) collective-permute-start(f32[64,128]{1,0:T(8,128)S(1)} %get-tuple-element.40), channel_id=1, source_target_pairs={{0,16},{16,0},{1,17},{17,1},{2,18},{18,2},{3,19},{19,3},{4,20},{20... | collective-permute-start | bytes 98312 | tf_op jit(solution)/shard_map/ppermute | solution.py:19
  65.2 3.2 %copy-start.4 = (f32[2,64,128]{2,1,0:T(8,128)}, f32[2,64,128]{2,1,0:T(8,128)S(1)}, u32[]{:S(2)}) copy-start(f32[2,64,128]{2,1,0:T(8,128)S(1)} %bitcast_dynamic-update-slice_fusion.3) | copy-start | bytes 196612
  68.4 0.8 %copy-start.3 = (f32[4,4,64,128]{3,2,1,0:T(8,128)}, f32[4,4,64,128]{3,2,1,0:T(8,128)S(1)}, u32[]{:S(2)}) copy-start(f32[4,4,64,128]{3,2,1,0:T(8,128)S(1)} %bitcast_dynamic-update-slice_fusion) | copy-start | bytes 1572868

commit v3 on v2

--- a/solution.py
+++ b/solution.py
@@ -9,9 +9,12 @@
 
 
 BITS = 13
+STEPS = 128
+TOP = 32700.0
 LANES = 128
 F32 = jnp.float32
 BF16 = jnp.bfloat16
+I16 = jnp.int16
 MIB = 1 << 20
 
 
@@ -171,6 +174,33 @@
             outs[h][pl.ds(dst, sub), :] = total_ref[pl.ds(src, sub), :]
 
 
+def scale_code(block):
+    most = jnp.max(jnp.abs(block), axis=0, keepdims=True)
+    return jnp.ceil(jnp.log2(jnp.maximum(most, 1e-30)) * STEPS).astype(jnp.int32)
+
+
+def encode(block, code):
+    factor = jnp.exp2(code.astype(F32) * (-1.0 / STEPS)) * TOP
+    return jnp.floor(block * factor + 0.5).astype(jnp.int32).astype(jnp.int16)
+
+
+def decode(codes, code):
+    factor = jnp.exp2(code.astype(F32) * (1.0 / STEPS)) * (1.0 / TOP)
+    return codes.astype(jnp.int32).astype(F32) * factor
+
+
+def stack_codes(rows_of):
+    at = lax.broadcasted_iota(jnp.int32, (scale_rows(len(rows_of)), LANES), 0)
+    tile = jnp.zeros(at.shape, jnp.int32)
+    for place, row in rows_of:
+        tile = jnp.where(at == place, jnp.broadcast_to(row, at.shape), tile)
+    return tile.astype(jnp.int16)
+
+
+def scale_rows(blocks):
+    return pl.cdiv(blocks, 16) * 16
+
+
 def merge_kernel(low, high, rel, me_ref, column_ref, *rest):
     pulls, shares, outs = rest[:high], rest[high : high + rel], rest[high + rel : -1]
     total_ref = rest[-1]
@@ -185,40 +215,85 @@
             )
         total_ref[k * rank : (k + 1) * rank, :] = acc
     size = total_ref.shape[0] // low
-    block = shares[0].shape[0] // low
+    sub = shares[0].shape[0] // low // high
     for q in range(low):
-        part = shares[0][q * block : (q + 1) * block, :]
-        for h in range(1, rel):
-            part = part + shares[h][q * block : (q + 1) * block, :]
-        outs[q][:block, :] = part
+        blocks = []
+        for d in range(high):
+            at = slice((q * high + d) * sub, (q * high + d + 1) * sub)
+            part = shares[0][at, :]
+            for h in range(1, rel):
+                part = part + shares[h][at, :]
+            blocks.append(part)
         src = pl.multiple_of(jnp.bitwise_xor(near, q) * size, size)
-        outs[q][block:, :] = total_ref[pl.ds(src, size), :]
+        blocks.append(total_ref[pl.ds(src, size), :])
+        codes, at = [], 0
+        for block in blocks:
+            span = slice(at, at + block.shape[0])
+            if q == 0:
+                outs[q][span, :] = block
+            else:
+                codes.append(scale_code(block))
+                outs[q][span, :] = encode(block, codes[-1])
+            at += block.shape[0]
+        if q > 0:
+            outs[q][at:, :] = stack_codes(list(enumerate(codes)))
 
 
 def near_kernel(low, high, scale, *rest):
-    parts, outs = rest[:low], rest[low:]
-    total = parts[0][...]
-    for q in range(1, low):
-        total = total + parts[q][...]
-    size = total.shape[0] - outs[0].shape[0]
-    sub = size // (high - 1)
-    core = total[high * sub :, :] * scale
+    parts, (owned_ref, core_ref, *outs) = rest[:low], rest[low:]
+    sub = owned_ref.shape[0]
+    size = parts[0].shape[0] - high * sub
+    scales = [part[high * sub + size :, :].astype(jnp.int32) for part in parts[1:]]
+    sums = []
+    for b in range(high + 1):
+        span = slice(b * sub, (b + 1) * sub) if b < high else slice(b * sub, b * sub + size)
+        total = parts[0][span, :]
+        for part, code in zip(parts[1:], scales):
+            total = total + decode(part[span, :], code[b : b + 1, :])
+        sums.append(total)
+    core = sums[high] * scale
+    core_code = scale_code(core)
+    core_codes = encode(core, core_code)
+    owned_ref[...] = sums[0]
+    core_ref[:size, :] = core_codes
+    core_ref[size:, :] = stack_codes([(1, core_code)])
+    for d in range(1, high):
+        code = scale_code(sums[d])
+        out = outs[d - 1]
+        out[:size, :] = core_codes
+        out[size : size + sub, :] = encode(sums[d], code)
+        out[size + sub :, :] = stack_codes([(0, code), (1, core_code)])
+
+
+def far_kernel(low, high, root, me_ref, mine_ref, core_ref, *rest):
+    parts, (owned_ref, column_ref) = rest[:-2], rest[-2:]
+    sub = owned_ref.shape[0]
+    size = parts[0].shape[0] - sub - scale_rows(2)
+    far = me_ref[0] // low
+    total, codes = mine_ref[...], []
     for d in range(high):
-        outs[d][:sub, :] = total[d * sub : (d + 1) * sub, :]
-        outs[d][sub:, :] = core
-
-
-def far_kernel(low, high, root, me_ref, *rest):
-    parts, (owned_ref, column_ref) = rest[:high], rest[high:]
-    sub, size = owned_ref.shape[0], column_ref.shape[0] // high
-    far = me_ref[0] // low
-    total = parts[0][:sub, :]
-    for d in range(1, high):
-        total = total + parts[d][:sub, :]
+        ref = core_ref if d == 0 else parts[d - 1]
+        code = ref[ref.shape[0] - scale_rows(2) :, :].astype(jnp.int32)
+        place = jnp.bitwise_xor(far, d)
+        at = pl.multiple_of(place * size, size)
+        column_ref[pl.ds(at, size), :] = ref[:size, :]
+        codes.append((place, code[1:2, :]))
+        if d > 0:
+            total = total + decode(ref[size : size + sub, :], code[0:1, :])
     owned_ref[...] = total / jnp.sqrt(F32(root))
-    for d in range(high):
-        at = pl.multiple_of(jnp.bitwise_xor(far, d) * size, size)
-        column_ref[pl.ds(at, size), :] = parts[d][sub:, :]
+    column_ref[high * size :, :] = stack_codes(codes)
+
+
+def place_kernel(low, high, me_ref, *rest):
+    columns, out_ref = rest[:-1], rest[-1]
+    size = out_ref.shape[0] // low // high
+    near = jnp.bitwise_and(me_ref[0], low - 1)
+    for q in range(low):
+        codes = columns[q][high * size :, :].astype(jnp.int32)
+        for d in range(high):
+            block = decode(columns[q][d * size : (d + 1) * size, :], codes[d : d + 1, :])
+            at = pl.multiple_of((d * low + jnp.bitwise_xor(near, q)) * size, size)
+            out_ref[pl.ds(at, size), :] = block
 
 
 def gradients(facts, observed, factors, cores):
@@ -351,29 +426,31 @@
         functools.partial(merge_kernel, low, high, rel),
         in_specs=[pl.BlockSpec(memory_space=pltpu.SMEM)]
         + [pl.BlockSpec(memory_space=pltpu.VMEM)] * (1 + high + rel),
-        out_shape=[shape((high * sub + size, rank), F32)] * low,
+        out_shape=[shape((high * sub + size, rank), F32)]
+        + [shape((high * sub + size + scale_rows(high + 1), rank), I16)] * (low - 1),
         scratch_shapes=[pltpu.VMEM((per * rank, rank), F32)],
         compiler_params=pltpu.CompilerParams(vmem_limit_bytes=8 * MIB),
         name="merge_kernel",
     )(me, column, *pulls, *shares)
     merged = from_partners(merged[0], low, lambda q: near_swap(merged[q], q))
 
-    parts = pl.pallas_call(
+    mine, core_codes, *parts = pl.pallas_call(
         functools.partial(near_kernel, low, high, rank / n_all),
-        out_shape=[shape((sub + size, rank), F32)] * high,
+        out_shape=[shape((sub, rank), F32), shape((size + scale_rows(2), rank), I16)]
+        + [shape((sub + size + scale_rows(2), rank), I16)] * (high - 1),
         compiler_params=pltpu.CompilerParams(vmem_limit_bytes=6 * MIB),
         name="near_kernel",
     )(*merged)
-    parts = from_partners(parts[0], high, lambda d: far_swap(parts[d], d))
+    parts = from_partners(None, high, lambda d: far_swap(parts[d - 1], d))[1:]
 
     owned, core_column = pl.pallas_call(
         functools.partial(far_kernel, low, high, n_all * relations * rel),
         in_specs=[pl.BlockSpec(memory_space=pltpu.SMEM)]
-        + [pl.BlockSpec(memory_space=pltpu.VMEM)] * high,
-        out_shape=[shape((sub, rank), F32), shape((high * size, rank), F32)],
+        + [pl.BlockSpec(memory_space=pltpu.VMEM)] * (high + 1),
+        out_shape=[shape((sub, rank), F32), shape((high * size + scale_rows(high), rank), I16)],
         compiler_params=pltpu.CompilerParams(vmem_limit_bytes=4 * MIB),
         name="far_kernel",
-    )(me, *parts)
+    )(me, mine, core_codes, *parts)
 
     grad_factors = jnp.zeros((rel, sub, rank), F32)
     for h in range(rel):
@@ -381,11 +458,15 @@
         grad_factors = lax.dynamic_update_index_in_dim(grad_factors, piece, here ^ h, 0)
     grad_factors = grad_factors.reshape(rows, rank)
 
-    grad_cores = jnp.zeros((high, low, size, rank), F32)
-    near = lax.axis_index("ent") & (low - 1)
-    core_column = core_column.reshape(high, size, rank)
-    for q, piece in enumerate(from_partners(core_column, low, lambda q: near_swap(core_column, q))):
-        grad_cores = lax.dynamic_update_index_in_dim(grad_cores, piece, near ^ q, 1)
+    columns = from_partners(core_column, low, lambda q: near_swap(core_column, q))
+    grad_cores = pl.pallas_call(
+        functools.partial(place_kernel, low, high),
+        in_specs=[pl.BlockSpec(memory_space=pltpu.SMEM)]
+        + [pl.BlockSpec(memory_space=pltpu.VMEM)] * low,
+        out_shape=shape((relations * rank, rank), F32),
+        compiler_params=pltpu.CompilerParams(vmem_limit_bytes=4 * MIB),
+        name="place_kernel",
+    )(me, *columns)
     return grad_factors, grad_cores.reshape(relations, rank, rank)
 
 

time: 69.4 us -> 67.2 us (0.968)
  waiting for transfers between devices: 22.8 us -> 19.9 us
  Pallas kernels: 14.7 us -> 16.3 us
  local copies, waits for them, and re-layouts: 5.39 us -> 4.52 us
    ppermute x20, waiting for transfers between devices: 22.8 us -> 19.9 us  [swap(): return lax.ppermute(x, axis, [(i, i ^ distance) for i in range(size)])]
    pallas_call x0 -> x1, Pallas kernels: none -> 1.39 us  [gradients(): pl.pallas_call(functools.partial(place_kernel, low, high), in_specs=[pl.B...]
    unnamed x15 -> x13, local copies, waits for them, and re-layouts: 3.71 us -> 2.93 us
where the time goes in v3:
time: 67.2 us; the launch traced here: 67 us
  starting transfers between devices  25.3 us (38%)
  waiting for transfers between devices  19.9 us (30%)
  Pallas kernels  16.3 us (24%)
  local copies, waits for them, and re-layouts  4.52 us (7%)
  between operations  0.82 us (1%)
    ppermute x20, starting transfers between devices, swap(): return lax.ppermute(x, axis, [(i, i ^ distance) for i in range(size)])  25.3 us
    ppermute x20, waiting for transfers between devices, swap(): return lax.ppermute(x, axis, [(i, i ^ distance) for i in range(size)])  19.9 us
    pallas_call x1, Pallas kernels, gradients(): rows_call(me, err, left, cores.reshape(relations * rank, rank), column, *...  5.78 us
    pallas_call x1, Pallas kernels, gradients(): pl.pallas_call(functools.partial(late_kernel, low, high, first), grid_spe...  5.21 us
    unnamed x13, local copies, waits for them, and re-layouts  2.93 us
    pallas_call x1, Pallas kernels, gradients(): pl.pallas_call(functools.partial(early_kernel, low, high), grid_spec=pltp...  2.29 us
    slice x1, local copies, waits for them, and re-layouts, gradients(): packed = observed[:, :half] | jnp.left_shift(observed[:, half:], 16)  1.53 us
    pallas_call x1, Pallas kernels, gradients(): pl.pallas_call(functools.partial(place_kernel, low, high), in_specs=[pl.B...  1.39 us
  transfers between devices with their start and end apart: 20, of which 13 were waited for; matrix products, arithmetic and copies ran while one was open for 4% of the time, Pallas kernels for 3%

profile of v3, /device:TPU:0, one launch (start us, length us, event | category | flops | bytes accessed | tf_op | source)
XLA Modules:
  0.0 67.0 jit_solution(12052842243195059931)
XLA Ops:
  0.7 3.1 %collective-permute-start = (bf16[128,128]{1,0:T(8,128)(2,1)}, bf16[128,128]{1,0:T(8,128)(2,1)S(1)}, u32[]{:S(2)}, u32[]{:S(2)}) collective-permute-start(bf16[128,128]{1,0:T(8,128)(2,1)} %own_ref.1), channel_id=1, source_target_pairs={{0,4},{1,5},{2,6},{3,7},{4,0},{5,1},{6,2},{7,3},{8,12},{9,13},{10,... | collective-permute-start | bytes 98312 | tf_op jit(solution)/shard_map/ppermute | solution.py:22
  3.8 2.6 %collective-permute-start.1 = (bf16[128,128]{1,0:T(8,128)(2,1)}, bf16[128,128]{1,0:T(8,128)(2,1)S(1)}, u32[]{:S(2)}, u32[]{:S(2)}) collective-permute-start(bf16[128,128]{1,0:T(8,128)(2,1)} %own_ref.1), channel_id=1, source_target_pairs={{0,8},{1,9},{2,10},{3,11},{4,12},{5,13},{6,14},{7,15},{8,0},{9,1},... | collective-permute-start | bytes 98312 | tf_op jit(solution)/shard_map/ppermute | solution.py:22
  6.4 1.5 %fusion = (s32[8,64,158]{1,0,2:T(8,128)S(1)}, s32[8,64,158]{1,0,2:T(8,128)S(1)}) fusion(s32[8,128,158]{1,0,2:T(8,128)} %param.5), kind=kLoop, calls=%fused_computation.8 | loop fusion | bytes 1294336 | tf_op jit(solution)/shard_map/slice | solution.py:319
  7.9 0.4 copy.10
  8.2 0.3 copy.9
  8.6 0.1 shift-left_or_fusion
  8.8 0.0 collective-permute-done
  8.8 0.6 collective-permute-done.1
  9.4 2.9 %collective-permute-done.2 = bf16[128,128]{1,0:T(8,128)(2,1)S(1)} collective-permute-done((bf16[128,128]{1,0:T(8,128)(2,1)}, bf16[128,128]{1,0:T(8,128)(2,1)S(1)}, u32[]{:S(2)}, u32[]{:S(2)}) %collective-permute-start.2) | collective-permute-done | bytes 32800 | tf_op jit(solution)/shard_map/ppermute | solution.py:22
  12.3 1.5 %collective-permute-start.3 = (bf16[512,128]{1,0:T(8,128)(2,1)S(1)}, bf16[512,128]{1,0:T(8,128)(2,1)S(1)}, u32[]{:S(2)}, u32[]{:S(2)}) collective-permute-start(bf16[512,128]{1,0:T(8,128)(2,1)S(1)} %constant_dynamic-update-slice_fusion.column_ref.rest_0_), channel_id=1, source_target_pairs={{0,1},{1,0},{2,3},{3,2},{4,5},{5,4},{6,7},{7,6},{8,9},{9,8},{10,11... | collective-permute-start | bytes 393224 | tf_op jit(solution)/shard_map/ppermute | solution.py:22
  13.8 1.5 %collective-permute-start.4 = (bf16[512,128]{1,0:T(8,128)(2,1)S(1)}, bf16[512,128]{1,0:T(8,128)(2,1)S(1)}, u32[]{:S(2)}, u32[]{:S(2)}) collective-permute-start(bf16[512,128]{1,0:T(8,128)(2,1)S(1)} %constant_dynamic-update-slice_fusion.column_ref.rest_0_), channel_id=1, source_target_pairs={{0,2},{1,3},{2,0},{3,1},{4,6},{5,7},{6,4},{7,5},{8,10},{9,11},{10,... | collective-permute-start | bytes 393224 | tf_op jit(solution)/shard_map/ppermute | solution.py:22
  15.3 0.5 collective-permute-start.5
  15.8 0.1 pad_add_fusion.me_ref
  15.9 2.2 %copy-done = bf16[8,128,2048]{2,1,0:T(8,128)(2,1)S(1)} copy-done((bf16[8,128,2048]{2,1,0:T(8,128)(2,1)S(1)}, bf16[8,128,2048]{2,1,0:T(8,128)(2,1)}, u32[]{:S(2)}) %copy-start) | copy-done | bytes 4194328
  18.0 2.3 %early_kernel.1 = (bf16[8,1024,256]{2,1,0:T(8,128)(2,1)S(1)}, bf16[1024,128]{1,0:T(8,128)(2,1)S(1)}, f32[1024,128]{1,0:T(8,128)S(1)}) custom-call(s32[2]{0:T(128)S(1)} %pad_add_fusion.me_ref, s32[8,64,256]{2,1,0:T(8,128)S(1)} %pad.4.words_ref, bf16[8,128,2048]{2,1,0:T(8,128)(2,1)S(1)} %copy-done, bf16[8,128,2048]{2,1,0:T(8,128)(2,1)S(1)} %copy-done, ...), custom_call_target="tpu_custom_call" | custom-call | flops 268435456 | bytes 2097152 | tf_op jit(solution)/shard_map/early_kernel/pallas_call | solution.py:340
  20.3 0.0 collective-permute-done.3.rest_0_.rest_1_
  20.4 0.8 %collective-permute-done.5.rest_2_.rest_3_ = bf16[512,128]{1,0:T(8,128)(2,1)S(1)} collective-permute-done((bf16[512,128]{1,0:T(8,128)(2,1)S(1)}, bf16[512,128]{1,0:T(8,128)(2,1)S(1)}, u32[]{:S(2)}, u32[]{:S(2)}) %collective-permute-start.5) | collective-permute-done | bytes 131104 | tf_op jit(solution)/shard_map/ppermute | solution.py:22
  21.2 5.2 %late_kernel.1 = (bf16[8,1024,256]{2,1,0:T(8,128)(2,1)S(1)}, bf16[256,128]{1,0:T(8,128)(2,1)S(1)}, bf16[256,128]{1,0:T(8,128)(2,1)S(1)}, bf16[256,128]{1,0:T(8,128)(2,1)S(1)}, bf16[256,128]{1,0:T(8,128)(2,1)S(1)}) custom-call(s32[2]{0:T(128)S(1)} %pad_add_fusion.me_ref, s32[8,64,256]{2,1,0:T(8,128)S(1)} %pad.4.words_ref, ...), custom_call_target="tpu_custom_call", output_to_operand_aliasing={{0}: (6, {})} | custom-call | flops 805306368 | bytes 6291456 | tf_op jit(solution)/shard_map/late_kernel/pallas_call | solution.py:369
  26.4 5.8 %rows_kernel.1 = (f32[1024,128]{1,0:T(8,128)S(1)}, f32[1024,128]{1,0:T(8,128)S(1)}) custom-call(s32[2]{0:T(128)S(1)} %pad_add_fusion.me_ref, bf16[8,1024,256]{2,1,0:T(8,128)(2,1)S(1)} %get-tuple-element.30.err_ref, bf16[1024,128]{1,0:T(8,128)(2,1)S(1)} %get-tuple-element.23.left_ref, bf16[1024,128]{1,0:T(8,128)(2,1)S(1)} %bitcast.9, ...), custom_call_target="tpu_custom_call" | custom-call | flops 1610612736 | bytes 12582912 | tf_op jit(solution)/shard_map/rows_kernel/pallas_call | solution.py:421
  32.2 0.1 collective-permute-start.9
  32.3 0.1 collective-permute-start.6
  32.3 1.3 %collective-permute-start.7 = (bf16[256,128]{1,0:T(8,128)(2,1)S(1)}, bf16[256,128]{1,0:T(8,128)(2,1)S(1)}, u32[]{:S(2)}, u32[]{:S(2)}) collective-permute-start(bf16[256,128]{1,0:T(8,128)(2,1)S(1)} %get-tuple-element.28), channel_id=1, source_target_pairs={{0,8},{1,9},{2,10},{3,11},{4,12},{5,13},{6,14},{7,15},{8,0},{9,1},... | collective-permute-start | bytes 196616 | tf_op jit(solution)/shard_map/ppermute | solution.py:22
  33.7 3.0 %collective-permute-start.8 = (bf16[256,128]{1,0:T(8,128)(2,1)S(1)}, bf16[256,128]{1,0:T(8,128)(2,1)S(1)}, u32[]{:S(2)}, u32[]{:S(2)}) collective-permute-start(bf16[256,128]{1,0:T(8,128)(2,1)S(1)} %get-tuple-element.29), channel_id=1, source_target_pairs={{0,12},{1,13},{2,14},{3,15},{4,8},{5,9},{6,10},{7,11},{8,4},{9,5},... | collective-permute-start | bytes 196616 | tf_op jit(solution)/shard_map/ppermute | solution.py:22
  36.7 1.1 %collective-permute-done.6.rest_1_ = bf16[256,128]{1,0:T(8,128)(2,1)S(1)} collective-permute-done((bf16[256,128]{1,0:T(8,128)(2,1)S(1)}, bf16[256,128]{1,0:T(8,128)(2,1)S(1)}, u32[]{:S(2)}, u32[]{:S(2)}) %collective-permute-start.6) | collective-permute-done | bytes 65568 | tf_op jit(solution)/shard_map/ppermute | solution.py:22
  37.8 3.3 %collective-permute-done.7.rest_2_ = bf16[256,128]{1,0:T(8,128)(2,1)S(1)} collective-permute-done((bf16[256,128]{1,0:T(8,128)(2,1)S(1)}, bf16[256,128]{1,0:T(8,128)(2,1)S(1)}, u32[]{:S(2)}, u32[]{:S(2)}) %collective-permute-start.7) | collective-permute-done | bytes 65568 | tf_op jit(solution)/shard_map/ppermute | solution.py:22
  41.1 0.0 collective-permute-done.8.rest_3_
  41.1 0.0 collective-permute-done.9.rest_5_
  41.1 0.9 %merge_kernel.1 = (f32[320,128]{1,0:T(8,128)S(1)}, s16[336,128]{1,0:T(8,128)(2,1)S(1)}, s16[336,128]{1,0:T(8,128)(2,1)S(1)}, s16[336,128]{1,0:T(8,128)(2,1)S(1)}) custom-call(s32[2]{0:T(128)S(1)} %pad_add_fusion.me_ref, bf16[512,128]{1,0:T(8,128)(2,1)S(1)} %constant_dynamic-update-slice_fusion.column_ref.rest_0_, ...), custom_call_target="tpu_custom_call" | custom-call | tf_op jit(solution)/shard_map/merge_kernel/pallas_call | solution.py:425
  42.0 0.8 %collective-permute-start.10 = (s16[336,128]{1,0:T(8,128)(2,1)S(1)}, s16[336,128]{1,0:T(8,128)(2,1)S(1)}, u32[]{:S(2)}, u32[]{:S(2)}) collective-permute-start(s16[336,128]{1,0:T(8,128)(2,1)S(1)} %get-tuple-element.34), channel_id=1, source_target_pairs={{0,1},{1,0},{2,3},{3,2},{4,5},{5,4},{6,7},{7,6},{8,9},{9,8},{10,11... | collective-permute-start | bytes 258056 | tf_op jit(solution)/shard_map/ppermute | solution.py:22
  42.8 1.5 %collective-permute-start.11 = (s16[336,128]{1,0:T(8,128)(2,1)S(1)}, s16[336,128]{1,0:T(8,128)(2,1)S(1)}, u32[]{:S(2)}, u32[]{:S(2)}) collective-permute-start(s16[336,128]{1,0:T(8,128)(2,1)S(1)} %get-tuple-element.35), channel_id=1, source_target_pairs={{0,2},{1,3},{2,0},{3,1},{4,6},{5,7},{6,4},{7,5},{8,10},{9,11},{10,... | collective-permute-start | bytes 258056 | tf_op jit(solution)/shard_map/ppermute | solution.py:22
  44.3 1.2 %collective-permute-start.12 = (s16[336,128]{1,0:T(8,128)(2,1)S(1)}, s16[336,128]{1,0:T(8,128)(2,1)S(1)}, u32[]{:S(2)}, u32[]{:S(2)}) collective-permute-start(s16[336,128]{1,0:T(8,128)(2,1)S(1)} %get-tuple-element.36), channel_id=1, source_target_pairs={{0,3},{1,2},{2,1},{3,0},{4,7},{5,6},{6,5},{7,4},{8,11},{9,10},{10,... | collective-permute-start | bytes 258056 | tf_op jit(solution)/shard_map/ppermute | solution.py:22
  45.6 1.0 %collective-permute-done.10.rest_1_ = s16[336,128]{1,0:T(8,128)(2,1)S(1)} collective-permute-done((s16[336,128]{1,0:T(8,128)(2,1)S(1)}, s16[336,128]{1,0:T(8,128)(2,1)S(1)}, u32[]{:S(2)}, u32[]{:S(2)}) %collective-permute-start.10) | collective-permute-done | bytes 86048 | tf_op jit(solution)/shard_map/ppermute | solution.py:22
  46.6 1.0 %collective-permute-done.11.rest_2_ = s16[336,128]{1,0:T(8,128)(2,1)S(1)} collective-permute-done((s16[336,128]{1,0:T(8,128)(2,1)S(1)}, s16[336,128]{1,0:T(8,128)(2,1)S(1)}, u32[]{:S(2)}, u32[]{:S(2)}) %collective-permute-start.11) | collective-permute-done | bytes 86048 | tf_op jit(solution)/shard_map/ppermute | solution.py:22
  47.6 2.1 %collective-permute-done.12.rest_3_ = s16[336,128]{1,0:T(8,128)(2,1)S(1)} collective-permute-done((s16[336,128]{1,0:T(8,128)(2,1)S(1)}, s16[336,128]{1,0:T(8,128)(2,1)S(1)}, u32[]{:S(2)}, u32[]{:S(2)}) %collective-permute-start.12) | collective-permute-done | bytes 86048 | tf_op jit(solution)/shard_map/ppermute | solution.py:22
  49.7 0.1 near_kernel.1
  49.8 1.4 %collective-permute-start.13 = (s16[144,128]{1,0:T(8,128)(2,1)S(1)}, s16[144,128]{1,0:T(8,128)(2,1)S(1)}, u32[]{:S(2)}, u32[]{:S(2)}) collective-permute-start(s16[144,128]{1,0:T(8,128)(2,1)S(1)} %get-tuple-element.39), channel_id=1, source_target_pairs={{0,4},{1,5},{2,6},{3,7},{4,0},{5,1},{6,2},{7,3},{8,12},{9,13},{10,... | collective-permute-start | bytes 110600 | tf_op jit(solution)/shard_map/ppermute | solution.py:22
  51.3 0.9 %collective-permute-start.14 = (s16[144,128]{1,0:T(8,128)(2,1)S(1)}, s16[144,128]{1,0:T(8,128)(2,1)S(1)}, u32[]{:S(2)}, u32[]{:S(2)}) collective-permute-start(s16[144,128]{1,0:T(8,128)(2,1)S(1)} %get-tuple-element.40), channel_id=1, source_target_pairs={{0,8},{1,9},{2,10},{3,11},{4,12},{5,13},{6,14},{7,15},{8,0},{9,1},... | collective-permute-start | bytes 110600 | tf_op jit(solution)/shard_map/ppermute | solution.py:22
  52.2 2.1 %collective-permute-start.15 = (s16[144,128]{1,0:T(8,128)(2,1)S(1)}, s16[144,128]{1,0:T(8,128)(2,1)S(1)}, u32[]{:S(2)}, u32[]{:S(2)}) collective-permute-start(s16[144,128]{1,0:T(8,128)(2,1)S(1)} %get-tuple-element.41), channel_id=1, source_target_pairs={{0,12},{1,13},{2,14},{3,15},{4,8},{5,9},{6,10},{7,11},{8,4},{9,5},... | collective-permute-start | bytes 110600 | tf_op jit(solution)/shard_map/ppermute | solution.py:22
  54.3 2.2 %collective-permute-done.14.rest_1_ = s16[144,128]{1,0:T(8,128)(2,1)S(1)} collective-permute-done((s16[144,128]{1,0:T(8,128)(2,1)S(1)}, s16[144,128]{1,0:T(8,128)(2,1)S(1)}, u32[]{:S(2)}, u32[]{:S(2)}) %collective-permute-start.14) | collective-permute-done | bytes 36896 | tf_op jit(solution)/shard_map/ppermute | solution.py:22
  56.5 1.4 %collective-permute-done.15.rest_2_ = s16[144,128]{1,0:T(8,128)(2,1)S(1)} collective-permute-done((s16[144,128]{1,0:T(8,128)(2,1)S(1)}, s16[144,128]{1,0:T(8,128)(2,1)S(1)}, u32[]{:S(2)}, u32[]{:S(2)}) %collective-permute-start.15) | collective-permute-done | bytes 36896 | tf_op jit(solution)/shard_map/ppermute | solution.py:22
  57.9 0.6 far_kernel.1
  58.5 0.6 collective-permute-start.17
  59.1 1.2 %collective-permute-start.18 = (s16[272,128]{1,0:T(8,128)(2,1)S(1)}, s16[272,128]{1,0:T(8,128)(2,1)S(1)}, u32[]{:S(2)}, u32[]{:S(2)}) collective-permute-start(s16[272,128]{1,0:T(8,128)(2,1)S(1)} %get-tuple-element.43.rest_0_), channel_id=1, source_target_pairs={{0,2},{1,3},{2,0},{3,1},{4,6},{5,7},{6,4},{7,5},{8,10},{9,11},{10,... | collective-permute-start | bytes 208904 | tf_op jit(solution)/shard_map/ppermute | solution.py:22
  60.4 1.7 %collective-permute-start.19 = (s16[272,128]{1,0:T(8,128)(2,1)S(1)}, s16[272,128]{1,0:T(8,128)(2,1)S(1)}, u32[]{:S(2)}, u32[]{:S(2)}) collective-permute-start(s16[272,128]{1,0:T(8,128)(2,1)S(1)} %get-tuple-element.43.rest_0_), channel_id=1, source_target_pairs={{0,3},{1,2},{2,1},{3,0},{4,7},{5,6},{6,5},{7,4},{8,11},{9,10},{10,... | collective-permute-start | bytes 208904 | tf_op jit(solution)/shard_map/ppermute | solution.py:22
  62.1 1.2 %collective-permute-done.16 = f32[64,128]{1,0:T(8,128)S(1)} collective-permute-done((f32[64,128]{1,0:T(8,128)S(1)}, f32[64,128]{1,0:T(8,128)S(1)}, u32[]{:S(2)}, u32[]{:S(2)}) %collective-permute-start.16) | collective-permute-done | bytes 32800 | tf_op jit(solution)/shard_map/ppermute | solution.py:22
  63.3 0.2 collective-permute-done.18.rest_2_
  63.5 2.1 %collective-permute-done.19.rest_3_ = s16[272,128]{1,0:T(8,128)(2,1)S(1)} collective-permute-done((s16[272,128]{1,0:T(8,128)(2,1)S(1)}, s16[272,128]{1,0:T(8,128)(2,1)S(1)}, u32[]{:S(2)}, u32[]{:S(2)}) %collective-permute-start.19) | collective-permute-done | bytes 69664 | tf_op jit(solution)/shard_map/ppermute | solution.py:22
  65.6 1.4 %place_kernel.1 = f32[1024,128]{1,0:T(8,128)} custom-call(s32[2]{0:T(128)S(1)} %pad_add_fusion.me_ref, s16[272,128]{1,0:T(8,128)(2,1)S(1)} %get-tuple-element.43.rest_0_, s16[272,128]{1,0:T(8,128)(2,1)S(1)} %collective-permute-done.17.rest_1_, s16[272,128]{1,0:T(8,128)(2,1)S(1)} %collective-permute-done.18.rest_2_, ...), custom_call_target="tpu_custom_call" | custom-call | tf_op jit(solution)/shard_map/place_kernel/pallas_call | solution.py:462
  (20 shorter events, 0.1 us)
Async XLA Ops:
  0.6 8.1 %copy-start.2 = (bf16[128,128]{1,0:T(8,128)(2,1)S(1)}, bf16[128,128]{1,0:T(8,128)(2,1)}, u32[]{:S(2)}) copy-start(bf16[128,128]{1,0:T(8,128)(2,1)} %own_ref.1) | copy-start | bytes 98308
  0.6 15.2 %copy-start.1 = (bf16[8,128,128]{2,1,0:T(8,128)(2,1)S(1)}, bf16[8,128,128]{2,1,0:T(8,128)(2,1)}, u32[]{:S(2)}) copy-start(bf16[8,128,128]{2,1,0:T(8,128)(2,1)} %cores_ref.1) | copy-start | bytes 786436
  0.7 8.1 %collective-permute-start = (bf16[128,128]{1,0:T(8,128)(2,1)}, bf16[128,128]{1,0:T(8,128)(2,1)S(1)}, u32[]{:S(2)}, u32[]{:S(2)}) collective-permute-start(bf16[128,128]{1,0:T(8,128)(2,1)} %own_ref.1), channel_id=1, source_target_pairs={{0,4},{1,5},{2,6},{3,7},{4,0},{5,1},{6,2},{7,3},{8,12},{9,13},{10,... | collective-permute-start | bytes 98312 | tf_op jit(solution)/shard_map/ppermute | solution.py:22
  3.8 5.6 %collective-permute-start.1 = (bf16[128,128]{1,0:T(8,128)(2,1)}, bf16[128,128]{1,0:T(8,128)(2,1)S(1)}, u32[]{:S(2)}, u32[]{:S(2)}) collective-permute-start(bf16[128,128]{1,0:T(8,128)(2,1)} %own_ref.1), channel_id=1, source_target_pairs={{0,8},{1,9},{2,10},{3,11},{4,12},{5,13},{6,14},{7,15},{8,0},{9,1},... | collective-permute-start | bytes 98312 | tf_op jit(solution)/shard_map/ppermute | solution.py:22
  6.4 5.9 %collective-permute-start.2 = (bf16[128,128]{1,0:T(8,128)(2,1)}, bf16[128,128]{1,0:T(8,128)(2,1)S(1)}, u32[]{:S(2)}, u32[]{:S(2)}) collective-permute-start(bf16[128,128]{1,0:T(8,128)(2,1)} %own_ref.1), channel_id=1, source_target_pairs={{0,12},{1,13},{2,14},{3,15},{4,8},{5,9},{6,10},{7,11},{8,4},{9,5},... | collective-permute-start | bytes 98312 | tf_op jit(solution)/shard_map/ppermute | solution.py:22
  12.3 8.1 %collective-permute-start.3 = (bf16[512,128]{1,0:T(8,128)(2,1)S(1)}, bf16[512,128]{1,0:T(8,128)(2,1)S(1)}, u32[]{:S(2)}, u32[]{:S(2)}) collective-permute-start(bf16[512,128]{1,0:T(8,128)(2,1)S(1)} %constant_dynamic-update-slice_fusion.column_ref.rest_0_), channel_id=1, source_target_pairs={{0,1},{1,0},{2,3},{3,2},{4,5},{5,4},{6,7},{7,6},{8,9},{9,8},{10,11... | collective-permute-start | bytes 393224 | tf_op jit(solution)/shard_map/ppermute | solution.py:22
  13.8 6.6 %collective-permute-start.4 = (bf16[512,128]{1,0:T(8,128)(2,1)S(1)}, bf16[512,128]{1,0:T(8,128)(2,1)S(1)}, u32[]{:S(2)}, u32[]{:S(2)}) collective-permute-start(bf16[512,128]{1,0:T(8,128)(2,1)S(1)} %constant_dynamic-update-slice_fusion.column_ref.rest_0_), channel_id=1, source_target_pairs={{0,2},{1,3},{2,0},{3,1},{4,6},{5,7},{6,4},{7,5},{8,10},{9,11},{10,... | collective-permute-start | bytes 393224 | tf_op jit(solution)/shard_map/ppermute | solution.py:22
  15.3 5.9 %collective-permute-start.5 = (bf16[512,128]{1,0:T(8,128)(2,1)S(1)}, bf16[512,128]{1,0:T(8,128)(2,1)S(1)}, u32[]{:S(2)}, u32[]{:S(2)}) collective-permute-start(bf16[512,128]{1,0:T(8,128)(2,1)S(1)} %constant_dynamic-update-slice_fusion.column_ref.rest_0_), channel_id=1, source_target_pairs={{0,3},{1,2},{2,1},{3,0},{4,7},{5,6},{6,5},{7,4},{8,11},{9,10},{10,... | collective-permute-start | bytes 393224 | tf_op jit(solution)/shard_map/ppermute | solution.py:22
  15.9 2.2 %copy-start = (bf16[8,128,2048]{2,1,0:T(8,128)(2,1)S(1)}, bf16[8,128,2048]{2,1,0:T(8,128)(2,1)}, u32[]{:S(2)}) copy-start(bf16[8,128,2048]{2,1,0:T(8,128)(2,1)} %facts1_ref.3) | copy-start | bytes 12582916
  32.2 8.9 %collective-permute-start.9 = (f32[1024,128]{1,0:T(8,128)S(1)}, f32[1024,128]{1,0:T(8,128)S(1)}, u32[]{:S(2)}, u32[]{:S(2)}) collective-permute-start(f32[1024,128]{1,0:T(8,128)S(1)} %get-tuple-element.32), channel_id=1, source_target_pairs={{0,16},{16,0},{1,17},{17,1},{2,18},{18,2},{3,19},{19,3},{4,20},{20... | collective-permute-start | bytes 1572872 | tf_op jit(solution)/shard_map/ppermute | solution.py:22
  32.3 5.5 %collective-permute-start.6 = (bf16[256,128]{1,0:T(8,128)(2,1)S(1)}, bf16[256,128]{1,0:T(8,128)(2,1)S(1)}, u32[]{:S(2)}, u32[]{:S(2)}) collective-permute-start(bf16[256,128]{1,0:T(8,128)(2,1)S(1)} %get-tuple-element.27), channel_id=1, source_target_pairs={{0,4},{1,5},{2,6},{3,7},{4,0},{5,1},{6,2},{7,3},{8,12},{9,13},{10,... | collective-permute-start | bytes 196616 | tf_op jit(solution)/shard_map/ppermute | solution.py:22
  32.3 8.7 %collective-permute-start.7 = (bf16[256,128]{1,0:T(8,128)(2,1)S(1)}, bf16[256,128]{1,0:T(8,128)(2,1)S(1)}, u32[]{:S(2)}, u32[]{:S(2)}) collective-permute-start(bf16[256,128]{1,0:T(8,128)(2,1)S(1)} %get-tuple-element.28), channel_id=1, source_target_pairs={{0,8},{1,9},{2,10},{3,11},{4,12},{5,13},{6,14},{7,15},{8,0},{9,1},... | collective-permute-start | bytes 196616 | tf_op jit(solution)/shard_map/ppermute | solution.py:22
  33.7 7.4 %collective-permute-start.8 = (bf16[256,128]{1,0:T(8,128)(2,1)S(1)}, bf16[256,128]{1,0:T(8,128)(2,1)S(1)}, u32[]{:S(2)}, u32[]{:S(2)}) collective-permute-start(bf16[256,128]{1,0:T(8,128)(2,1)S(1)} %get-tuple-element.29), channel_id=1, source_target_pairs={{0,12},{1,13},{2,14},{3,15},{4,8},{5,9},{6,10},{7,11},{8,4},{9,5},... | collective-permute-start | bytes 196616 | tf_op jit(solution)/shard_map/ppermute | solution.py:22
  42.0 4.6 %collective-permute-start.10 = (s16[336,128]{1,0:T(8,128)(2,1)S(1)}, s16[336,128]{1,0:T(8,128)(2,1)S(1)}, u32[]{:S(2)}, u32[]{:S(2)}) collective-permute-start(s16[336,128]{1,0:T(8,128)(2,1)S(1)} %get-tuple-element.34), channel_id=1, source_target_pairs={{0,1},{1,0},{2,3},{3,2},{4,5},{5,4},{6,7},{7,6},{8,9},{9,8},{10,11... | collective-permute-start | bytes 258056 | tf_op jit(solution)/shard_map/ppermute | solution.py:22
  42.8 4.8 %collective-permute-start.11 = (s16[336,128]{1,0:T(8,128)(2,1)S(1)}, s16[336,128]{1,0:T(8,128)(2,1)S(1)}, u32[]{:S(2)}, u32[]{:S(2)}) collective-permute-start(s16[336,128]{1,0:T(8,128)(2,1)S(1)} %get-tuple-element.35), channel_id=1, source_target_pairs={{0,2},{1,3},{2,0},{3,1},{4,6},{5,7},{6,4},{7,5},{8,10},{9,11},{10,... | collective-permute-start | bytes 258056 | tf_op jit(solution)/shard_map/ppermute | solution.py:22
  44.3 5.4 %collective-permute-start.12 = (s16[336,128]{1,0:T(8,128)(2,1)S(1)}, s16[336,128]{1,0:T(8,128)(2,1)S(1)}, u32[]{:S(2)}, u32[]{:S(2)}) collective-permute-start(s16[336,128]{1,0:T(8,128)(2,1)S(1)} %get-tuple-element.36), channel_id=1, source_target_pairs={{0,3},{1,2},{2,1},{3,0},{4,7},{5,6},{6,5},{7,4},{8,11},{9,10},{10,... | collective-permute-start | bytes 258056 | tf_op jit(solution)/shard_map/ppermute | solution.py:22
  49.8 4.5 %collective-permute-start.13 = (s16[144,128]{1,0:T(8,128)(2,1)S(1)}, s16[144,128]{1,0:T(8,128)(2,1)S(1)}, u32[]{:S(2)}, u32[]{:S(2)}) collective-permute-start(s16[144,128]{1,0:T(8,128)(2,1)S(1)} %get-tuple-element.39), channel_id=1, source_target_pairs={{0,4},{1,5},{2,6},{3,7},{4,0},{5,1},{6,2},{7,3},{8,12},{9,13},{10,... | collective-permute-start | bytes 110600 | tf_op jit(solution)/shard_map/ppermute | solution.py:22
  51.3 5.3 %collective-permute-start.14 = (s16[144,128]{1,0:T(8,128)(2,1)S(1)}, s16[144,128]{1,0:T(8,128)(2,1)S(1)}, u32[]{:S(2)}, u32[]{:S(2)}) collective-permute-start(s16[144,128]{1,0:T(8,128)(2,1)S(1)} %get-tuple-element.40), channel_id=1, source_target_pairs={{0,8},{1,9},{2,10},{3,11},{4,12},{5,13},{6,14},{7,15},{8,0},{9,1},... | collective-permute-start | bytes 110600 | tf_op jit(solution)/shard_map/ppermute | solution.py:22
  52.2 5.8 %collective-permute-start.15 = (s16[144,128]{1,0:T(8,128)(2,1)S(1)}, s16[144,128]{1,0:T(8,128)(2,1)S(1)}, u32[]{:S(2)}, u32[]{:S(2)}) collective-permute-start(s16[144,128]{1,0:T(8,128)(2,1)S(1)} %get-tuple-element.41), channel_id=1, source_target_pairs={{0,12},{1,13},{2,14},{3,15},{4,8},{5,9},{6,10},{7,11},{8,4},{9,5},... | collective-permute-start | bytes 110600 | tf_op jit(solution)/shard_map/ppermute | solution.py:22
  58.5 4.8 %collective-permute-start.17 = (s16[272,128]{1,0:T(8,128)(2,1)S(1)}, s16[272,128]{1,0:T(8,128)(2,1)S(1)}, u32[]{:S(2)}, u32[]{:S(2)}) collective-permute-start(s16[272,128]{1,0:T(8,128)(2,1)S(1)} %get-tuple-element.43.rest_0_), channel_id=1, source_target_pairs={{0,1},{1,0},{2,3},{3,2},{4,5},{5,4},{6,7},{7,6},{8,9},{9,8},{10,11... | collective-permute-start | bytes 208904 | tf_op jit(solution)/shard_map/ppermute | solution.py:22
  59.1 4.3 %collective-permute-start.18 = (s16[272,128]{1,0:T(8,128)(2,1)S(1)}, s16[272,128]{1,0:T(8,128)(2,1)S(1)}, u32[]{:S(2)}, u32[]{:S(2)}) collective-permute-start(s16[272,128]{1,0:T(8,128)(2,1)S(1)} %get-tuple-element.43.rest_0_), channel_id=1, source_target_pairs={{0,2},{1,3},{2,0},{3,1},{4,6},{5,7},{6,4},{7,5},{8,10},{9,11},{10,... | collective-permute-start | bytes 208904 | tf_op jit(solution)/shard_map/ppermute | solution.py:22
  60.4 5.2 %collective-permute-start.19 = (s16[272,128]{1,0:T(8,128)(2,1)S(1)}, s16[272,128]{1,0:T(8,128)(2,1)S(1)}, u32[]{:S(2)}, u32[]{:S(2)}) collective-permute-start(s16[272,128]{1,0:T(8,128)(2,1)S(1)} %get-tuple-element.43.rest_0_), channel_id=1, source_target_pairs={{0,3},{1,2},{2,1},{3,0},{4,7},{5,6},{6,5},{7,4},{8,11},{9,10},{10,... | collective-permute-start | bytes 208904 | tf_op jit(solution)/shard_map/ppermute | solution.py:22
  62.1 1.2 %collective-permute-start.16 = (f32[64,128]{1,0:T(8,128)S(1)}, f32[64,128]{1,0:T(8,128)S(1)}, u32[]{:S(2)}, u32[]{:S(2)}) collective-permute-start(f32[64,128]{1,0:T(8,128)S(1)} %get-tuple-element.42), channel_id=1, source_target_pairs={{0,16},{16,0},{1,17},{17,1},{2,18},{18,2},{3,19},{19,3},{4,20},{20... | collective-permute-start | bytes 98312 | tf_op jit(solution)/shard_map/ppermute | solution.py:22
  63.3 3.7 %copy-start.3 = (f32[2,64,128]{2,1,0:T(8,128)}, f32[2,64,128]{2,1,0:T(8,128)S(1)}, u32[]{:S(2)}) copy-start(f32[2,64,128]{2,1,0:T(8,128)S(1)} %bitcast_dynamic-update-slice_fusion) | copy-start | bytes 196612

commit v4 on v3

--- a/solution.py
+++ b/solution.py
@@ -216,84 +216,96 @@
         total_ref[k * rank : (k + 1) * rank, :] = acc
     size = total_ref.shape[0] // low
     sub = shares[0].shape[0] // low // high
+    core_at = high * sub
+    core_codes = []
+    for b in range(low):
+        block = total_ref[b * size : (b + 1) * size, :]
+        core_codes.append(scale_code(block))
+        coded = encode(block, core_codes[-1])
+        for out in outs[1:]:
+            out[core_at + b * size : core_at + (b + 1) * size, :] = coded
     for q in range(low):
-        blocks = []
+        codes = []
         for d in range(high):
             at = slice((q * high + d) * sub, (q * high + d + 1) * sub)
             part = shares[0][at, :]
             for h in range(1, rel):
                 part = part + shares[h][at, :]
-            blocks.append(part)
-        src = pl.multiple_of(jnp.bitwise_xor(near, q) * size, size)
-        blocks.append(total_ref[pl.ds(src, size), :])
-        codes, at = [], 0
-        for block in blocks:
-            span = slice(at, at + block.shape[0])
+            span = slice(d * sub, (d + 1) * sub)
             if q == 0:
-                outs[q][span, :] = block
+                outs[q][span, :] = part
             else:
-                codes.append(scale_code(block))
-                outs[q][span, :] = encode(block, codes[-1])
-            at += block.shape[0]
+                codes.append(scale_code(part))
+                outs[q][span, :] = encode(part, codes[-1])
         if q > 0:
-            outs[q][at:, :] = stack_codes(list(enumerate(codes)))
+            outs[q][core_at + low * size :, :] = stack_codes(list(enumerate(codes + core_codes)))
 
 
 def near_kernel(low, high, scale, *rest):
-    parts, (owned_ref, core_ref, *outs) = rest[:low], rest[low:]
-    sub = owned_ref.shape[0]
-    size = parts[0].shape[0] - high * sub
-    scales = [part[high * sub + size :, :].astype(jnp.int32) for part in parts[1:]]
+    (own_ref, *parts), (owned_ref, *outs) = rest[: low + 1], rest[low + 1 :]
+    sub, core_at = owned_ref.shape[0], own_ref.shape[0]
+    size = (parts[0].shape[0] - core_at - scale_rows(high + low)) // low
+    scales = [part[core_at + low * size :, :].astype(jnp.int32) for part in parts]
     sums = []
-    for b in range(high + 1):
-        span = slice(b * sub, (b + 1) * sub) if b < high else slice(b * sub, b * sub + size)
-        total = parts[0][span, :]
-        for part, code in zip(parts[1:], scales):
-            total = total + decode(part[span, :], code[b : b + 1, :])
+    for d in range(high):
+        span = slice(d * sub, (d + 1) * sub)
+        total = own_ref[span, :]
+        for part, code in zip(parts[1:], scales[1:]):
+            total = total + decode(part[span, :], code[d : d + 1, :])
         sums.append(total)
-    core = sums[high] * scale
-    core_code = scale_code(core)
-    core_codes = encode(core, core_code)
     owned_ref[...] = sums[0]
-    core_ref[:size, :] = core_codes
-    core_ref[size:, :] = stack_codes([(1, core_code)])
+    core_codes = []
+    for b in range(low):
+        span = slice(core_at + b * size, core_at + (b + 1) * size)
+        terms = [
+            decode(part[span, :], code[high + b : high + b + 1, :])
+            for part, code in zip(parts, scales)
+        ]
+        while len(terms) > 1:
+            terms = [terms[i] + terms[i + 1] for i in range(0, len(terms), 2)]
+        core = terms[0] * scale
+        core_codes.append(scale_code(core))
+        coded = encode(core, core_codes[-1])
+        for out in outs:
+            out[b * size : (b + 1) * size, :] = coded
     for d in range(1, high):
         code = scale_code(sums[d])
         out = outs[d - 1]
-        out[:size, :] = core_codes
-        out[size : size + sub, :] = encode(sums[d], code)
-        out[size + sub :, :] = stack_codes([(0, code), (1, core_code)])
-
-
-def far_kernel(low, high, root, me_ref, mine_ref, core_ref, *rest):
-    parts, (owned_ref, column_ref) = rest[:-2], rest[-2:]
+        out[low * size : low * size + sub, :] = encode(sums[d], code)
+        out[low * size + sub :, :] = stack_codes(list(enumerate(core_codes + [code])))
+
+
+def far_kernel(low, root, mine_ref, *rest):
+    parts, owned_ref = rest[:-1], rest[-1]
     sub = owned_ref.shape[0]
-    size = parts[0].shape[0] - sub - scale_rows(2)
+    tile = scale_rows(low + 1)
+    total = mine_ref[...]
+    for part in parts:
+        end = part.shape[0] - tile
+        code = part[end:, :].astype(jnp.int32)
+        total = total + decode(part[end - sub : end, :], code[low : low + 1, :])
+    owned_ref[...] = total / jnp.sqrt(F32(root))
+
+
+def place_kernel(low, high, size, me_ref, *rest):
+    parts, (out_ref, block_ref, sems) = rest[:-3], rest[-3:]
     far = me_ref[0] // low
-    total, codes = mine_ref[...], []
+    copies = []
     for d in range(high):
-        ref = core_ref if d == 0 else parts[d - 1]
-        code = ref[ref.shape[0] - scale_rows(2) :, :].astype(jnp.int32)
-        place = jnp.bitwise_xor(far, d)
-        at = pl.multiple_of(place * size, size)
-        column_ref[pl.ds(at, size), :] = ref[:size, :]
-        codes.append((place, code[1:2, :]))
-        if d > 0:
-            total = total + decode(ref[size : size + sub, :], code[0:1, :])
-    owned_ref[...] = total / jnp.sqrt(F32(root))
-    column_ref[high * size :, :] = stack_codes(codes)
-
-
-def place_kernel(low, high, me_ref, *rest):
-    columns, out_ref = rest[:-1], rest[-1]
-    size = out_ref.shape[0] // low // high
-    near = jnp.bitwise_and(me_ref[0], low - 1)
-    for q in range(low):
-        codes = columns[q][high * size :, :].astype(jnp.int32)
-        for d in range(high):
-            block = decode(columns[q][d * size : (d + 1) * size, :], codes[d : d + 1, :])
-            at = pl.multiple_of((d * low + jnp.bitwise_xor(near, q)) * size, size)
-            out_ref[pl.ds(at, size), :] = block
+        tile = parts[d].shape[0] - scale_rows(low + 1)
+        code = parts[d][tile:, :].astype(jnp.int32)
+        for b in range(low):
+            span = slice(b * size, (b + 1) * size)
+            block_ref[d, span, :] = decode(parts[d][span, :], code[b : b + 1, :])
+        at = pl.multiple_of(jnp.bitwise_xor(far, d) * (low * size), low * size)
+        copies.append(
+            pltpu.make_async_copy(
+                block_ref.at[d], out_ref.at[pl.ds(at, low * size), :], sems.at[d]
+            )
+        )
+        copies[-1].start()
+    for copy in copies:
+        copy.wait()
 
 
 def gradients(facts, observed, factors, cores):
@@ -426,31 +438,31 @@
         functools.partial(merge_kernel, low, high, rel),
         in_specs=[pl.BlockSpec(memory_space=pltpu.SMEM)]
         + [pl.BlockSpec(memory_space=pltpu.VMEM)] * (1 + high + rel),
-        out_shape=[shape((high * sub + size, rank), F32)]
-        + [shape((high * sub + size + scale_rows(high + 1), rank), I16)] * (low - 1),
+        out_shape=[shape((high * sub, rank), F32)]
+        + [shape((high * sub + low * size + scale_rows(high + low), rank), I16)] * (low - 1),
         scratch_shapes=[pltpu.VMEM((per * rank, rank), F32)],
         compiler_params=pltpu.CompilerParams(vmem_limit_bytes=8 * MIB),
         name="merge_kernel",
     )(me, column, *pulls, *shares)
-    merged = from_partners(merged[0], low, lambda q: near_swap(merged[q], q))
-
-    mine, core_codes, *parts = pl.pallas_call(
+    mine, sent = merged[:2]
+    merged = from_partners(sent, low, lambda q: near_swap(merged[q], q))
+
+    mine, *parts = pl.pallas_call(
         functools.partial(near_kernel, low, high, rank / n_all),
-        out_shape=[shape((sub, rank), F32), shape((size + scale_rows(2), rank), I16)]
-        + [shape((sub + size + scale_rows(2), rank), I16)] * (high - 1),
+        out_shape=[shape((sub, rank), F32)]
+        + [shape((low * size + sub + scale_rows(low + 1), rank), I16)] * (high - 1),
         compiler_params=pltpu.CompilerParams(vmem_limit_bytes=6 * MIB),
         name="near_kernel",
-    )(*merged)
-    parts = from_partners(None, high, lambda d: far_swap(parts[d - 1], d))[1:]
-
-    owned, core_column = pl.pallas_call(
-        functools.partial(far_kernel, low, high, n_all * relations * rel),
-        in_specs=[pl.BlockSpec(memory_space=pltpu.SMEM)]
-        + [pl.BlockSpec(memory_space=pltpu.VMEM)] * (high + 1),
-        out_shape=[shape((sub, rank), F32), shape((high * size + scale_rows(high), rank), I16)],
+    )(mine, *merged)
+    sent = parts[0]
+    parts = from_partners(sent, high, lambda d: far_swap(parts[d - 1], d))
+
+    owned = pl.pallas_call(
+        functools.partial(far_kernel, low, n_all * relations * rel),
+        out_shape=shape((sub, rank), F32),
         compiler_params=pltpu.CompilerParams(vmem_limit_bytes=4 * MIB),
         name="far_kernel",
-    )(me, mine, core_codes, *parts)
+    )(mine, *parts[1:])
 
     grad_factors = jnp.zeros((rel, sub, rank), F32)
     for h in range(rel):
@@ -458,15 +470,19 @@
         grad_factors = lax.dynamic_update_index_in_dim(grad_factors, piece, here ^ h, 0)
     grad_factors = grad_factors.reshape(rows, rank)
 
-    columns = from_partners(core_column, low, lambda q: near_swap(core_column, q))
     grad_cores = pl.pallas_call(
-        functools.partial(place_kernel, low, high),
+        functools.partial(place_kernel, low, high, size),
         in_specs=[pl.BlockSpec(memory_space=pltpu.SMEM)]
-        + [pl.BlockSpec(memory_space=pltpu.VMEM)] * low,
+        + [pl.BlockSpec(memory_space=pltpu.VMEM)] * high,
+        out_specs=pl.BlockSpec(memory_space=pl.ANY),
         out_shape=shape((relations * rank, rank), F32),
+        scratch_shapes=[
+            pltpu.VMEM((high, low * size, rank), F32),
+            pltpu.SemaphoreType.DMA((high,)),
+        ],
         compiler_params=pltpu.CompilerParams(vmem_limit_bytes=4 * MIB),
         name="place_kernel",
-    )(me, *columns)
+    )(me, *parts)
     return grad_factors, grad_cores.reshape(relations, rank, rank)
 
 

time: 67.2 us -> 62.4 us (0.929)
  starting transfers between devices: 25.3 us -> 21.8 us
  waiting for transfers between devices: 19.9 us -> 18.4 us
    ppermute x20 -> x17, starting transfers between devices: 25.3 us -> 21.8 us  [swap(): return lax.ppermute(x, axis, [(i, i ^ distance) for i in range(size)])]
    ppermute x20 -> x17, waiting for transfers between devices: 19.9 us -> 18.4 us  [swap(): return lax.ppermute(x, axis, [(i, i ^ distance) for i in range(size)])]
  transfers between devices with their start and end apart: 20 -> 17, of which waited for: 13 -> 10; matrix products, arithmetic and copies ran while one was open for 4% -> 4% of each run, Pallas kernels for 3% -> 6%
where the time goes in v4:
time: 62.4 us; the launch traced here: 62.2 us
  starting transfers between devices  21.8 us (35%)
  waiting for transfers between devices  18.4 us (29%)
  Pallas kernels  15.9 us (25%)
  local copies, waits for them, and re-layouts  5.15 us (8%)
  between operations  0.85 us (1%)
    ppermute x17, starting transfers between devices, swap(): return lax.ppermute(x, axis, [(i, i ^ distance) for i in range(size)])  21.8 us
    ppermute x17, waiting for transfers between devices, swap(): return lax.ppermute(x, axis, [(i, i ^ distance) for i in range(size)])  18.4 us
    pallas_call x1, Pallas kernels, gradients(): rows_call(me, err, left, cores.reshape(relations * rank, rank), column, *...  5.78 us
    pallas_call x1, Pallas kernels, gradients(): pl.pallas_call(functools.partial(late_kernel, low, high, first), grid_spe...  5.21 us
    unnamed x13, local copies, waits for them, and re-layouts  3.55 us
    pallas_call x1, Pallas kernels, gradients(): pl.pallas_call(functools.partial(early_kernel, low, high), grid_spec=pltp...  2.29 us
    slice x1, local copies, waits for them, and re-layouts, gradients(): packed = observed[:, :half] | jnp.left_shift(observed[:, half:], 16)  1.53 us
    pallas_call x1, Pallas kernels, gradients(): pl.pallas_call(functools.partial(place_kernel, low, high, size), in_specs...  1.38 us
  transfers between devices with their start and end apart: 17, of which 10 were waited for; matrix products, arithmetic and copies ran while one was open for 4% of the time, Pallas kernels for 6%

profile of v4, /device:TPU:0, one launch (start us, length us, event | category | flops | bytes accessed | tf_op | source)
XLA Modules:
  0.0 62.2 jit_solution(2354731792809341661)
XLA Ops:
  0.7 3.1 %collective-permute-start = (bf16[128,128]{1,0:T(8,128)(2,1)}, bf16[128,128]{1,0:T(8,128)(2,1)S(1)}, u32[]{:S(2)}, u32[]{:S(2)}) collective-permute-start(bf16[128,128]{1,0:T(8,128)(2,1)} %own_ref.1), channel_id=1, source_target_pairs={{0,4},{1,5},{2,6},{3,7},{4,0},{5,1},{6,2},{7,3},{8,12},{9,13},{10,... | collective-permute-start | bytes 98312 | tf_op jit(solution)/shard_map/ppermute | solution.py:22
  3.8 2.6 %collective-permute-start.1 = (bf16[128,128]{1,0:T(8,128)(2,1)}, bf16[128,128]{1,0:T(8,128)(2,1)S(1)}, u32[]{:S(2)}, u32[]{:S(2)}) collective-permute-start(bf16[128,128]{1,0:T(8,128)(2,1)} %own_ref.1), channel_id=1, source_target_pairs={{0,8},{1,9},{2,10},{3,11},{4,12},{5,13},{6,14},{7,15},{8,0},{9,1},... | collective-permute-start | bytes 98312 | tf_op jit(solution)/shard_map/ppermute | solution.py:22
  6.4 0.0 collective-permute-start.2
  6.4 1.5 %fusion = (s32[8,64,158]{1,0,2:T(8,128)S(1)}, s32[8,64,158]{1,0,2:T(8,128)S(1)}) fusion(s32[8,128,158]{1,0,2:T(8,128)} %param.5), kind=kLoop, calls=%fused_computation.8 | loop fusion | bytes 1294336 | tf_op jit(solution)/shard_map/slice | solution.py:331
  7.9 0.4 copy.10
  8.2 0.3 copy.9
  8.6 0.1 shift-left_or_fusion
  8.8 0.0 collective-permute-done
  8.8 0.6 collective-permute-done.1
  9.4 2.9 %collective-permute-done.2 = bf16[128,128]{1,0:T(8,128)(2,1)S(1)} collective-permute-done((bf16[128,128]{1,0:T(8,128)(2,1)}, bf16[128,128]{1,0:T(8,128)(2,1)S(1)}, u32[]{:S(2)}, u32[]{:S(2)}) %collective-permute-start.2) | collective-permute-done | bytes 32800 | tf_op jit(solution)/shard_map/ppermute | solution.py:22
  12.3 1.5 %collective-permute-start.3 = (bf16[512,128]{1,0:T(8,128)(2,1)S(1)}, bf16[512,128]{1,0:T(8,128)(2,1)S(1)}, u32[]{:S(2)}, u32[]{:S(2)}) collective-permute-start(bf16[512,128]{1,0:T(8,128)(2,1)S(1)} %constant_dynamic-update-slice_fusion.column_ref.rest_0_), channel_id=1, source_target_pairs={{0,1},{1,0},{2,3},{3,2},{4,5},{5,4},{6,7},{7,6},{8,9},{9,8},{10,11... | collective-permute-start | bytes 393224 | tf_op jit(solution)/shard_map/ppermute | solution.py:22
  13.8 1.5 %collective-permute-start.4 = (bf16[512,128]{1,0:T(8,128)(2,1)S(1)}, bf16[512,128]{1,0:T(8,128)(2,1)S(1)}, u32[]{:S(2)}, u32[]{:S(2)}) collective-permute-start(bf16[512,128]{1,0:T(8,128)(2,1)S(1)} %constant_dynamic-update-slice_fusion.column_ref.rest_0_), channel_id=1, source_target_pairs={{0,2},{1,3},{2,0},{3,1},{4,6},{5,7},{6,4},{7,5},{8,10},{9,11},{10,... | collective-permute-start | bytes 393224 | tf_op jit(solution)/shard_map/ppermute | solution.py:22
  15.3 0.5 collective-permute-start.5
  15.8 0.1 pad_add_fusion.me_ref
  15.9 2.2 %copy-done = bf16[8,128,2048]{2,1,0:T(8,128)(2,1)S(1)} copy-done((bf16[8,128,2048]{2,1,0:T(8,128)(2,1)S(1)}, bf16[8,128,2048]{2,1,0:T(8,128)(2,1)}, u32[]{:S(2)}) %copy-start) | copy-done | bytes 4194328
  18.0 2.3 %early_kernel.1 = (bf16[8,1024,256]{2,1,0:T(8,128)(2,1)S(1)}, bf16[1024,128]{1,0:T(8,128)(2,1)S(1)}, f32[1024,128]{1,0:T(8,128)S(1)}) custom-call(s32[2]{0:T(128)S(1)} %pad_add_fusion.me_ref, s32[8,64,256]{2,1,0:T(8,128)S(1)} %pad.4.words_ref, bf16[8,128,2048]{2,1,0:T(8,128)(2,1)S(1)} %copy-done, bf16[8,128,2048]{2,1,0:T(8,128)(2,1)S(1)} %copy-done, ...), custom_call_target="tpu_custom_call" | custom-call | flops 268435456 | bytes 2097152 | tf_op jit(solution)/shard_map/early_kernel/pallas_call | solution.py:352
  20.3 0.0 collective-permute-done.3.rest_0_.rest_1_
  20.4 0.0 collective-permute-done.4.rest_1_.rest_2_
  20.4 0.8 %collective-permute-done.5.rest_2_.rest_3_ = bf16[512,128]{1,0:T(8,128)(2,1)S(1)} collective-permute-done((bf16[512,128]{1,0:T(8,128)(2,1)S(1)}, bf16[512,128]{1,0:T(8,128)(2,1)S(1)}, u32[]{:S(2)}, u32[]{:S(2)}) %collective-permute-start.5) | collective-permute-done | bytes 131104 | tf_op jit(solution)/shard_map/ppermute | solution.py:22
  21.2 5.2 %late_kernel.1 = (bf16[8,1024,256]{2,1,0:T(8,128)(2,1)S(1)}, bf16[256,128]{1,0:T(8,128)(2,1)S(1)}, bf16[256,128]{1,0:T(8,128)(2,1)S(1)}, bf16[256,128]{1,0:T(8,128)(2,1)S(1)}, bf16[256,128]{1,0:T(8,128)(2,1)S(1)}) custom-call(s32[2]{0:T(128)S(1)} %pad_add_fusion.me_ref, s32[8,64,256]{2,1,0:T(8,128)S(1)} %pad.4.words_ref, ...), custom_call_target="tpu_custom_call", output_to_operand_aliasing={{0}: (6, {})} | custom-call | flops 805306368 | bytes 6291456 | tf_op jit(solution)/shard_map/late_kernel/pallas_call | solution.py:381
  26.4 5.8 %rows_kernel.1 = (f32[1024,128]{1,0:T(8,128)S(1)}, f32[1024,128]{1,0:T(8,128)S(1)}) custom-call(s32[2]{0:T(128)S(1)} %pad_add_fusion.me_ref, bf16[8,1024,256]{2,1,0:T(8,128)(2,1)S(1)} %get-tuple-element.27.err_ref, bf16[1024,128]{1,0:T(8,128)(2,1)S(1)} %get-tuple-element.20.left_ref, bf16[1024,128]{1,0:T(8,128)(2,1)S(1)} %bitcast.9, ...), custom_call_target="tpu_custom_call" | custom-call | flops 1610612736 | bytes 12582912 | tf_op jit(solution)/shard_map/rows_kernel/pallas_call | solution.py:433
  32.2 0.1 collective-permute-start.9
  32.3 0.1 collective-permute-start.6
  32.3 1.3 %collective-permute-start.7 = (bf16[256,128]{1,0:T(8,128)(2,1)S(1)}, bf16[256,128]{1,0:T(8,128)(2,1)S(1)}, u32[]{:S(2)}, u32[]{:S(2)}) collective-permute-start(bf16[256,128]{1,0:T(8,128)(2,1)S(1)} %get-tuple-element.25), channel_id=1, source_target_pairs={{0,8},{1,9},{2,10},{3,11},{4,12},{5,13},{6,14},{7,15},{8,0},{9,1},... | collective-permute-start | bytes 196616 | tf_op jit(solution)/shard_map/ppermute | solution.py:22
  33.7 3.0 %collective-permute-start.8 = (bf16[256,128]{1,0:T(8,128)(2,1)S(1)}, bf16[256,128]{1,0:T(8,128)(2,1)S(1)}, u32[]{:S(2)}, u32[]{:S(2)}) collective-permute-start(bf16[256,128]{1,0:T(8,128)(2,1)S(1)} %get-tuple-element.26), channel_id=1, source_target_pairs={{0,12},{1,13},{2,14},{3,15},{4,8},{5,9},{6,10},{7,11},{8,4},{9,5},... | collective-permute-start | bytes 196616 | tf_op jit(solution)/shard_map/ppermute | solution.py:22
  36.7 1.1 %collective-permute-done.6.rest_1_ = bf16[256,128]{1,0:T(8,128)(2,1)S(1)} collective-permute-done((bf16[256,128]{1,0:T(8,128)(2,1)S(1)}, bf16[256,128]{1,0:T(8,128)(2,1)S(1)}, u32[]{:S(2)}, u32[]{:S(2)}) %collective-permute-start.6) | collective-permute-done | bytes 65568 | tf_op jit(solution)/shard_map/ppermute | solution.py:22
  37.8 3.3 %collective-permute-done.7.rest_2_ = bf16[256,128]{1,0:T(8,128)(2,1)S(1)} collective-permute-done((bf16[256,128]{1,0:T(8,128)(2,1)S(1)}, bf16[256,128]{1,0:T(8,128)(2,1)S(1)}, u32[]{:S(2)}, u32[]{:S(2)}) %collective-permute-start.7) | collective-permute-done | bytes 65568 | tf_op jit(solution)/shard_map/ppermute | solution.py:22
  41.1 0.0 collective-permute-done.8.rest_3_
  41.1 0.0 collective-permute-done.9.rest_5_
  41.1 1.0 %merge_kernel.1 = (f32[256,128]{1,0:T(8,128)S(1)}, s16[528,128]{1,0:T(8,128)(2,1)S(1)}, s16[528,128]{1,0:T(8,128)(2,1)S(1)}, s16[528,128]{1,0:T(8,128)(2,1)S(1)}) custom-call(s32[2]{0:T(128)S(1)} %pad_add_fusion.me_ref, bf16[512,128]{1,0:T(8,128)(2,1)S(1)} %constant_dynamic-update-slice_fusion.column_ref.rest_0_, ...), custom_call_target="tpu_custom_call" | custom-call | tf_op jit(solution)/shard_map/merge_kernel/pallas_call | solution.py:437
  42.1 0.8 %collective-permute-start.10 = (s16[528,128]{1,0:T(8,128)(2,1)S(1)}, s16[528,128]{1,0:T(8,128)(2,1)S(1)}, u32[]{:S(2)}, u32[]{:S(2)}) collective-permute-start(s16[528,128]{1,0:T(8,128)(2,1)S(1)} %get-tuple-element.31.rest_1_), channel_id=1, source_target_pairs={{0,1},{1,0},{2,3},{3,2},{4,5},{5,4},{6,7},{7,6},{8,9},{9,8},{10,11... | collective-permute-start | bytes 405512 | tf_op jit(solution)/shard_map/ppermute | solution.py:22
  42.9 1.5 %collective-permute-start.11 = (s16[528,128]{1,0:T(8,128)(2,1)S(1)}, s16[528,128]{1,0:T(8,128)(2,1)S(1)}, u32[]{:S(2)}, u32[]{:S(2)}) collective-permute-start(s16[528,128]{1,0:T(8,128)(2,1)S(1)} %get-tuple-element.32), channel_id=1, source_target_pairs={{0,2},{1,3},{2,0},{3,1},{4,6},{5,7},{6,4},{7,5},{8,10},{9,11},{10,... | collective-permute-start | bytes 405512 | tf_op jit(solution)/shard_map/ppermute | solution.py:22
  44.4 1.2 %collective-permute-start.12 = (s16[528,128]{1,0:T(8,128)(2,1)S(1)}, s16[528,128]{1,0:T(8,128)(2,1)S(1)}, u32[]{:S(2)}, u32[]{:S(2)}) collective-permute-start(s16[528,128]{1,0:T(8,128)(2,1)S(1)} %get-tuple-element.33), channel_id=1, source_target_pairs={{0,3},{1,2},{2,1},{3,0},{4,7},{5,6},{6,5},{7,4},{8,11},{9,10},{10,... | collective-permute-start | bytes 405512 | tf_op jit(solution)/shard_map/ppermute | solution.py:22
  45.6 1.9 %collective-permute-done.10.rest_2_ = s16[528,128]{1,0:T(8,128)(2,1)S(1)} collective-permute-done((s16[528,128]{1,0:T(8,128)(2,1)S(1)}, s16[528,128]{1,0:T(8,128)(2,1)S(1)}, u32[]{:S(2)}, u32[]{:S(2)}) %collective-permute-start.10) | collective-permute-done | bytes 135200 | tf_op jit(solution)/shard_map/ppermute | solution.py:22
  47.5 1.2 %collective-permute-done.11.rest_3_ = s16[528,128]{1,0:T(8,128)(2,1)S(1)} collective-permute-done((s16[528,128]{1,0:T(8,128)(2,1)S(1)}, s16[528,128]{1,0:T(8,128)(2,1)S(1)}, u32[]{:S(2)}, u32[]{:S(2)}) %collective-permute-start.11) | collective-permute-done | bytes 135200 | tf_op jit(solution)/shard_map/ppermute | solution.py:22
  48.7 1.6 %collective-permute-done.12.rest_4_ = s16[528,128]{1,0:T(8,128)(2,1)S(1)} collective-permute-done((s16[528,128]{1,0:T(8,128)(2,1)S(1)}, s16[528,128]{1,0:T(8,128)(2,1)S(1)}, u32[]{:S(2)}, u32[]{:S(2)}) %collective-permute-start.12) | collective-permute-done | bytes 135200 | tf_op jit(solution)/shard_map/ppermute | solution.py:22
  50.3 0.2 near_kernel.1
  50.5 1.9 %collective-permute-start.13 = (s16[336,128]{1,0:T(8,128)(2,1)S(1)}, s16[336,128]{1,0:T(8,128)(2,1)S(1)}, u32[]{:S(2)}, u32[]{:S(2)}) collective-permute-start(s16[336,128]{1,0:T(8,128)(2,1)S(1)} %get-tuple-element.35.rest_0_), channel_id=1, source_target_pairs={{0,4},{1,5},{2,6},{3,7},{4,0},{5,1},{6,2},{7,3},{8,12},{9,13},{10,... | collective-permute-start | bytes 258056 | tf_op jit(solution)/shard_map/ppermute | solution.py:22
  52.4 0.8 %collective-permute-start.14 = (s16[336,128]{1,0:T(8,128)(2,1)S(1)}, s16[336,128]{1,0:T(8,128)(2,1)S(1)}, u32[]{:S(2)}, u32[]{:S(2)}) collective-permute-start(s16[336,128]{1,0:T(8,128)(2,1)S(1)} %get-tuple-element.36), channel_id=1, source_target_pairs={{0,8},{1,9},{2,10},{3,11},{4,12},{5,13},{6,14},{7,15},{8,0},{9,1},... | collective-permute-start | bytes 258056 | tf_op jit(solution)/shard_map/ppermute | solution.py:22
  53.2 1.8 %collective-permute-start.15 = (s16[336,128]{1,0:T(8,128)(2,1)S(1)}, s16[336,128]{1,0:T(8,128)(2,1)S(1)}, u32[]{:S(2)}, u32[]{:S(2)}) collective-permute-start(s16[336,128]{1,0:T(8,128)(2,1)S(1)} %get-tuple-element.37), channel_id=1, source_target_pairs={{0,12},{1,13},{2,14},{3,15},{4,8},{5,9},{6,10},{7,11},{8,4},{9,5},... | collective-permute-start | bytes 258056 | tf_op jit(solution)/shard_map/ppermute | solution.py:22
  55.0 0.1 collective-permute-done.13.rest_0_.rest_1_
  55.1 5.0 %collective-permute-done.14.rest_1_.rest_2_ = s16[336,128]{1,0:T(8,128)(2,1)S(1)} collective-permute-done((s16[336,128]{1,0:T(8,128)(2,1)S(1)}, s16[336,128]{1,0:T(8,128)(2,1)S(1)}, u32[]{:S(2)}, u32[]{:S(2)}) %collective-permute-start.14) | collective-permute-done | bytes 86048 | tf_op jit(solution)/shard_map/ppermute | solution.py:22
  60.1 0.0 collective-permute-done.15.rest_2_.rest_3_
  60.1 0.1 collective-permute-start.16
  60.2 1.4 %place_kernel.1 = f32[1024,128]{1,0:T(8,128)} custom-call(s32[2]{0:T(128)S(1)} %pad_add_fusion.me_ref, s16[336,128]{1,0:T(8,128)(2,1)S(1)} %get-tuple-element.35.rest_0_, s16[336,128]{1,0:T(8,128)(2,1)S(1)} %collective-permute-done.13.rest_0_.rest_1_, s16[336,128]{1,0:T(8,128)(2,1)S(1)} %collective-permute-done.14.rest_1_.rest_2_, ...), custom_call_target="tpu_custom_call" | custom-call | tf_op jit(solution)/shard_map/place_kernel/pallas_call | solution.py:473
  61.6 0.0 collective-permute-done.16
  61.6 0.0 copy-start.3
  61.6 0.6 copy-done.3
  (14 shorter events, 0.1 us)
Async XLA Ops:
  0.6 8.1 %copy-start.2 = (bf16[128,128]{1,0:T(8,128)(2,1)S(1)}, bf16[128,128]{1,0:T(8,128)(2,1)}, u32[]{:S(2)}) copy-start(bf16[128,128]{1,0:T(8,128)(2,1)} %own_ref.1) | copy-start | bytes 98308
  0.6 15.2 %copy-start.1 = (bf16[8,128,128]{2,1,0:T(8,128)(2,1)S(1)}, bf16[8,128,128]{2,1,0:T(8,128)(2,1)}, u32[]{:S(2)}) copy-start(bf16[8,128,128]{2,1,0:T(8,128)(2,1)} %cores_ref.1) | copy-start | bytes 786436
  0.7 8.1 %collective-permute-start = (bf16[128,128]{1,0:T(8,128)(2,1)}, bf16[128,128]{1,0:T(8,128)(2,1)S(1)}, u32[]{:S(2)}, u32[]{:S(2)}) collective-permute-start(bf16[128,128]{1,0:T(8,128)(2,1)} %own_ref.1), channel_id=1, source_target_pairs={{0,4},{1,5},{2,6},{3,7},{4,0},{5,1},{6,2},{7,3},{8,12},{9,13},{10,... | collective-permute-start | bytes 98312 | tf_op jit(solution)/shard_map/ppermute | solution.py:22
  3.8 5.6 %collective-permute-start.1 = (bf16[128,128]{1,0:T(8,128)(2,1)}, bf16[128,128]{1,0:T(8,128)(2,1)S(1)}, u32[]{:S(2)}, u32[]{:S(2)}) collective-permute-start(bf16[128,128]{1,0:T(8,128)(2,1)} %own_ref.1), channel_id=1, source_target_pairs={{0,8},{1,9},{2,10},{3,11},{4,12},{5,13},{6,14},{7,15},{8,0},{9,1},... | collective-permute-start | bytes 98312 | tf_op jit(solution)/shard_map/ppermute | solution.py:22
  6.4 5.9 %collective-permute-start.2 = (bf16[128,128]{1,0:T(8,128)(2,1)}, bf16[128,128]{1,0:T(8,128)(2,1)S(1)}, u32[]{:S(2)}, u32[]{:S(2)}) collective-permute-start(bf16[128,128]{1,0:T(8,128)(2,1)} %own_ref.1), channel_id=1, source_target_pairs={{0,12},{1,13},{2,14},{3,15},{4,8},{5,9},{6,10},{7,11},{8,4},{9,5},... | collective-permute-start | bytes 98312 | tf_op jit(solution)/shard_map/ppermute | solution.py:22
  12.3 8.1 %collective-permute-start.3 = (bf16[512,128]{1,0:T(8,128)(2,1)S(1)}, bf16[512,128]{1,0:T(8,128)(2,1)S(1)}, u32[]{:S(2)}, u32[]{:S(2)}) collective-permute-start(bf16[512,128]{1,0:T(8,128)(2,1)S(1)} %constant_dynamic-update-slice_fusion.column_ref.rest_0_), channel_id=1, source_target_pairs={{0,1},{1,0},{2,3},{3,2},{4,5},{5,4},{6,7},{7,6},{8,9},{9,8},{10,11... | collective-permute-start | bytes 393224 | tf_op jit(solution)/shard_map/ppermute | solution.py:22
  13.8 6.6 %collective-permute-start.4 = (bf16[512,128]{1,0:T(8,128)(2,1)S(1)}, bf16[512,128]{1,0:T(8,128)(2,1)S(1)}, u32[]{:S(2)}, u32[]{:S(2)}) collective-permute-start(bf16[512,128]{1,0:T(8,128)(2,1)S(1)} %constant_dynamic-update-slice_fusion.column_ref.rest_0_), channel_id=1, source_target_pairs={{0,2},{1,3},{2,0},{3,1},{4,6},{5,7},{6,4},{7,5},{8,10},{9,11},{10,... | collective-permute-start | bytes 393224 | tf_op jit(solution)/shard_map/ppermute | solution.py:22
  15.3 5.9 %collective-permute-start.5 = (bf16[512,128]{1,0:T(8,128)(2,1)S(1)}, bf16[512,128]{1,0:T(8,128)(2,1)S(1)}, u32[]{:S(2)}, u32[]{:S(2)}) collective-permute-start(bf16[512,128]{1,0:T(8,128)(2,1)S(1)} %constant_dynamic-update-slice_fusion.column_ref.rest_0_), channel_id=1, source_target_pairs={{0,3},{1,2},{2,1},{3,0},{4,7},{5,6},{6,5},{7,4},{8,11},{9,10},{10,... | collective-permute-start | bytes 393224 | tf_op jit(solution)/shard_map/ppermute | solution.py:22
  15.9 2.2 %copy-start = (bf16[8,128,2048]{2,1,0:T(8,128)(2,1)S(1)}, bf16[8,128,2048]{2,1,0:T(8,128)(2,1)}, u32[]{:S(2)}) copy-start(bf16[8,128,2048]{2,1,0:T(8,128)(2,1)} %facts1_ref.3) | copy-start | bytes 12582916
  32.2 8.9 %collective-permute-start.9 = (f32[1024,128]{1,0:T(8,128)S(1)}, f32[1024,128]{1,0:T(8,128)S(1)}, u32[]{:S(2)}, u32[]{:S(2)}) collective-permute-start(f32[1024,128]{1,0:T(8,128)S(1)} %get-tuple-element.29), channel_id=1, source_target_pairs={{0,16},{16,0},{1,17},{17,1},{2,18},{18,2},{3,19},{19,3},{4,20},{20... | collective-permute-start | bytes 1572872 | tf_op jit(solution)/shard_map/ppermute | solution.py:22
  32.3 5.5 %collective-permute-start.6 = (bf16[256,128]{1,0:T(8,128)(2,1)S(1)}, bf16[256,128]{1,0:T(8,128)(2,1)S(1)}, u32[]{:S(2)}, u32[]{:S(2)}) collective-permute-start(bf16[256,128]{1,0:T(8,128)(2,1)S(1)} %get-tuple-element.24), channel_id=1, source_target_pairs={{0,4},{1,5},{2,6},{3,7},{4,0},{5,1},{6,2},{7,3},{8,12},{9,13},{10,... | collective-permute-start | bytes 196616 | tf_op jit(solution)/shard_map/ppermute | solution.py:22
  32.3 8.7 %collective-permute-start.7 = (bf16[256,128]{1,0:T(8,128)(2,1)S(1)}, bf16[256,128]{1,0:T(8,128)(2,1)S(1)}, u32[]{:S(2)}, u32[]{:S(2)}) collective-permute-start(bf16[256,128]{1,0:T(8,128)(2,1)S(1)} %get-tuple-element.25), channel_id=1, source_target_pairs={{0,8},{1,9},{2,10},{3,11},{4,12},{5,13},{6,14},{7,15},{8,0},{9,1},... | collective-permute-start | bytes 196616 | tf_op jit(solution)/shard_map/ppermute | solution.py:22
  33.7 7.4 %collective-permute-start.8 = (bf16[256,128]{1,0:T(8,128)(2,1)S(1)}, bf16[256,128]{1,0:T(8,128)(2,1)S(1)}, u32[]{:S(2)}, u32[]{:S(2)}) collective-permute-start(bf16[256,128]{1,0:T(8,128)(2,1)S(1)} %get-tuple-element.26), channel_id=1, source_target_pairs={{0,12},{1,13},{2,14},{3,15},{4,8},{5,9},{6,10},{7,11},{8,4},{9,5},... | collective-permute-start | bytes 196616 | tf_op jit(solution)/shard_map/ppermute | solution.py:22
  42.1 5.5 %collective-permute-start.10 = (s16[528,128]{1,0:T(8,128)(2,1)S(1)}, s16[528,128]{1,0:T(8,128)(2,1)S(1)}, u32[]{:S(2)}, u32[]{:S(2)}) collective-permute-start(s16[528,128]{1,0:T(8,128)(2,1)S(1)} %get-tuple-element.31.rest_1_), channel_id=1, source_target_pairs={{0,1},{1,0},{2,3},{3,2},{4,5},{5,4},{6,7},{7,6},{8,9},{9,8},{10,11... | collective-permute-start | bytes 405512 | tf_op jit(solution)/shard_map/ppermute | solution.py:22
  42.9 5.9 %collective-permute-start.11 = (s16[528,128]{1,0:T(8,128)(2,1)S(1)}, s16[528,128]{1,0:T(8,128)(2,1)S(1)}, u32[]{:S(2)}, u32[]{:S(2)}) collective-permute-start(s16[528,128]{1,0:T(8,128)(2,1)S(1)} %get-tuple-element.32), channel_id=1, source_target_pairs={{0,2},{1,3},{2,0},{3,1},{4,6},{5,7},{6,4},{7,5},{8,10},{9,11},{10,... | collective-permute-start | bytes 405512 | tf_op jit(solution)/shard_map/ppermute | solution.py:22
  44.4 5.9 %collective-permute-start.12 = (s16[528,128]{1,0:T(8,128)(2,1)S(1)}, s16[528,128]{1,0:T(8,128)(2,1)S(1)}, u32[]{:S(2)}, u32[]{:S(2)}) collective-permute-start(s16[528,128]{1,0:T(8,128)(2,1)S(1)} %get-tuple-element.33), channel_id=1, source_target_pairs={{0,3},{1,2},{2,1},{3,0},{4,7},{5,6},{6,5},{7,4},{8,11},{9,10},{10,... | collective-permute-start | bytes 405512 | tf_op jit(solution)/shard_map/ppermute | solution.py:22
  50.5 4.6 %collective-permute-start.13 = (s16[336,128]{1,0:T(8,128)(2,1)S(1)}, s16[336,128]{1,0:T(8,128)(2,1)S(1)}, u32[]{:S(2)}, u32[]{:S(2)}) collective-permute-start(s16[336,128]{1,0:T(8,128)(2,1)S(1)} %get-tuple-element.35.rest_0_), channel_id=1, source_target_pairs={{0,4},{1,5},{2,6},{3,7},{4,0},{5,1},{6,2},{7,3},{8,12},{9,13},{10,... | collective-permute-start | bytes 258056 | tf_op jit(solution)/shard_map/ppermute | solution.py:22
  52.4 7.6 %collective-permute-start.14 = (s16[336,128]{1,0:T(8,128)(2,1)S(1)}, s16[336,128]{1,0:T(8,128)(2,1)S(1)}, u32[]{:S(2)}, u32[]{:S(2)}) collective-permute-start(s16[336,128]{1,0:T(8,128)(2,1)S(1)} %get-tuple-element.36), channel_id=1, source_target_pairs={{0,8},{1,9},{2,10},{3,11},{4,12},{5,13},{6,14},{7,15},{8,0},{9,1},... | collective-permute-start | bytes 258056 | tf_op jit(solution)/shard_map/ppermute | solution.py:22
  53.2 6.9 %collective-permute-start.15 = (s16[336,128]{1,0:T(8,128)(2,1)S(1)}, s16[336,128]{1,0:T(8,128)(2,1)S(1)}, u32[]{:S(2)}, u32[]{:S(2)}) collective-permute-start(s16[336,128]{1,0:T(8,128)(2,1)S(1)} %get-tuple-element.37), channel_id=1, source_target_pairs={{0,12},{1,13},{2,14},{3,15},{4,8},{5,9},{6,10},{7,11},{8,4},{9,5},... | collective-permute-start | bytes 258056 | tf_op jit(solution)/shard_map/ppermute | solution.py:22
  60.1 1.5 %collective-permute-start.16 = (f32[64,128]{1,0:T(8,128)S(1)}, f32[64,128]{1,0:T(8,128)S(1)}, u32[]{:S(2)}, u32[]{:S(2)}) collective-permute-start(f32[64,128]{1,0:T(8,128)S(1)} %far_kernel.1), channel_id=1, source_target_pairs={{0,16},{16,0},{1,17},{17,1},{2,18},{18,2},{3,19},{19,3},{4,20},{20... | collective-permute-start | bytes 98312 | tf_op jit(solution)/shard_map/ppermute | solution.py:22
  61.6 0.6 %copy-start.3 = (f32[2,64,128]{2,1,0:T(8,128)}, f32[2,64,128]{2,1,0:T(8,128)S(1)}, u32[]{:S(2)}) copy-start(f32[2,64,128]{2,1,0:T(8,128)S(1)} %bitcast_dynamic-update-slice_fusion) | copy-start | bytes 196612

commit v5 on v4

--- a/solution.py
+++ b/solution.py
@@ -16,6 +16,7 @@
 BF16 = jnp.bfloat16
 I16 = jnp.int16
 MIB = 1 << 20
+LARGE = pltpu.CompilerParams(vmem_limit_bytes=24 * MIB)
 
 
 def swap(x, axis, size, distance):
@@ -45,21 +46,11 @@
     return jnp.bitwise_xor(me, (slot % high) * low + slot // high)
 
 
-def take_pair(pieces, pair, scratch, size):
-    inside = pieces[0].shape[0] // size
-    for p, piece in enumerate(pieces):
-        for i in range(inside):
-
-            @pl.when(pair == p * inside + i)
-            def _():
-                scratch[...] = piece[i * size : (i + 1) * size, :]
-
-
-def add_err(pair, me, low, high, left_ref, piece, words_ref, facts, err_ref, acc_ref):
+def add_err(pair, me, low, high, left_ref, piece, words_ref, facts_ref, err_ref, at_pair, acc):
     relations, half = words_ref.shape[0], words_ref.shape[1]
     rows, width = 2 * half, piece.shape[0] // 2
     lane = lax.broadcasted_iota(jnp.int32, (half, LANES), 1)
-    words, bits, blocks = [], [], []
+    words, bits, blocks, columns = [], [], [], []
     for s in range(2):
         chip = chip_of(me, 2 * pair + s, low, high)
         column = lax.rem(chip, BITS) * LANES + lane
@@ -67,111 +58,92 @@
         words.append(word)
         bits.append(jnp.left_shift(1, column - word * BITS))
         blocks.append(pl.multiple_of(lax.div(chip, BITS) * LANES, LANES))
-
-    def at(k):
-        return slice(k * rows, (k + 1) * rows)
-
-    whole_model = nt(left_ref[...], piece)
+        columns.append(pl.multiple_of(chip * width, width))
+    model = nt(left_ref[...], piece)
     errs = []
     for k in range(relations):
-        model = whole_model[at(k), :]
+        at = slice(k * rows, (k + 1) * rows)
         tiles = []
         for s in range(2):
             marks = jnp.take_along_axis(
                 words_ref[k, :, pl.ds(blocks[s], LANES)], words[s], axis=1
             )
-            data = facts[s][k].astype(F32)
-            diff = model[:, s * width : (s + 1) * width] - data
+            data = facts_ref[k, :, pl.ds(columns[s], width)].astype(F32)
+            diff = model[at, s * width : (s + 1) * width] - data
             top = jnp.where((marks & bits[s]) != 0, diff[:half], 0.0)
             low_bits = jnp.left_shift(bits[s], 16)
             bottom = jnp.where((marks & low_bits) != 0, diff[half:], 0.0)
             tiles.append(jnp.concatenate([top, bottom], axis=0).astype(BF16))
-        err = jnp.concatenate(tiles, axis=1)
-        err_ref[0, at(k), :] = err
-        errs.append(err)
-    acc_ref[...] += nn(jnp.concatenate(errs, axis=0), piece)
+        errs.append(jnp.concatenate(tiles, axis=1))
+        err_ref[at_pair, at, :] = errs[-1]
+    acc[...] += nn(jnp.concatenate(errs, axis=0), piece)
 
 
 def early_kernel(
-    low, high, me_ref, words_ref, facts0_ref, facts1_ref, own_ref, cores_ref, column_ref,
+    low, high, me_ref, words_ref, facts_ref, own_ref, cores_ref, column_ref,
     err_ref, left_ref, acc_ref,
 ):
-    pair = pl.program_id(0)
     rows = own_ref.shape[0]
-
-    @pl.when(pair == 0)
-    def _():
-        acc_ref[...] = jnp.zeros_like(acc_ref)
-        for k in range(cores_ref.shape[0]):
-            left_ref[k * rows : (k + 1) * rows, :] = nn(own_ref[...], cores_ref[k]).astype(BF16)
-
-    add_err(
-        pair, me_ref[0], low, high, left_ref, column_ref[...], words_ref,
-        (facts0_ref, facts1_ref), err_ref, acc_ref,
-    )
-
-
-def late_kernel(
-    low, high, first, me_ref, words_ref, facts0_ref, facts1_ref, left_ref, part_ref, _, *rest
-):
-    pieces, (err_ref, *pulls) = rest[: low - 1], rest[low - 1 : -2]
-    piece_ref, acc_ref = rest[-2:]
-    step = pl.program_id(0)
-
-    @pl.when(step == 0)
-    def _():
-        acc_ref[...] = part_ref[...]
-
-    take_pair(pieces, step, piece_ref, piece_ref.shape[0])
-    add_err(
-        step + first, me_ref[0], low, high, left_ref, piece_ref[...], words_ref,
-        (facts0_ref, facts1_ref), err_ref, acc_ref,
-    )
-
-    @pl.when(step == pl.num_programs(0) - 1)
-    def _():
-        size = pulls[0].shape[0]
-        far = me_ref[0] // low
-        for d in range(high):
-            at = pl.multiple_of(jnp.bitwise_xor(far, d) * size, size)
-            pulls[d][...] = acc_ref[pl.ds(at, size), :].astype(BF16)
-
-
-def rows_kernel(low, rel, me_ref, err_ref, left_ref, cores_ref, *rest):
-    pieces, outs = rest[:low], rest[low : low + rel]
-    piece_ref, _, total_ref, own_ref = rest[low + rel :]
+    acc_ref[...] = jnp.zeros_like(acc_ref)
+    for k in range(cores_ref.shape[0]):
+        left_ref[k * rows : (k + 1) * rows, :] = nn(own_ref[...], cores_ref[k]).astype(BF16)
+    for pair in range(err_ref.shape[0]):
+        piece = column_ref[2 * pair * rows : 2 * (pair + 1) * rows, :]
+        add_err(
+            pair, me_ref[0], low, high, left_ref, piece, words_ref, facts_ref, err_ref, pair, acc_ref
+        )
+
+
+def late_kernel(low, high, me_ref, words_ref, facts_ref, left_ref, part_ref, *rest):
+    pieces, (err_ref, *pulls) = rest[: low - 1], rest[low - 1 : -1]
+    acc_ref = rest[-1]
+    acc_ref[...] = part_ref[...]
+    first = high // 2
+    wide = err_ref.shape[2]
+    for step in range(err_ref.shape[0]):
+        q, inside = divmod(step, first)
+        piece = pieces[q][inside * wide : (inside + 1) * wide, :]
+        add_err(
+            step + first, me_ref[0], low, high, left_ref, piece, words_ref, facts_ref,
+            err_ref, step, acc_ref,
+        )
+    size = pulls[0].shape[0]
+    far = me_ref[0] // low
+    for d in range(high):
+        at = pl.multiple_of(jnp.bitwise_xor(far, d) * size, size)
+        pulls[d][...] = acc_ref[pl.ds(at, size), :].astype(BF16)
+
+
+def rows_kernel(rel, me_ref, err_ref, left_ref, cores_ref, *rest):
+    pieces, outs, total_ref = rest[: -rel - 1], rest[-rel - 1 : -1], rest[-1]
     mine = me_ref[1]
-    step, pairs = pl.program_id(0), pl.num_programs(0)
-    pair = lax.rem(step + 1, pairs)
-
-    @pl.when(step == 0)
-    def _():
-        own_ref[...] = jnp.zeros_like(own_ref)
-
-    take_pair(pieces, pair, piece_ref, piece_ref.shape[0])
     rank = left_ref.shape[1]
-    rows = piece_ref.shape[0] // 2
+    wide = err_ref.shape[2]
+    rows = wide // 2
+    sub = rows // rel
     relations = cores_ref.shape[0] // rank
-    own = own_ref[...]
-    right_all = nt(piece_ref[...], cores_ref[...]).astype(BF16)
-    total_ref[...] = tn(err_ref[0], left_ref[...])
-    for p in range(relations):
-        own = own + nn(
-            err_ref[0, p * rows : (p + 1) * rows, :], right_all[:, p * rank : (p + 1) * rank]
-        )
-    own_ref[...] = own
-
-    @pl.when(step == pairs - 1)
-    def _():
-        total_ref[:rows, :] += own_ref[...]
-
-    sub = rows // rel
-    for h in range(rel):
-        piece = jnp.bitwise_xor(mine, h) * sub
+    inside = pieces[0].shape[0] // wide
+    own = None
+
+    def put(block, at):
+        for h in range(rel):
+            src = pl.multiple_of(at + jnp.bitwise_xor(mine, h) * sub, sub)
+            outs[h][block * sub : (block + 1) * sub, :] = total_ref[pl.ds(src, sub), :]
+
+    pairs = err_ref.shape[0]
+    for pair in range(pairs):
+        q, at = divmod(pair, inside)
+        piece = pieces[q][at * wide : (at + 1) * wide, :]
+        right = nt(piece, cores_ref[...]).astype(BF16)
+        start = pair * wide
+        total_ref[start : start + wide, :] = tn(err_ref[pair], left_ref[...])
+        for k in range(relations):
+            term = nn(err_ref[pair, k * rows : (k + 1) * rows, :], right[:, k * rank : (k + 1) * rank])
+            own = term if own is None else own + term
         for s in range(2):
-            src = pl.multiple_of(piece + s * rows, sub)
-            dst = pl.multiple_of((2 * pair + s) * sub, sub)
-            outs[h][pl.ds(dst, sub), :] = total_ref[pl.ds(src, sub), :]
+            put(2 * pair + s, start + s * rows)
+    total_ref[pairs * wide :, :] = own
+    put(2 * pairs, pairs * wide)
 
 
 def scale_code(block):
@@ -202,8 +174,8 @@
 
 
 def merge_kernel(low, high, rel, me_ref, column_ref, *rest):
-    pulls, shares, outs = rest[:high], rest[high : high + rel], rest[high + rel : -1]
-    total_ref = rest[-1]
+    pulls, early = rest[:high], rest[high : high + rel]
+    late, outs, total_ref = rest[high + rel : high + 2 * rel], rest[high + 2 * rel : -1], rest[-1]
     rank = column_ref.shape[1]
     rows = column_ref.shape[0] // high
     near = jnp.bitwise_and(me_ref[0], low - 1)
@@ -215,7 +187,7 @@
             )
         total_ref[k * rank : (k + 1) * rank, :] = acc
     size = total_ref.shape[0] // low
-    sub = shares[0].shape[0] // low // high
+    sub = early[0].shape[0] // (high + 1)
     core_at = high * sub
     core_codes = []
     for b in range(low):
@@ -227,10 +199,13 @@
     for q in range(low):
         codes = []
         for d in range(high):
-            at = slice((q * high + d) * sub, (q * high + d + 1) * sub)
-            part = shares[0][at, :]
+            shares, slot = (early, d) if q == 0 else (late, (q - 1) * high + d)
+            part = shares[0][slot * sub : (slot + 1) * sub, :]
             for h in range(1, rel):
-                part = part + shares[h][at, :]
+                part = part + shares[h][slot * sub : (slot + 1) * sub, :]
+            if q == 0 and d == 0:
+                for share in early + late:
+                    part = part + share[share.shape[0] - sub :, :]
             span = slice(d * sub, (d + 1) * sub)
             if q == 0:
                 outs[q][span, :] = part
@@ -332,118 +307,76 @@
     spare = -packed.shape[2] % LANES
     packed = jnp.pad(packed, ((0, 0), (0, 0), (0, spare)))
 
-    def whole(shape):
-        return pl.BlockSpec(shape, lambda t, me: (0,) * len(shape))
-
-    def facts_block(first, s):
-        return pl.BlockSpec(
-            (relations, rows, rows),
-            lambda t, me: (0, 0, chip_of(me[0], 2 * (t + first) + s, low, high)),
-        )
-
     stack, pairs, first = relations * rows, ent // 2, high // 2
     wide = 2 * rows
+    sub = rows // rel
     shape = jax.ShapeDtypeStruct
-    cost = lambda share: pl.CostEstimate(
-        flops=int(4 * stack * n_all * rank * share),
-        bytes_accessed=int(4 * stack * n_all * share),
-        transcendentals=0,
-    )
-    err, left, part = pl.pallas_call(
+    smem = pl.BlockSpec(memory_space=pltpu.SMEM)
+    vmem = pl.BlockSpec(memory_space=pltpu.VMEM)
+
+    def cost(share):
+        return pl.CostEstimate(
+            flops=int(4 * stack * n_all * rank * share),
+            bytes_accessed=int(4 * stack * n_all * share),
+            transcendentals=0,
+        )
+
+    early_call = pl.pallas_call(
         functools.partial(early_kernel, low, high),
-        grid_spec=pltpu.PrefetchScalarGridSpec(
-            num_scalar_prefetch=1,
-            grid=(first,),
-            in_specs=[
-                whole(packed.shape),
-                facts_block(0, 0),
-                facts_block(0, 1),
-                whole((rows, rank)),
-                whole(cores.shape),
-                pl.BlockSpec((wide, rank), lambda t, me: (t, 0)),
-            ],
-            out_specs=[
-                pl.BlockSpec((1, stack, wide), lambda t, me: (t, 0, 0)),
-                whole((stack, rank)),
-                whole((stack, rank)),
-            ],
-        ),
+        in_specs=[smem] + [vmem] * 5,
         out_shape=[
-            shape((pairs, stack, wide), BF16),
+            shape((first, stack, wide), BF16),
             shape((stack, rank), BF16),
             shape((stack, rank), F32),
         ],
+        compiler_params=LARGE,
         cost_estimate=cost(first / pairs),
-        compiler_params=pltpu.CompilerParams(vmem_limit_bytes=16 * MIB),
         name="early_kernel",
-    )(me, packed, facts, facts, factors, cores, column)
-
-    err, *pulls = pl.pallas_call(
-        functools.partial(late_kernel, low, high, first),
-        grid_spec=pltpu.PrefetchScalarGridSpec(
-            num_scalar_prefetch=1,
-            grid=(pairs - first,),
-            in_specs=[
-                whole(packed.shape),
-                facts_block(first, 0),
-                facts_block(first, 1),
-                whole((stack, rank)),
-                whole((stack, rank)),
-                pl.BlockSpec(memory_space=pl.ANY),
-            ]
-            + [whole(column.shape)] * (low - 1),
-            out_specs=[pl.BlockSpec((1, stack, wide), lambda t, me: (t + first, 0, 0))]
-            + [whole((per * rows, rank))] * high,
-            scratch_shapes=[pltpu.VMEM((wide, rank), BF16), pltpu.VMEM((stack, rank), F32)],
-        ),
-        out_shape=[shape(err.shape, BF16)] + [shape((per * rows, rank), BF16)] * high,
-        input_output_aliases={6: 0},
+    )
+    early_err, left, part = early_call(me, packed, facts, factors, cores, column)
+
+    def rows_call(blocks):
+        return pl.pallas_call(
+            functools.partial(rows_kernel, rel),
+            in_specs=[smem] + [vmem] * (3 + (1 if blocks == first else low - 1)),
+            out_shape=[shape(((2 * blocks + 1) * sub, rank), F32)] * rel,
+            scratch_shapes=[pltpu.VMEM((blocks * wide + rows, rank), F32)],
+            compiler_params=LARGE,
+            cost_estimate=cost(1.5 * blocks / pairs),
+            name="rows_kernel",
+        )
+
+    stacked = cores.reshape(relations * rank, rank)
+    early_shares = rows_call(first)(me, early_err, left, stacked, column)
+
+    late_call = pl.pallas_call(
+        functools.partial(late_kernel, low, high),
+        in_specs=[smem] + [vmem] * (3 + low),
+        out_shape=[shape((pairs - first, stack, wide), BF16)]
+        + [shape((per * rows, rank), BF16)] * high,
+        scratch_shapes=[pltpu.VMEM((stack, rank), F32)],
+        compiler_params=LARGE,
         cost_estimate=cost(1 - first / pairs),
-        compiler_params=pltpu.CompilerParams(vmem_limit_bytes=16 * MIB),
         name="late_kernel",
-    )(me, packed, facts, facts, left, part, err, *nears)
-
+    )
+    late_err, *pulls = late_call(me, packed, facts, left, part, *nears)
     pulls = from_partners(pulls[0], high, lambda d: far_swap(pulls[d], d))
 
-    sub = rows // rel
-    rows_call = pl.pallas_call(
-        functools.partial(rows_kernel, low, rel),
-        grid_spec=pltpu.PrefetchScalarGridSpec(
-            num_scalar_prefetch=1,
-            grid=(pairs,),
-            in_specs=[
-                pl.BlockSpec((1, stack, wide), lambda t, me: ((t + 1) % pairs, 0, 0)),
-                whole((stack, rank)),
-                whole((relations * rank, rank)),
-            ]
-            + [whole(column.shape)] * low,
-            out_specs=[whole((ent * sub, rank))] * rel,
-            scratch_shapes=[
-                pltpu.VMEM((wide, rank), BF16),
-                pltpu.VMEM((wide, relations * rank), BF16),
-                pltpu.VMEM((wide, rank), F32),
-                pltpu.VMEM((rows, rank), F32),
-            ],
-        ),
-        out_shape=[shape((ent * sub, rank), F32)] * rel,
-        cost_estimate=cost(1.5),
-        compiler_params=pltpu.CompilerParams(vmem_limit_bytes=16 * MIB),
-        name="rows_kernel",
-    )
-    shares = rows_call(me, err, left, cores.reshape(relations * rank, rank), column, *nears)
-    shares = [shares[0]] + [swap(shares[h], "rel", rel, h) for h in range(1, rel)]
+    late_shares = rows_call(pairs - first)(me, late_err, left, stacked, *nears)
+    early_shares = from_partners(early_shares[0], rel, lambda h: swap(early_shares[h], "rel", rel, h))
+    late_shares = from_partners(late_shares[0], rel, lambda h: swap(late_shares[h], "rel", rel, h))
 
     size = per * rank // low
     merged = pl.pallas_call(
         functools.partial(merge_kernel, low, high, rel),
         in_specs=[pl.BlockSpec(memory_space=pltpu.SMEM)]
-        + [pl.BlockSpec(memory_space=pltpu.VMEM)] * (1 + high + rel),
+        + [pl.BlockSpec(memory_space=pltpu.VMEM)] * (1 + high + 2 * rel),
         out_shape=[shape((high * sub, rank), F32)]
         + [shape((high * sub + low * size + scale_rows(high + low), rank), I16)] * (low - 1),
         scratch_shapes=[pltpu.VMEM((per * rank, rank), F32)],
         compiler_params=pltpu.CompilerParams(vmem_limit_bytes=8 * MIB),
         name="merge_kernel",
-    )(me, column, *pulls, *shares)
+    )(me, column, *pulls, *early_shares, *late_shares)
     mine, sent = merged[:2]
     merged = from_partners(sent, low, lambda q: near_swap(merged[q], q))
 

time: 62.4 us -> 58.4 us (0.936)
  Pallas kernels: 15.9 us -> 11.7 us
  starting transfers between devices: 21.8 us -> 22.6 us
    pallas_call x3 -> x4, Pallas kernels: 13.3 us -> 9.08 us  [the longest x1 3.29 us: gradients(): late_shares = rows_call(pairs - first)(me, late_err, left, stacked, *nears)]
    ppermute x17 -> x18, starting transfers between devices: 21.8 us -> 22.6 us  [swap(): return lax.ppermute(x, axis, [(i, i ^ distance) for i in range(size)])]
    ppermute x17 -> x18, waiting for transfers between devices: 18.4 us -> 17.8 us  [swap(): return lax.ppermute(x, axis, [(i, i ^ distance) for i in range(size)])]
  transfers between devices with their start and end apart: 17 -> 18, of which waited for: 10 -> 11; matrix products, arithmetic and copies ran while one was open for 4% -> 4% of each run, Pallas kernels for 6% -> 8%
where the time goes in v5:
time: 58.4 us; the launch traced here: 58.2 us
  starting transfers between devices  22.6 us (39%)
  waiting for transfers between devices  17.8 us (30%)
  Pallas kernels  11.7 us (20%)
  local copies, waits for them, and re-layouts  5.15 us (9%)
  between operations  0.82 us (1%)
    ppermute x18, starting transfers between devices, swap(): return lax.ppermute(x, axis, [(i, i ^ distance) for i in range(size)])  22.6 us
    ppermute x18, waiting for transfers between devices, swap(): return lax.ppermute(x, axis, [(i, i ^ distance) for i in range(size)])  17.8 us
    unnamed x13, local copies, waits for them, and re-layouts  3.55 us
    pallas_call x1, Pallas kernels, gradients(): late_shares = rows_call(pairs - first)(me, late_err, left, stacked, *nears)  3.29 us
    pallas_call x1, Pallas kernels, gradients(): late_err, *pulls = late_call(me, packed, facts, left, part, *nears)  2.75 us
    pallas_call x1, Pallas kernels, gradients(): early_shares = rows_call(first)(me, early_err, left, stacked, column)  1.56 us
    slice x1, local copies, waits for them, and re-layouts, gradients(): packed = observed[:, :half] | jnp.left_shift(observed[:, half:], 16)  1.53 us
    pallas_call x1, Pallas kernels, gradients(): early_call(me, packed, facts, factors, cores, column)  1.48 us
  transfers between devices with their start and end apart: 18, of which 11 were waited for; matrix products, arithmetic and copies ran while one was open for 4% of the time, Pallas kernels for 8%

profile of v5, /device:TPU:0, one launch (start us, length us, event | category | flops | bytes accessed | tf_op | source)
XLA Modules:
  0.0 58.2 jit_solution(4025855712367662581)
XLA Ops:
  0.7 5.1 %collective-permute-start.2 = (bf16[128,128]{1,0:T(8,128)(2,1)}, bf16[128,128]{1,0:T(8,128)(2,1)S(1)}, u32[]{:S(2)}, u32[]{:S(2)}) collective-permute-start(bf16[128,128]{1,0:T(8,128)(2,1)} %own_ref.1), channel_id=1, source_target_pairs={{0,12},{1,13},{2,14},{3,15},{4,8},{5,9},{6,10},{7,11},{8,4},{9,5},... | collective-permute-start | bytes 98312 | tf_op jit(solution)/shard_map/ppermute | solution.py:23
  5.8 0.0 collective-permute-start.1
  5.8 0.6 %collective-permute-start = (bf16[128,128]{1,0:T(8,128)(2,1)}, bf16[128,128]{1,0:T(8,128)(2,1)S(1)}, u32[]{:S(2)}, u32[]{:S(2)}) collective-permute-start(bf16[128,128]{1,0:T(8,128)(2,1)} %own_ref.1), channel_id=1, source_target_pairs={{0,4},{1,5},{2,6},{3,7},{4,0},{5,1},{6,2},{7,3},{8,12},{9,13},{10,... | collective-permute-start | bytes 98312 | tf_op jit(solution)/shard_map/ppermute | solution.py:23
  6.4 1.5 %fusion = (s32[8,64,158]{1,0,2:T(8,128)S(1)}, s32[8,64,158]{1,0,2:T(8,128)S(1)}) fusion(s32[8,128,158]{1,0,2:T(8,128)} %param.5), kind=kLoop, calls=%fused_computation.8 | loop fusion | bytes 1294336 | tf_op jit(solution)/shard_map/slice | solution.py:306
  8.0 0.4 copy.9
  8.3 0.3 copy.8
  8.7 0.1 shift-left_or_fusion
  8.9 1.1 %collective-permute-done = bf16[128,128]{1,0:T(8,128)(2,1)S(1)} collective-permute-done((bf16[128,128]{1,0:T(8,128)(2,1)}, bf16[128,128]{1,0:T(8,128)(2,1)S(1)}, u32[]{:S(2)}, u32[]{:S(2)}) %collective-permute-start) | collective-permute-done | bytes 32800 | tf_op jit(solution)/shard_map/ppermute | solution.py:23
  9.9 0.9 %collective-permute-done.1 = bf16[128,128]{1,0:T(8,128)(2,1)S(1)} collective-permute-done((bf16[128,128]{1,0:T(8,128)(2,1)}, bf16[128,128]{1,0:T(8,128)(2,1)S(1)}, u32[]{:S(2)}, u32[]{:S(2)}) %collective-permute-start.1) | collective-permute-done | bytes 32800 | tf_op jit(solution)/shard_map/ppermute | solution.py:23
  10.8 0.0 collective-permute-done.2
  10.8 2.5 %collective-permute-start.5 = (bf16[512,128]{1,0:T(8,128)(2,1)S(1)}, bf16[512,128]{1,0:T(8,128)(2,1)S(1)}, u32[]{:S(2)}, u32[]{:S(2)}) collective-permute-start(bf16[512,128]{1,0:T(8,128)(2,1)S(1)} %constant_dynamic-update-slice_fusion.column_ref.rest_0_), channel_id=1, source_target_pairs={{0,3},{1,2},{2,1},{3,0},{4,7},{5,6},{6,5},{7,4},{8,11},{9,10},{10,... | collective-permute-start | bytes 393224 | tf_op jit(solution)/shard_map/ppermute | solution.py:23
  13.4 0.5 collective-permute-start.4
  13.9 0.5 collective-permute-start.3
  14.4 0.1 pad_add_fusion.me_ref
  14.5 2.2 %copy-done = bf16[8,128,2048]{2,1,0:T(8,128)(2,1)S(1)} copy-done((bf16[8,128,2048]{2,1,0:T(8,128)(2,1)S(1)}, bf16[8,128,2048]{2,1,0:T(8,128)(2,1)}, u32[]{:S(2)}) %copy-start) | copy-done | bytes 4194328
  16.7 1.5 %early_kernel.1 = (bf16[2,1024,256]{2,1,0:T(8,128)(2,1)S(1)}, bf16[1024,128]{1,0:T(8,128)(2,1)S(1)}, f32[1024,128]{1,0:T(8,128)S(1)}) custom-call(s32[2]{0:T(128)S(1)} %pad_add_fusion.me_ref, s32[8,64,256]{2,1,0:T(8,128)S(1)} %pad.4.words_ref, bf16[8,128,2048]{2,1,0:T(8,128)(2,1)S(1)} %copy-done, bf16[128,128]{1,0:T(8,128)(2,1)S(1)} %copy-done.2, ...), custom_call_target="tpu_custom_call" | custom-call | flops 268435456 | bytes 2097152 | tf_op jit(solution)/shard_map/early_kernel/pallas_call | solution.py:336
  18.2 0.0 collective-permute-done.5.rest_2_
  18.2 0.8 %collective-permute-done.4.rest_1_ = bf16[512,128]{1,0:T(8,128)(2,1)S(1)} collective-permute-done((bf16[512,128]{1,0:T(8,128)(2,1)S(1)}, bf16[512,128]{1,0:T(8,128)(2,1)S(1)}, u32[]{:S(2)}, u32[]{:S(2)}) %collective-permute-start.4) | collective-permute-done | bytes 131104 | tf_op jit(solution)/shard_map/ppermute | solution.py:23
  19.0 2.7 %late_kernel.1 = (bf16[6,1024,256]{2,1,0:T(8,128)(2,1)S(1)}, bf16[256,128]{1,0:T(8,128)(2,1)S(1)}, bf16[256,128]{1,0:T(8,128)(2,1)S(1)}, bf16[256,128]{1,0:T(8,128)(2,1)S(1)}, bf16[256,128]{1,0:T(8,128)(2,1)S(1)}) custom-call(s32[2]{0:T(128)S(1)} %pad_add_fusion.me_ref, s32[8,64,256]{2,1,0:T(8,128)S(1)} %pad.4.words_ref, bf16[8,128,2048]{2,1,0:T(8,128)(2,1)S(1)} %copy-done, ...), custom_call_target="tpu_custom_call" | custom-call | flops 805306368 | bytes 6291456 | tf_op jit(solution)/shard_map/late_kernel/pallas_call | solution.py:362
  21.7 3.3 %rows_kernel.3 = (f32[832,128]{1,0:T(8,128)S(1)}, f32[832,128]{1,0:T(8,128)S(1)}) custom-call(s32[2]{0:T(128)S(1)} %pad_add_fusion.me_ref, bf16[6,1024,256]{2,1,0:T(8,128)(2,1)S(1)} %get-tuple-element.31.err_ref, bf16[1024,128]{1,0:T(8,128)(2,1)S(1)} %get-tuple-element.22.left_ref, bf16[1024,128]{1,0:T(8,128)(2,1)S(1)} %bitcast.9, ...), custom_call_target="tpu_custom_call" | custom-call | flops 1207959552 | bytes 9437184 | tf_op jit(solution)/shard_map/rows_kernel/pallas_call | solution.py:365
  25.0 0.1 collective-permute-start.10
  25.1 1.6 %rows_kernel.2 = (f32[320,128]{1,0:T(8,128)S(1)}, f32[320,128]{1,0:T(8,128)S(1)}) custom-call(s32[2]{0:T(128)S(1)} %pad_add_fusion.me_ref, bf16[2,1024,256]{2,1,0:T(8,128)(2,1)S(1)} %get-tuple-element.28.err_ref, bf16[1024,128]{1,0:T(8,128)(2,1)S(1)} %get-tuple-element.22.left_ref, bf16[1024,128]{1,0:T(8,128)(2,1)S(1)} %bitcast.10, ...), custom_call_target="tpu_custom_call" | custom-call | flops 402653184 | bytes 3145728 | tf_op jit(solution)/shard_map/rows_kernel/pallas_call | solution.py:350
  26.7 0.6 collective-permute-start.9
  27.2 0.0 collective-permute-start.6
  27.2 2.5 %collective-permute-start.7 = (bf16[256,128]{1,0:T(8,128)(2,1)S(1)}, bf16[256,128]{1,0:T(8,128)(2,1)S(1)}, u32[]{:S(2)}, u32[]{:S(2)}) collective-permute-start(bf16[256,128]{1,0:T(8,128)(2,1)S(1)} %get-tuple-element.26), channel_id=1, source_target_pairs={{0,8},{1,9},{2,10},{3,11},{4,12},{5,13},{6,14},{7,15},{8,0},{9,1},... | collective-permute-start | bytes 196616 | tf_op jit(solution)/shard_map/ppermute | solution.py:23
  29.8 1.8 %collective-permute-start.8 = (bf16[256,128]{1,0:T(8,128)(2,1)S(1)}, bf16[256,128]{1,0:T(8,128)(2,1)S(1)}, u32[]{:S(2)}, u32[]{:S(2)}) collective-permute-start(bf16[256,128]{1,0:T(8,128)(2,1)S(1)} %get-tuple-element.27), channel_id=1, source_target_pairs={{0,12},{1,13},{2,14},{3,15},{4,8},{5,9},{6,10},{7,11},{8,4},{9,5},... | collective-permute-start | bytes 196616 | tf_op jit(solution)/shard_map/ppermute | solution.py:23
  31.6 0.0 collective-permute-done.9.rest_5_
  31.6 1.3 %collective-permute-done.6.rest_1_ = bf16[256,128]{1,0:T(8,128)(2,1)S(1)} collective-permute-done((bf16[256,128]{1,0:T(8,128)(2,1)S(1)}, bf16[256,128]{1,0:T(8,128)(2,1)S(1)}, u32[]{:S(2)}, u32[]{:S(2)}) %collective-permute-start.6) | collective-permute-done | bytes 65568 | tf_op jit(solution)/shard_map/ppermute | solution.py:23
  32.9 0.0 collective-permute-done.7.rest_2_
  32.9 2.9 %collective-permute-done.8.rest_3_ = bf16[256,128]{1,0:T(8,128)(2,1)S(1)} collective-permute-done((bf16[256,128]{1,0:T(8,128)(2,1)S(1)}, bf16[256,128]{1,0:T(8,128)(2,1)S(1)}, u32[]{:S(2)}, u32[]{:S(2)}) %collective-permute-start.8) | collective-permute-done | bytes 65568 | tf_op jit(solution)/shard_map/ppermute | solution.py:23
  35.8 1.0 %merge_kernel.1 = (f32[256,128]{1,0:T(8,128)S(1)}, s16[528,128]{1,0:T(8,128)(2,1)S(1)}, s16[528,128]{1,0:T(8,128)(2,1)S(1)}, s16[528,128]{1,0:T(8,128)(2,1)S(1)}) custom-call(s32[2]{0:T(128)S(1)} %pad_add_fusion.me_ref, bf16[512,128]{1,0:T(8,128)(2,1)S(1)} %constant_dynamic-update-slice_fusion.column_ref.rest_0_, ...), custom_call_target="tpu_custom_call" | custom-call | tf_op jit(solution)/shard_map/merge_kernel/pallas_call | solution.py:370
  36.8 1.5 %collective-permute-start.12 = (s16[528,128]{1,0:T(8,128)(2,1)S(1)}, s16[528,128]{1,0:T(8,128)(2,1)S(1)}, u32[]{:S(2)}, u32[]{:S(2)}) collective-permute-start(s16[528,128]{1,0:T(8,128)(2,1)S(1)} %get-tuple-element.36), channel_id=1, source_target_pairs={{0,2},{1,3},{2,0},{3,1},{4,6},{5,7},{6,4},{7,5},{8,10},{9,11},{10,... | collective-permute-start | bytes 405512 | tf_op jit(solution)/shard_map/ppermute | solution.py:23
  38.4 1.6 %collective-permute-start.13 = (s16[528,128]{1,0:T(8,128)(2,1)S(1)}, s16[528,128]{1,0:T(8,128)(2,1)S(1)}, u32[]{:S(2)}, u32[]{:S(2)}) collective-permute-start(s16[528,128]{1,0:T(8,128)(2,1)S(1)} %get-tuple-element.37), channel_id=1, source_target_pairs={{0,3},{1,2},{2,1},{3,0},{4,7},{5,6},{6,5},{7,4},{8,11},{9,10},{10,... | collective-permute-start | bytes 405512 | tf_op jit(solution)/shard_map/ppermute | solution.py:23
  40.0 0.4 collective-permute-start.11
  40.4 3.4 %collective-permute-done.12.rest_3_ = s16[528,128]{1,0:T(8,128)(2,1)S(1)} collective-permute-done((s16[528,128]{1,0:T(8,128)(2,1)S(1)}, s16[528,128]{1,0:T(8,128)(2,1)S(1)}, u32[]{:S(2)}, u32[]{:S(2)}) %collective-permute-start.12) | collective-permute-done | bytes 135200 | tf_op jit(solution)/shard_map/ppermute | solution.py:23
  43.8 0.9 %collective-permute-done.13.rest_4_ = s16[528,128]{1,0:T(8,128)(2,1)S(1)} collective-permute-done((s16[528,128]{1,0:T(8,128)(2,1)S(1)}, s16[528,128]{1,0:T(8,128)(2,1)S(1)}, u32[]{:S(2)}, u32[]{:S(2)}) %collective-permute-start.13) | collective-permute-done | bytes 135200 | tf_op jit(solution)/shard_map/ppermute | solution.py:23
  44.8 0.6 %collective-permute-done.11.rest_2_ = s16[528,128]{1,0:T(8,128)(2,1)S(1)} collective-permute-done((s16[528,128]{1,0:T(8,128)(2,1)S(1)}, s16[528,128]{1,0:T(8,128)(2,1)S(1)}, u32[]{:S(2)}, u32[]{:S(2)}) %collective-permute-start.11) | collective-permute-done | bytes 135200 | tf_op jit(solution)/shard_map/ppermute | solution.py:23
  45.4 0.2 near_kernel.1
  45.6 3.7 %collective-permute-start.15 = (s16[336,128]{1,0:T(8,128)(2,1)S(1)}, s16[336,128]{1,0:T(8,128)(2,1)S(1)}, u32[]{:S(2)}, u32[]{:S(2)}) collective-permute-start(s16[336,128]{1,0:T(8,128)(2,1)S(1)} %get-tuple-element.40), channel_id=1, source_target_pairs={{0,8},{1,9},{2,10},{3,11},{4,12},{5,13},{6,14},{7,15},{8,0},{9,1},... | collective-permute-start | bytes 258056 | tf_op jit(solution)/shard_map/ppermute | solution.py:23
  49.3 0.9 %collective-permute-start.16 = (s16[336,128]{1,0:T(8,128)(2,1)S(1)}, s16[336,128]{1,0:T(8,128)(2,1)S(1)}, u32[]{:S(2)}, u32[]{:S(2)}) collective-permute-start(s16[336,128]{1,0:T(8,128)(2,1)S(1)} %get-tuple-element.41), channel_id=1, source_target_pairs={{0,12},{1,13},{2,14},{3,15},{4,8},{5,9},{6,10},{7,11},{8,4},{9,5},... | collective-permute-start | bytes 258056 | tf_op jit(solution)/shard_map/ppermute | solution.py:23
  50.2 0.0 collective-permute-start.14
  50.2 4.1 %collective-permute-done.15.rest_1_.rest_2_ = s16[336,128]{1,0:T(8,128)(2,1)S(1)} collective-permute-done((s16[336,128]{1,0:T(8,128)(2,1)S(1)}, s16[336,128]{1,0:T(8,128)(2,1)S(1)}, u32[]{:S(2)}, u32[]{:S(2)}) %collective-permute-start.15) | collective-permute-done | bytes 86048 | tf_op jit(solution)/shard_map/ppermute | solution.py:23
  54.3 1.3 %collective-permute-done.16.rest_2_.rest_3_ = s16[336,128]{1,0:T(8,128)(2,1)S(1)} collective-permute-done((s16[336,128]{1,0:T(8,128)(2,1)S(1)}, s16[336,128]{1,0:T(8,128)(2,1)S(1)}, u32[]{:S(2)}, u32[]{:S(2)}) %collective-permute-start.16) | collective-permute-done | bytes 86048 | tf_op jit(solution)/shard_map/ppermute | solution.py:23
  55.7 0.3 collective-permute-done.14.rest_0_.rest_1_
  56.0 0.1 collective-permute-start.17
  56.1 1.4 %place_kernel.1 = f32[1024,128]{1,0:T(8,128)} custom-call(s32[2]{0:T(128)S(1)} %pad_add_fusion.me_ref, s16[336,128]{1,0:T(8,128)(2,1)S(1)} %get-tuple-element.39.rest_0_, s16[336,128]{1,0:T(8,128)(2,1)S(1)} %collective-permute-done.14.rest_0_.rest_1_, s16[336,128]{1,0:T(8,128)(2,1)S(1)} %collective-permute-done.15.rest_1_.rest_2_, ...), custom_call_target="tpu_custom_call" | custom-call | tf_op jit(solution)/shard_map/place_kernel/pallas_call | solution.py:406
  57.6 0.0 copy-start.3
  57.6 0.6 %copy-done.3 = f32[2,64,128]{2,1,0:T(8,128)} copy-done((f32[2,64,128]{2,1,0:T(8,128)}, f32[2,64,128]{2,1,0:T(8,128)S(1)}, u32[]{:S(2)}) %copy-start.3) | copy-done | bytes 65560
  (17 shorter events, 0.1 us)
Async XLA Ops:
  0.6 8.2 %copy-start.2 = (bf16[128,128]{1,0:T(8,128)(2,1)S(1)}, bf16[128,128]{1,0:T(8,128)(2,1)}, u32[]{:S(2)}) copy-start(bf16[128,128]{1,0:T(8,128)(2,1)} %own_ref.1) | copy-start | bytes 98308
  0.6 13.8 %copy-start.1 = (bf16[8,128,128]{2,1,0:T(8,128)(2,1)S(1)}, bf16[8,128,128]{2,1,0:T(8,128)(2,1)}, u32[]{:S(2)}) copy-start(bf16[8,128,128]{2,1,0:T(8,128)(2,1)} %cores_ref.1) | copy-start | bytes 786436
  0.7 10.2 %collective-permute-start.2 = (bf16[128,128]{1,0:T(8,128)(2,1)}, bf16[128,128]{1,0:T(8,128)(2,1)S(1)}, u32[]{:S(2)}, u32[]{:S(2)}) collective-permute-start(bf16[128,128]{1,0:T(8,128)(2,1)} %own_ref.1), channel_id=1, source_target_pairs={{0,12},{1,13},{2,14},{3,15},{4,8},{5,9},{6,10},{7,11},{8,4},{9,5},... | collective-permute-start | bytes 98312 | tf_op jit(solution)/shard_map/ppermute | solution.py:23
  5.8 5.0 %collective-permute-start.1 = (bf16[128,128]{1,0:T(8,128)(2,1)}, bf16[128,128]{1,0:T(8,128)(2,1)S(1)}, u32[]{:S(2)}, u32[]{:S(2)}) collective-permute-start(bf16[128,128]{1,0:T(8,128)(2,1)} %own_ref.1), channel_id=1, source_target_pairs={{0,8},{1,9},{2,10},{3,11},{4,12},{5,13},{6,14},{7,15},{8,0},{9,1},... | collective-permute-start | bytes 98312 | tf_op jit(solution)/shard_map/ppermute | solution.py:23
  5.8 4.1 %collective-permute-start = (bf16[128,128]{1,0:T(8,128)(2,1)}, bf16[128,128]{1,0:T(8,128)(2,1)S(1)}, u32[]{:S(2)}, u32[]{:S(2)}) collective-permute-start(bf16[128,128]{1,0:T(8,128)(2,1)} %own_ref.1), channel_id=1, source_target_pairs={{0,4},{1,5},{2,6},{3,7},{4,0},{5,1},{6,2},{7,3},{8,12},{9,13},{10,... | collective-permute-start | bytes 98312 | tf_op jit(solution)/shard_map/ppermute | solution.py:23
  10.8 7.3 %collective-permute-start.5 = (bf16[512,128]{1,0:T(8,128)(2,1)S(1)}, bf16[512,128]{1,0:T(8,128)(2,1)S(1)}, u32[]{:S(2)}, u32[]{:S(2)}) collective-permute-start(bf16[512,128]{1,0:T(8,128)(2,1)S(1)} %constant_dynamic-update-slice_fusion.column_ref.rest_0_), channel_id=1, source_target_pairs={{0,3},{1,2},{2,1},{3,0},{4,7},{5,6},{6,5},{7,4},{8,11},{9,10},{10,... | collective-permute-start | bytes 393224 | tf_op jit(solution)/shard_map/ppermute | solution.py:23
  13.4 5.6 %collective-permute-start.4 = (bf16[512,128]{1,0:T(8,128)(2,1)S(1)}, bf16[512,128]{1,0:T(8,128)(2,1)S(1)}, u32[]{:S(2)}, u32[]{:S(2)}) collective-permute-start(bf16[512,128]{1,0:T(8,128)(2,1)S(1)} %constant_dynamic-update-slice_fusion.column_ref.rest_0_), channel_id=1, source_target_pairs={{0,2},{1,3},{2,0},{3,1},{4,6},{5,7},{6,4},{7,5},{8,10},{9,11},{10,... | collective-permute-start | bytes 393224 | tf_op jit(solution)/shard_map/ppermute | solution.py:23
  13.9 5.1 %collective-permute-start.3 = (bf16[512,128]{1,0:T(8,128)(2,1)S(1)}, bf16[512,128]{1,0:T(8,128)(2,1)S(1)}, u32[]{:S(2)}, u32[]{:S(2)}) collective-permute-start(bf16[512,128]{1,0:T(8,128)(2,1)S(1)} %constant_dynamic-update-slice_fusion.column_ref.rest_0_), channel_id=1, source_target_pairs={{0,1},{1,0},{2,3},{3,2},{4,5},{5,4},{6,7},{7,6},{8,9},{9,8},{10,11... | collective-permute-start | bytes 393224 | tf_op jit(solution)/shard_map/ppermute | solution.py:23
  14.5 2.2 %copy-start = (bf16[8,128,2048]{2,1,0:T(8,128)(2,1)S(1)}, bf16[8,128,2048]{2,1,0:T(8,128)(2,1)}, u32[]{:S(2)}) copy-start(bf16[8,128,2048]{2,1,0:T(8,128)(2,1)} %facts_ref.3) | copy-start | bytes 12582916
  25.0 10.8 %collective-permute-start.10 = (f32[832,128]{1,0:T(8,128)S(1)}, f32[832,128]{1,0:T(8,128)S(1)}, u32[]{:S(2)}, u32[]{:S(2)}) collective-permute-start(f32[832,128]{1,0:T(8,128)S(1)} %get-tuple-element.33), channel_id=1, source_target_pairs={{0,16},{16,0},{1,17},{17,1},{2,18},{18,2},{3,19},{19,3},{4,20},{20... | collective-permute-start | bytes 1277960 | tf_op jit(solution)/shard_map/ppermute | solution.py:23
  26.7 5.0 %collective-permute-start.9 = (f32[320,128]{1,0:T(8,128)S(1)}, f32[320,128]{1,0:T(8,128)S(1)}, u32[]{:S(2)}, u32[]{:S(2)}) collective-permute-start(f32[320,128]{1,0:T(8,128)S(1)} %get-tuple-element.30), channel_id=1, source_target_pairs={{0,16},{16,0},{1,17},{17,1},{2,18},{18,2},{3,19},{19,3},{4,20},{20... | collective-permute-start | bytes 491528 | tf_op jit(solution)/shard_map/ppermute | solution.py:23
  27.2 5.7 %collective-permute-start.6 = (bf16[256,128]{1,0:T(8,128)(2,1)S(1)}, bf16[256,128]{1,0:T(8,128)(2,1)S(1)}, u32[]{:S(2)}, u32[]{:S(2)}) collective-permute-start(bf16[256,128]{1,0:T(8,128)(2,1)S(1)} %get-tuple-element.25), channel_id=1, source_target_pairs={{0,4},{1,5},{2,6},{3,7},{4,0},{5,1},{6,2},{7,3},{8,12},{9,13},{10,... | collective-permute-start | bytes 196616 | tf_op jit(solution)/shard_map/ppermute | solution.py:23
  27.2 5.7 %collective-permute-start.7 = (bf16[256,128]{1,0:T(8,128)(2,1)S(1)}, bf16[256,128]{1,0:T(8,128)(2,1)S(1)}, u32[]{:S(2)}, u32[]{:S(2)}) collective-permute-start(bf16[256,128]{1,0:T(8,128)(2,1)S(1)} %get-tuple-element.26), channel_id=1, source_target_pairs={{0,8},{1,9},{2,10},{3,11},{4,12},{5,13},{6,14},{7,15},{8,0},{9,1},... | collective-permute-start | bytes 196616 | tf_op jit(solution)/shard_map/ppermute | solution.py:23
  29.8 6.1 %collective-permute-start.8 = (bf16[256,128]{1,0:T(8,128)(2,1)S(1)}, bf16[256,128]{1,0:T(8,128)(2,1)S(1)}, u32[]{:S(2)}, u32[]{:S(2)}) collective-permute-start(bf16[256,128]{1,0:T(8,128)(2,1)S(1)} %get-tuple-element.27), channel_id=1, source_target_pairs={{0,12},{1,13},{2,14},{3,15},{4,8},{5,9},{6,10},{7,11},{8,4},{9,5},... | collective-permute-start | bytes 196616 | tf_op jit(solution)/shard_map/ppermute | solution.py:23
  36.8 7.0 %collective-permute-start.12 = (s16[528,128]{1,0:T(8,128)(2,1)S(1)}, s16[528,128]{1,0:T(8,128)(2,1)S(1)}, u32[]{:S(2)}, u32[]{:S(2)}) collective-permute-start(s16[528,128]{1,0:T(8,128)(2,1)S(1)} %get-tuple-element.36), channel_id=1, source_target_pairs={{0,2},{1,3},{2,0},{3,1},{4,6},{5,7},{6,4},{7,5},{8,10},{9,11},{10,... | collective-permute-start | bytes 405512 | tf_op jit(solution)/shard_map/ppermute | solution.py:23
  38.4 6.4 %collective-permute-start.13 = (s16[528,128]{1,0:T(8,128)(2,1)S(1)}, s16[528,128]{1,0:T(8,128)(2,1)S(1)}, u32[]{:S(2)}, u32[]{:S(2)}) collective-permute-start(s16[528,128]{1,0:T(8,128)(2,1)S(1)} %get-tuple-element.37), channel_id=1, source_target_pairs={{0,3},{1,2},{2,1},{3,0},{4,7},{5,6},{6,5},{7,4},{8,11},{9,10},{10,... | collective-permute-start | bytes 405512 | tf_op jit(solution)/shard_map/ppermute | solution.py:23
  40.0 5.4 %collective-permute-start.11 = (s16[528,128]{1,0:T(8,128)(2,1)S(1)}, s16[528,128]{1,0:T(8,128)(2,1)S(1)}, u32[]{:S(2)}, u32[]{:S(2)}) collective-permute-start(s16[528,128]{1,0:T(8,128)(2,1)S(1)} %get-tuple-element.35.rest_1_), channel_id=1, source_target_pairs={{0,1},{1,0},{2,3},{3,2},{4,5},{5,4},{6,7},{7,6},{8,9},{9,8},{10,11... | collective-permute-start | bytes 405512 | tf_op jit(solution)/shard_map/ppermute | solution.py:23
  45.6 8.7 %collective-permute-start.15 = (s16[336,128]{1,0:T(8,128)(2,1)S(1)}, s16[336,128]{1,0:T(8,128)(2,1)S(1)}, u32[]{:S(2)}, u32[]{:S(2)}) collective-permute-start(s16[336,128]{1,0:T(8,128)(2,1)S(1)} %get-tuple-element.40), channel_id=1, source_target_pairs={{0,8},{1,9},{2,10},{3,11},{4,12},{5,13},{6,14},{7,15},{8,0},{9,1},... | collective-permute-start | bytes 258056 | tf_op jit(solution)/shard_map/ppermute | solution.py:23
  49.3 6.4 %collective-permute-start.16 = (s16[336,128]{1,0:T(8,128)(2,1)S(1)}, s16[336,128]{1,0:T(8,128)(2,1)S(1)}, u32[]{:S(2)}, u32[]{:S(2)}) collective-permute-start(s16[336,128]{1,0:T(8,128)(2,1)S(1)} %get-tuple-element.41), channel_id=1, source_target_pairs={{0,12},{1,13},{2,14},{3,15},{4,8},{5,9},{6,10},{7,11},{8,4},{9,5},... | collective-permute-start | bytes 258056 | tf_op jit(solution)/shard_map/ppermute | solution.py:23
  50.2 5.8 %collective-permute-start.14 = (s16[336,128]{1,0:T(8,128)(2,1)S(1)}, s16[336,128]{1,0:T(8,128)(2,1)S(1)}, u32[]{:S(2)}, u32[]{:S(2)}) collective-permute-start(s16[336,128]{1,0:T(8,128)(2,1)S(1)} %get-tuple-element.39.rest_0_), channel_id=1, source_target_pairs={{0,4},{1,5},{2,6},{3,7},{4,0},{5,1},{6,2},{7,3},{8,12},{9,13},{10,... | collective-permute-start | bytes 258056 | tf_op jit(solution)/shard_map/ppermute | solution.py:23
  56.0 1.5 %collective-permute-start.17 = (f32[64,128]{1,0:T(8,128)S(1)}, f32[64,128]{1,0:T(8,128)S(1)}, u32[]{:S(2)}, u32[]{:S(2)}) collective-permute-start(f32[64,128]{1,0:T(8,128)S(1)} %far_kernel.1), channel_id=1, source_target_pairs={{0,16},{16,0},{1,17},{17,1},{2,18},{18,2},{3,19},{19,3},{4,20},{20... | collective-permute-start | bytes 98312 | tf_op jit(solution)/shard_map/ppermute | solution.py:23
  57.6 0.6 %copy-start.3 = (f32[2,64,128]{2,1,0:T(8,128)}, f32[2,64,128]{2,1,0:T(8,128)S(1)}, u32[]{:S(2)}) copy-start(f32[2,64,128]{2,1,0:T(8,128)S(1)} %bitcast_dynamic-update-slice_fusion) | copy-start | bytes 196612

commit v6 on v5

--- a/solution.py
+++ b/solution.py
@@ -130,7 +130,7 @@
             src = pl.multiple_of(at + jnp.bitwise_xor(mine, h) * sub, sub)
             outs[h][block * sub : (block + 1) * sub, :] = total_ref[pl.ds(src, sub), :]
 
-    pairs = err_ref.shape[0]
+    pairs = len(pieces) * inside
     for pair in range(pairs):
         q, at = divmod(pair, inside)
         piece = pieces[q][at * wide : (at + 1) * wide, :]
@@ -138,7 +138,9 @@
         start = pair * wide
         total_ref[start : start + wide, :] = tn(err_ref[pair], left_ref[...])
         for k in range(relations):
-            term = nn(err_ref[pair, k * rows : (k + 1) * rows, :], right[:, k * rank : (k + 1) * rank])
+            term = nn(
+                err_ref[pair, k * rows : (k + 1) * rows, :], right[:, k * rank : (k + 1) * rank]
+            )
             own = term if own is None else own + term
         for s in range(2):
             put(2 * pair + s, start + s * rows)
@@ -173,29 +175,35 @@
     return pl.cdiv(blocks, 16) * 16
 
 
-def merge_kernel(low, high, rel, me_ref, column_ref, *rest):
-    pulls, early = rest[:high], rest[high : high + rel]
-    late, outs, total_ref = rest[high + rel : high + 2 * rel], rest[high + 2 * rel : -1], rest[-1]
-    rank = column_ref.shape[1]
+def core_kernel(low, high, column_ref, *rest):
+    pulls, out_ref = rest[:high], rest[high]
     rows = column_ref.shape[0] // high
-    near = jnp.bitwise_and(me_ref[0], low - 1)
+    total = []
     for k in range(pulls[0].shape[0] // rows):
-        acc = tn(column_ref[:rows, :], pulls[0][k * rows : (k + 1) * rows, :])
-        for d in range(1, high):
-            acc = acc + tn(
+        acc = None
+        for d in range(high):
+            term = tn(
                 column_ref[d * rows : (d + 1) * rows, :], pulls[d][k * rows : (k + 1) * rows, :]
             )
-        total_ref[k * rank : (k + 1) * rank, :] = acc
-    size = total_ref.shape[0] // low
+            acc = term if acc is None else acc + term
+        total.append(acc)
+    total = jnp.concatenate(total, axis=0)
+    size = total.shape[0] // low
+    codes = []
+    for b in range(low):
+        block = total[b * size : (b + 1) * size, :]
+        codes.append(scale_code(block))
+        out_ref[b * size : (b + 1) * size, :] = encode(block, codes[-1])
+    out_ref[low * size :, :] = stack_codes(list(enumerate(codes)))
+
+
+def merge_kernel(low, high, rel, core_ref, *rest):
+    early, late, outs = rest[:rel], rest[rel : 2 * rel], rest[2 * rel :]
     sub = early[0].shape[0] // (high + 1)
     core_at = high * sub
-    core_codes = []
-    for b in range(low):
-        block = total_ref[b * size : (b + 1) * size, :]
-        core_codes.append(scale_code(block))
-        coded = encode(block, core_codes[-1])
-        for out in outs[1:]:
-            out[core_at + b * size : core_at + (b + 1) * size, :] = coded
+    size = core_ref.shape[0] - scale_rows(low)
+    core_codes = core_ref[size:, :].astype(jnp.int32)
+    core_codes = [core_codes[b : b + 1, :] for b in range(low)]
     for q in range(low):
         codes = []
         for d in range(high):
@@ -213,7 +221,8 @@
                 codes.append(scale_code(part))
                 outs[q][span, :] = encode(part, codes[-1])
         if q > 0:
-            outs[q][core_at + low * size :, :] = stack_codes(list(enumerate(codes + core_codes)))
+            outs[q][core_at : core_at + size, :] = core_ref[:size, :]
+            outs[q][core_at + size :, :] = stack_codes(list(enumerate(codes + core_codes)))
 
 
 def near_kernel(low, high, scale, *rest):
@@ -338,7 +347,7 @@
     def rows_call(blocks):
         return pl.pallas_call(
             functools.partial(rows_kernel, rel),
-            in_specs=[smem] + [vmem] * (3 + (1 if blocks == first else low - 1)),
+            in_specs=[smem] + [vmem] * (3 + blocks // first),
             out_shape=[shape(((2 * blocks + 1) * sub, rank), F32)] * rel,
             scratch_shapes=[pltpu.VMEM((blocks * wide + rows, rank), F32)],
             compiler_params=LARGE,
@@ -346,8 +355,12 @@
             name="rows_kernel",
         )
 
+    def halves(shares):
+        return from_partners(shares[0], rel, lambda h: swap(shares[h], "rel", rel, h))
+
     stacked = cores.reshape(relations * rank, rank)
     early_shares = rows_call(first)(me, early_err, left, stacked, column)
+    early_shares = halves(early_shares)
 
     late_call = pl.pallas_call(
         functools.partial(late_kernel, low, high),
@@ -363,20 +376,26 @@
     pulls = from_partners(pulls[0], high, lambda d: far_swap(pulls[d], d))
 
     late_shares = rows_call(pairs - first)(me, late_err, left, stacked, *nears)
-    early_shares = from_partners(early_shares[0], rel, lambda h: swap(early_shares[h], "rel", rel, h))
-    late_shares = from_partners(late_shares[0], rel, lambda h: swap(late_shares[h], "rel", rel, h))
+    late_shares = halves(late_shares)
 
     size = per * rank // low
+    core_call = pl.pallas_call(
+        functools.partial(core_kernel, low, high),
+        in_specs=[vmem] * (1 + high),
+        out_shape=shape((low * size + scale_rows(low), rank), I16),
+        compiler_params=pltpu.CompilerParams(vmem_limit_bytes=8 * MIB),
+        cost_estimate=cost(0.1),
+        name="core_kernel",
+    )
+    core_codes = core_call(column, *pulls)
     merged = pl.pallas_call(
         functools.partial(merge_kernel, low, high, rel),
-        in_specs=[pl.BlockSpec(memory_space=pltpu.SMEM)]
-        + [pl.BlockSpec(memory_space=pltpu.VMEM)] * (1 + high + 2 * rel),
+        in_specs=[vmem] * (1 + 2 * rel),
         out_shape=[shape((high * sub, rank), F32)]
         + [shape((high * sub + low * size + scale_rows(high + low), rank), I16)] * (low - 1),
-        scratch_shapes=[pltpu.VMEM((per * rank, rank), F32)],
         compiler_params=pltpu.CompilerParams(vmem_limit_bytes=8 * MIB),
         name="merge_kernel",
-    )(me, column, *pulls, *early_shares, *late_shares)
+    )(core_codes, *early_shares, *late_shares)
     mine, sent = merged[:2]
     merged = from_partners(sent, low, lambda q: near_swap(merged[q], q))
 

time: 58.4 us -> 57.9 us (level)
    pallas_call x1, Pallas kernels: 0.99 us -> 0.19 us  [gradients(): pl.pallas_call(functools.partial(merge_kernel, low, high, rel), in_specs=...]
where the time goes in v6:
time: 57.9 us; the launch traced here: 57.7 us
  starting transfers between devices  22.6 us (39%)
  waiting for transfers between devices  17.8 us (31%)
  Pallas kernels  11.2 us (19%)
  local copies, waits for them, and re-layouts  5.15 us (9%)
  between operations  0.84 us (1%)
    ppermute x18, starting transfers between devices, swap(): return lax.ppermute(x, axis, [(i, i ^ distance) for i in range(size)])  22.6 us
    ppermute x18, waiting for transfers between devices, swap(): return lax.ppermute(x, axis, [(i, i ^ distance) for i in range(size)])  17.8 us
    unnamed x13, local copies, waits for them, and re-layouts  3.55 us
    pallas_call x1, Pallas kernels, gradients(): late_shares = rows_call(pairs - first)(me, late_err, left, stacked, *nears)  3.29 us
    pallas_call x1, Pallas kernels, gradients(): late_err, *pulls = late_call(me, packed, facts, left, part, *nears)  2.75 us
    pallas_call x1, Pallas kernels, gradients(): early_shares = rows_call(first)(me, early_err, left, stacked, column)  1.56 us
    slice x1, local copies, waits for them, and re-layouts, gradients(): packed = observed[:, :half] | jnp.left_shift(observed[:, half:], 16)  1.53 us
    pallas_call x1, Pallas kernels, gradients(): early_call(me, packed, facts, factors, cores, column)  1.48 us
  transfers between devices with their start and end apart: 18, of which 11 were waited for; matrix products, arithmetic and copies ran while one was open for 4% of the time, Pallas kernels for 8%

profile of v6, /device:TPU:0, one launch (start us, length us, event | category | flops | bytes accessed | tf_op | source)
XLA Modules:
  0.0 57.7 jit_solution(3664224542183332030)
XLA Ops:
  0.7 5.1 %collective-permute-start.2 = (bf16[128,128]{1,0:T(8,128)(2,1)}, bf16[128,128]{1,0:T(8,128)(2,1)S(1)}, u32[]{:S(2)}, u32[]{:S(2)}) collective-permute-start(bf16[128,128]{1,0:T(8,128)(2,1)} %own_ref.1), channel_id=1, source_target_pairs={{0,12},{1,13},{2,14},{3,15},{4,8},{5,9},{6,10},{7,11},{8,4},{9,5},... | collective-permute-start | bytes 98312 | tf_op jit(solution)/shard_map/ppermute | solution.py:23
  5.8 0.0 collective-permute-start.1
  5.8 0.6 %collective-permute-start = (bf16[128,128]{1,0:T(8,128)(2,1)}, bf16[128,128]{1,0:T(8,128)(2,1)S(1)}, u32[]{:S(2)}, u32[]{:S(2)}) collective-permute-start(bf16[128,128]{1,0:T(8,128)(2,1)} %own_ref.1), channel_id=1, source_target_pairs={{0,4},{1,5},{2,6},{3,7},{4,0},{5,1},{6,2},{7,3},{8,12},{9,13},{10,... | collective-permute-start | bytes 98312 | tf_op jit(solution)/shard_map/ppermute | solution.py:23
  6.4 1.5 %fusion = (s32[8,64,158]{1,0,2:T(8,128)S(1)}, s32[8,64,158]{1,0,2:T(8,128)S(1)}) fusion(s32[8,128,158]{1,0,2:T(8,128)} %param.5), kind=kLoop, calls=%fused_computation.8 | loop fusion | bytes 1294336 | tf_op jit(solution)/shard_map/slice | solution.py:315
  8.0 0.4 copy.9
  8.3 0.3 copy.8
  8.7 0.1 shift-left_or_fusion
  8.9 1.1 %collective-permute-done = bf16[128,128]{1,0:T(8,128)(2,1)S(1)} collective-permute-done((bf16[128,128]{1,0:T(8,128)(2,1)}, bf16[128,128]{1,0:T(8,128)(2,1)S(1)}, u32[]{:S(2)}, u32[]{:S(2)}) %collective-permute-start) | collective-permute-done | bytes 32800 | tf_op jit(solution)/shard_map/ppermute | solution.py:23
  9.9 0.9 %collective-permute-done.1 = bf16[128,128]{1,0:T(8,128)(2,1)S(1)} collective-permute-done((bf16[128,128]{1,0:T(8,128)(2,1)}, bf16[128,128]{1,0:T(8,128)(2,1)S(1)}, u32[]{:S(2)}, u32[]{:S(2)}) %collective-permute-start.1) | collective-permute-done | bytes 32800 | tf_op jit(solution)/shard_map/ppermute | solution.py:23
  10.8 2.5 %collective-permute-start.5 = (bf16[512,128]{1,0:T(8,128)(2,1)S(1)}, bf16[512,128]{1,0:T(8,128)(2,1)S(1)}, u32[]{:S(2)}, u32[]{:S(2)}) collective-permute-start(bf16[512,128]{1,0:T(8,128)(2,1)S(1)} %constant_dynamic-update-slice_fusion.column_ref.rest_0_), channel_id=1, source_target_pairs={{0,3},{1,2},{2,1},{3,0},{4,7},{5,6},{6,5},{7,4},{8,11},{9,10},{10,... | collective-permute-start | bytes 393224 | tf_op jit(solution)/shard_map/ppermute | solution.py:23
  13.4 0.5 collective-permute-start.4
  13.9 0.5 collective-permute-start.3
  14.4 0.1 pad_add_fusion.me_ref
  14.5 2.2 %copy-done = bf16[8,128,2048]{2,1,0:T(8,128)(2,1)S(1)} copy-done((bf16[8,128,2048]{2,1,0:T(8,128)(2,1)S(1)}, bf16[8,128,2048]{2,1,0:T(8,128)(2,1)}, u32[]{:S(2)}) %copy-start) | copy-done | bytes 4194328
  16.7 1.5 %early_kernel.1 = (bf16[2,1024,256]{2,1,0:T(8,128)(2,1)S(1)}, bf16[1024,128]{1,0:T(8,128)(2,1)S(1)}, f32[1024,128]{1,0:T(8,128)S(1)}) custom-call(s32[2]{0:T(128)S(1)} %pad_add_fusion.me_ref, s32[8,64,256]{2,1,0:T(8,128)S(1)} %pad.4.words_ref, bf16[8,128,2048]{2,1,0:T(8,128)(2,1)S(1)} %copy-done, bf16[128,128]{1,0:T(8,128)(2,1)S(1)} %copy-done.2, ...), custom_call_target="tpu_custom_call" | custom-call | flops 268435456 | bytes 2097152 | tf_op jit(solution)/shard_map/early_kernel/pallas_call | solution.py:345
  18.2 0.0 collective-permute-done.5.rest_2_
  18.2 0.8 %collective-permute-done.4.rest_1_ = bf16[512,128]{1,0:T(8,128)(2,1)S(1)} collective-permute-done((bf16[512,128]{1,0:T(8,128)(2,1)S(1)}, bf16[512,128]{1,0:T(8,128)(2,1)S(1)}, u32[]{:S(2)}, u32[]{:S(2)}) %collective-permute-start.4) | collective-permute-done | bytes 131104 | tf_op jit(solution)/shard_map/ppermute | solution.py:23
  19.0 2.7 %late_kernel.1 = (bf16[6,1024,256]{2,1,0:T(8,128)(2,1)S(1)}, bf16[256,128]{1,0:T(8,128)(2,1)S(1)}, bf16[256,128]{1,0:T(8,128)(2,1)S(1)}, bf16[256,128]{1,0:T(8,128)(2,1)S(1)}, bf16[256,128]{1,0:T(8,128)(2,1)S(1)}) custom-call(s32[2]{0:T(128)S(1)} %pad_add_fusion.me_ref, s32[8,64,256]{2,1,0:T(8,128)S(1)} %pad.4.words_ref, bf16[8,128,2048]{2,1,0:T(8,128)(2,1)S(1)} %copy-done, ...), custom_call_target="tpu_custom_call" | custom-call | flops 805306368 | bytes 6291456 | tf_op jit(solution)/shard_map/late_kernel/pallas_call | solution.py:375
  21.7 3.3 %rows_kernel.3 = (f32[832,128]{1,0:T(8,128)S(1)}, f32[832,128]{1,0:T(8,128)S(1)}) custom-call(s32[2]{0:T(128)S(1)} %pad_add_fusion.me_ref, bf16[6,1024,256]{2,1,0:T(8,128)(2,1)S(1)} %get-tuple-element.31.err_ref, bf16[1024,128]{1,0:T(8,128)(2,1)S(1)} %get-tuple-element.22.left_ref, bf16[1024,128]{1,0:T(8,128)(2,1)S(1)} %bitcast.9, ...), custom_call_target="tpu_custom_call" | custom-call | flops 1207959552 | bytes 9437184 | tf_op jit(solution)/shard_map/rows_kernel/pallas_call | solution.py:378
  25.0 0.1 collective-permute-start.10
  25.1 1.6 %rows_kernel.2 = (f32[320,128]{1,0:T(8,128)S(1)}, f32[320,128]{1,0:T(8,128)S(1)}) custom-call(s32[2]{0:T(128)S(1)} %pad_add_fusion.me_ref, bf16[2,1024,256]{2,1,0:T(8,128)(2,1)S(1)} %get-tuple-element.28.err_ref, bf16[1024,128]{1,0:T(8,128)(2,1)S(1)} %get-tuple-element.22.left_ref, bf16[1024,128]{1,0:T(8,128)(2,1)S(1)} %bitcast.10, ...), custom_call_target="tpu_custom_call" | custom-call | flops 402653184 | bytes 3145728 | tf_op jit(solution)/shard_map/rows_kernel/pallas_call | solution.py:362
  26.7 0.6 collective-permute-start.9
  27.2 0.0 collective-permute-start.6
  27.2 2.5 %collective-permute-start.7 = (bf16[256,128]{1,0:T(8,128)(2,1)S(1)}, bf16[256,128]{1,0:T(8,128)(2,1)S(1)}, u32[]{:S(2)}, u32[]{:S(2)}) collective-permute-start(bf16[256,128]{1,0:T(8,128)(2,1)S(1)} %get-tuple-element.26), channel_id=1, source_target_pairs={{0,8},{1,9},{2,10},{3,11},{4,12},{5,13},{6,14},{7,15},{8,0},{9,1},... | collective-permute-start | bytes 196616 | tf_op jit(solution)/shard_map/ppermute | solution.py:23
  29.8 1.8 %collective-permute-start.8 = (bf16[256,128]{1,0:T(8,128)(2,1)S(1)}, bf16[256,128]{1,0:T(8,128)(2,1)S(1)}, u32[]{:S(2)}, u32[]{:S(2)}) collective-permute-start(bf16[256,128]{1,0:T(8,128)(2,1)S(1)} %get-tuple-element.27), channel_id=1, source_target_pairs={{0,12},{1,13},{2,14},{3,15},{4,8},{5,9},{6,10},{7,11},{8,4},{9,5},... | collective-permute-start | bytes 196616 | tf_op jit(solution)/shard_map/ppermute | solution.py:23
  31.6 1.3 %collective-permute-done.6.rest_1_ = bf16[256,128]{1,0:T(8,128)(2,1)S(1)} collective-permute-done((bf16[256,128]{1,0:T(8,128)(2,1)S(1)}, bf16[256,128]{1,0:T(8,128)(2,1)S(1)}, u32[]{:S(2)}, u32[]{:S(2)}) %collective-permute-start.6) | collective-permute-done | bytes 65568 | tf_op jit(solution)/shard_map/ppermute | solution.py:23
  32.9 0.0 collective-permute-done.7.rest_2_
  32.9 2.9 %collective-permute-done.8.rest_3_ = bf16[256,128]{1,0:T(8,128)(2,1)S(1)} collective-permute-done((bf16[256,128]{1,0:T(8,128)(2,1)S(1)}, bf16[256,128]{1,0:T(8,128)(2,1)S(1)}, u32[]{:S(2)}, u32[]{:S(2)}) %collective-permute-start.8) | collective-permute-done | bytes 65568 | tf_op jit(solution)/shard_map/ppermute | solution.py:23
  35.8 0.3 core_kernel.1.core_ref
  36.2 0.2 merge_kernel.1
  36.4 1.5 %collective-permute-start.12 = (s16[528,128]{1,0:T(8,128)(2,1)S(1)}, s16[528,128]{1,0:T(8,128)(2,1)S(1)}, u32[]{:S(2)}, u32[]{:S(2)}) collective-permute-start(s16[528,128]{1,0:T(8,128)(2,1)S(1)} %get-tuple-element.36), channel_id=1, source_target_pairs={{0,2},{1,3},{2,0},{3,1},{4,6},{5,7},{6,4},{7,5},{8,10},{9,11},{10,... | collective-permute-start | bytes 405512 | tf_op jit(solution)/shard_map/ppermute | solution.py:23
  37.9 1.6 %collective-permute-start.13 = (s16[528,128]{1,0:T(8,128)(2,1)S(1)}, s16[528,128]{1,0:T(8,128)(2,1)S(1)}, u32[]{:S(2)}, u32[]{:S(2)}) collective-permute-start(s16[528,128]{1,0:T(8,128)(2,1)S(1)} %get-tuple-element.37), channel_id=1, source_target_pairs={{0,3},{1,2},{2,1},{3,0},{4,7},{5,6},{6,5},{7,4},{8,11},{9,10},{10,... | collective-permute-start | bytes 405512 | tf_op jit(solution)/shard_map/ppermute | solution.py:23
  39.5 0.4 collective-permute-start.11
  39.9 3.4 %collective-permute-done.12.rest_3_ = s16[528,128]{1,0:T(8,128)(2,1)S(1)} collective-permute-done((s16[528,128]{1,0:T(8,128)(2,1)S(1)}, s16[528,128]{1,0:T(8,128)(2,1)S(1)}, u32[]{:S(2)}, u32[]{:S(2)}) %collective-permute-start.12) | collective-permute-done | bytes 135200 | tf_op jit(solution)/shard_map/ppermute | solution.py:23
  43.4 0.9 %collective-permute-done.13.rest_4_ = s16[528,128]{1,0:T(8,128)(2,1)S(1)} collective-permute-done((s16[528,128]{1,0:T(8,128)(2,1)S(1)}, s16[528,128]{1,0:T(8,128)(2,1)S(1)}, u32[]{:S(2)}, u32[]{:S(2)}) %collective-permute-start.13) | collective-permute-done | bytes 135200 | tf_op jit(solution)/shard_map/ppermute | solution.py:23
  44.3 0.6 %collective-permute-done.11.rest_2_ = s16[528,128]{1,0:T(8,128)(2,1)S(1)} collective-permute-done((s16[528,128]{1,0:T(8,128)(2,1)S(1)}, s16[528,128]{1,0:T(8,128)(2,1)S(1)}, u32[]{:S(2)}, u32[]{:S(2)}) %collective-permute-start.11) | collective-permute-done | bytes 135200 | tf_op jit(solution)/shard_map/ppermute | solution.py:23
  44.9 0.2 near_kernel.1
  45.2 3.7 %collective-permute-start.15 = (s16[336,128]{1,0:T(8,128)(2,1)S(1)}, s16[336,128]{1,0:T(8,128)(2,1)S(1)}, u32[]{:S(2)}, u32[]{:S(2)}) collective-permute-start(s16[336,128]{1,0:T(8,128)(2,1)S(1)} %get-tuple-element.40), channel_id=1, source_target_pairs={{0,8},{1,9},{2,10},{3,11},{4,12},{5,13},{6,14},{7,15},{8,0},{9,1},... | collective-permute-start | bytes 258056 | tf_op jit(solution)/shard_map/ppermute | solution.py:23
  48.8 0.9 %collective-permute-start.16 = (s16[336,128]{1,0:T(8,128)(2,1)S(1)}, s16[336,128]{1,0:T(8,128)(2,1)S(1)}, u32[]{:S(2)}, u32[]{:S(2)}) collective-permute-start(s16[336,128]{1,0:T(8,128)(2,1)S(1)} %get-tuple-element.41), channel_id=1, source_target_pairs={{0,12},{1,13},{2,14},{3,15},{4,8},{5,9},{6,10},{7,11},{8,4},{9,5},... | collective-permute-start | bytes 258056 | tf_op jit(solution)/shard_map/ppermute | solution.py:23
  49.8 0.0 collective-permute-start.14
  49.8 4.1 %collective-permute-done.15.rest_1_.rest_2_ = s16[336,128]{1,0:T(8,128)(2,1)S(1)} collective-permute-done((s16[336,128]{1,0:T(8,128)(2,1)S(1)}, s16[336,128]{1,0:T(8,128)(2,1)S(1)}, u32[]{:S(2)}, u32[]{:S(2)}) %collective-permute-start.15) | collective-permute-done | bytes 86048 | tf_op jit(solution)/shard_map/ppermute | solution.py:23
  53.9 1.3 %collective-permute-done.16.rest_2_.rest_3_ = s16[336,128]{1,0:T(8,128)(2,1)S(1)} collective-permute-done((s16[336,128]{1,0:T(8,128)(2,1)S(1)}, s16[336,128]{1,0:T(8,128)(2,1)S(1)}, u32[]{:S(2)}, u32[]{:S(2)}) %collective-permute-start.16) | collective-permute-done | bytes 86048 | tf_op jit(solution)/shard_map/ppermute | solution.py:23
  55.2 0.3 collective-permute-done.14.rest_0_.rest_1_
  55.6 0.1 collective-permute-start.17
  55.7 1.4 %place_kernel.1 = f32[1024,128]{1,0:T(8,128)} custom-call(s32[2]{0:T(128)S(1)} %pad_add_fusion.me_ref, s16[336,128]{1,0:T(8,128)(2,1)S(1)} %get-tuple-element.39.rest_0_, s16[336,128]{1,0:T(8,128)(2,1)S(1)} %collective-permute-done.14.rest_0_.rest_1_, s16[336,128]{1,0:T(8,128)(2,1)S(1)} %collective-permute-done.15.rest_1_.rest_2_, ...), custom_call_target="tpu_custom_call" | custom-call | tf_op jit(solution)/shard_map/place_kernel/pallas_call | solution.py:425
  57.1 0.0 collective-permute-done.17
  57.1 0.0 copy-start.3
  57.1 0.6 %copy-done.3 = f32[2,64,128]{2,1,0:T(8,128)} copy-done((f32[2,64,128]{2,1,0:T(8,128)}, f32[2,64,128]{2,1,0:T(8,128)S(1)}, u32[]{:S(2)}) %copy-start.3) | copy-done | bytes 65560
  (18 shorter events, 0.1 us)
Async XLA Ops:
  0.6 8.2 %copy-start.2 = (bf16[128,128]{1,0:T(8,128)(2,1)S(1)}, bf16[128,128]{1,0:T(8,128)(2,1)}, u32[]{:S(2)}) copy-start(bf16[128,128]{1,0:T(8,128)(2,1)} %own_ref.1) | copy-start | bytes 98308
  0.6 13.8 %copy-start.1 = (bf16[8,128,128]{2,1,0:T(8,128)(2,1)S(1)}, bf16[8,128,128]{2,1,0:T(8,128)(2,1)}, u32[]{:S(2)}) copy-start(bf16[8,128,128]{2,1,0:T(8,128)(2,1)} %cores_ref.1) | copy-start | bytes 786436
  0.7 10.2 %collective-permute-start.2 = (bf16[128,128]{1,0:T(8,128)(2,1)}, bf16[128,128]{1,0:T(8,128)(2,1)S(1)}, u32[]{:S(2)}, u32[]{:S(2)}) collective-permute-start(bf16[128,128]{1,0:T(8,128)(2,1)} %own_ref.1), channel_id=1, source_target_pairs={{0,12},{1,13},{2,14},{3,15},{4,8},{5,9},{6,10},{7,11},{8,4},{9,5},... | collective-permute-start | bytes 98312 | tf_op jit(solution)/shard_map/ppermute | solution.py:23
  5.8 5.0 %collective-permute-start.1 = (bf16[128,128]{1,0:T(8,128)(2,1)}, bf16[128,128]{1,0:T(8,128)(2,1)S(1)}, u32[]{:S(2)}, u32[]{:S(2)}) collective-permute-start(bf16[128,128]{1,0:T(8,128)(2,1)} %own_ref.1), channel_id=1, source_target_pairs={{0,8},{1,9},{2,10},{3,11},{4,12},{5,13},{6,14},{7,15},{8,0},{9,1},... | collective-permute-start | bytes 98312 | tf_op jit(solution)/shard_map/ppermute | solution.py:23
  5.8 4.1 %collective-permute-start = (bf16[128,128]{1,0:T(8,128)(2,1)}, bf16[128,128]{1,0:T(8,128)(2,1)S(1)}, u32[]{:S(2)}, u32[]{:S(2)}) collective-permute-start(bf16[128,128]{1,0:T(8,128)(2,1)} %own_ref.1), channel_id=1, source_target_pairs={{0,4},{1,5},{2,6},{3,7},{4,0},{5,1},{6,2},{7,3},{8,12},{9,13},{10,... | collective-permute-start | bytes 98312 | tf_op jit(solution)/shard_map/ppermute | solution.py:23
  10.8 7.3 %collective-permute-start.5 = (bf16[512,128]{1,0:T(8,128)(2,1)S(1)}, bf16[512,128]{1,0:T(8,128)(2,1)S(1)}, u32[]{:S(2)}, u32[]{:S(2)}) collective-permute-start(bf16[512,128]{1,0:T(8,128)(2,1)S(1)} %constant_dynamic-update-slice_fusion.column_ref.rest_0_), channel_id=1, source_target_pairs={{0,3},{1,2},{2,1},{3,0},{4,7},{5,6},{6,5},{7,4},{8,11},{9,10},{10,... | collective-permute-start | bytes 393224 | tf_op jit(solution)/shard_map/ppermute | solution.py:23
  13.4 5.6 %collective-permute-start.4 = (bf16[512,128]{1,0:T(8,128)(2,1)S(1)}, bf16[512,128]{1,0:T(8,128)(2,1)S(1)}, u32[]{:S(2)}, u32[]{:S(2)}) collective-permute-start(bf16[512,128]{1,0:T(8,128)(2,1)S(1)} %constant_dynamic-update-slice_fusion.column_ref.rest_0_), channel_id=1, source_target_pairs={{0,2},{1,3},{2,0},{3,1},{4,6},{5,7},{6,4},{7,5},{8,10},{9,11},{10,... | collective-permute-start | bytes 393224 | tf_op jit(solution)/shard_map/ppermute | solution.py:23
  13.9 5.1 %collective-permute-start.3 = (bf16[512,128]{1,0:T(8,128)(2,1)S(1)}, bf16[512,128]{1,0:T(8,128)(2,1)S(1)}, u32[]{:S(2)}, u32[]{:S(2)}) collective-permute-start(bf16[512,128]{1,0:T(8,128)(2,1)S(1)} %constant_dynamic-update-slice_fusion.column_ref.rest_0_), channel_id=1, source_target_pairs={{0,1},{1,0},{2,3},{3,2},{4,5},{5,4},{6,7},{7,6},{8,9},{9,8},{10,11... | collective-permute-start | bytes 393224 | tf_op jit(solution)/shard_map/ppermute | solution.py:23
  14.5 2.2 %copy-start = (bf16[8,128,2048]{2,1,0:T(8,128)(2,1)S(1)}, bf16[8,128,2048]{2,1,0:T(8,128)(2,1)}, u32[]{:S(2)}) copy-start(bf16[8,128,2048]{2,1,0:T(8,128)(2,1)} %facts_ref.3) | copy-start | bytes 12582916
  25.0 11.2 %collective-permute-start.10 = (f32[832,128]{1,0:T(8,128)S(1)}, f32[832,128]{1,0:T(8,128)S(1)}, u32[]{:S(2)}, u32[]{:S(2)}) collective-permute-start(f32[832,128]{1,0:T(8,128)S(1)} %get-tuple-element.33), channel_id=1, source_target_pairs={{0,16},{16,0},{1,17},{17,1},{2,18},{18,2},{3,19},{19,3},{4,20},{20... | collective-permute-start | bytes 1277960 | tf_op jit(solution)/shard_map/ppermute | solution.py:23
  26.7 9.5 %collective-permute-start.9 = (f32[320,128]{1,0:T(8,128)S(1)}, f32[320,128]{1,0:T(8,128)S(1)}, u32[]{:S(2)}, u32[]{:S(2)}) collective-permute-start(f32[320,128]{1,0:T(8,128)S(1)} %get-tuple-element.30), channel_id=1, source_target_pairs={{0,16},{16,0},{1,17},{17,1},{2,18},{18,2},{3,19},{19,3},{4,20},{20... | collective-permute-start | bytes 491528 | tf_op jit(solution)/shard_map/ppermute | solution.py:23
  27.2 5.7 %collective-permute-start.6 = (bf16[256,128]{1,0:T(8,128)(2,1)S(1)}, bf16[256,128]{1,0:T(8,128)(2,1)S(1)}, u32[]{:S(2)}, u32[]{:S(2)}) collective-permute-start(bf16[256,128]{1,0:T(8,128)(2,1)S(1)} %get-tuple-element.25), channel_id=1, source_target_pairs={{0,4},{1,5},{2,6},{3,7},{4,0},{5,1},{6,2},{7,3},{8,12},{9,13},{10,... | collective-permute-start | bytes 196616 | tf_op jit(solution)/shard_map/ppermute | solution.py:23
  27.2 5.7 %collective-permute-start.7 = (bf16[256,128]{1,0:T(8,128)(2,1)S(1)}, bf16[256,128]{1,0:T(8,128)(2,1)S(1)}, u32[]{:S(2)}, u32[]{:S(2)}) collective-permute-start(bf16[256,128]{1,0:T(8,128)(2,1)S(1)} %get-tuple-element.26), channel_id=1, source_target_pairs={{0,8},{1,9},{2,10},{3,11},{4,12},{5,13},{6,14},{7,15},{8,0},{9,1},... | collective-permute-start | bytes 196616 | tf_op jit(solution)/shard_map/ppermute | solution.py:23
  29.8 6.1 %collective-permute-start.8 = (bf16[256,128]{1,0:T(8,128)(2,1)S(1)}, bf16[256,128]{1,0:T(8,128)(2,1)S(1)}, u32[]{:S(2)}, u32[]{:S(2)}) collective-permute-start(bf16[256,128]{1,0:T(8,128)(2,1)S(1)} %get-tuple-element.27), channel_id=1, source_target_pairs={{0,12},{1,13},{2,14},{3,15},{4,8},{5,9},{6,10},{7,11},{8,4},{9,5},... | collective-permute-start | bytes 196616 | tf_op jit(solution)/shard_map/ppermute | solution.py:23
  36.4 7.0 %collective-permute-start.12 = (s16[528,128]{1,0:T(8,128)(2,1)S(1)}, s16[528,128]{1,0:T(8,128)(2,1)S(1)}, u32[]{:S(2)}, u32[]{:S(2)}) collective-permute-start(s16[528,128]{1,0:T(8,128)(2,1)S(1)} %get-tuple-element.36), channel_id=1, source_target_pairs={{0,2},{1,3},{2,0},{3,1},{4,6},{5,7},{6,4},{7,5},{8,10},{9,11},{10,... | collective-permute-start | bytes 405512 | tf_op jit(solution)/shard_map/ppermute | solution.py:23
  37.9 6.4 %collective-permute-start.13 = (s16[528,128]{1,0:T(8,128)(2,1)S(1)}, s16[528,128]{1,0:T(8,128)(2,1)S(1)}, u32[]{:S(2)}, u32[]{:S(2)}) collective-permute-start(s16[528,128]{1,0:T(8,128)(2,1)S(1)} %get-tuple-element.37), channel_id=1, source_target_pairs={{0,3},{1,2},{2,1},{3,0},{4,7},{5,6},{6,5},{7,4},{8,11},{9,10},{10,... | collective-permute-start | bytes 405512 | tf_op jit(solution)/shard_map/ppermute | solution.py:23
  39.5 5.4 %collective-permute-start.11 = (s16[528,128]{1,0:T(8,128)(2,1)S(1)}, s16[528,128]{1,0:T(8,128)(2,1)S(1)}, u32[]{:S(2)}, u32[]{:S(2)}) collective-permute-start(s16[528,128]{1,0:T(8,128)(2,1)S(1)} %get-tuple-element.35.rest_1_), channel_id=1, source_target_pairs={{0,1},{1,0},{2,3},{3,2},{4,5},{5,4},{6,7},{7,6},{8,9},{9,8},{10,11... | collective-permute-start | bytes 405512 | tf_op jit(solution)/shard_map/ppermute | solution.py:23
  45.2 8.7 %collective-permute-start.15 = (s16[336,128]{1,0:T(8,128)(2,1)S(1)}, s16[336,128]{1,0:T(8,128)(2,1)S(1)}, u32[]{:S(2)}, u32[]{:S(2)}) collective-permute-start(s16[336,128]{1,0:T(8,128)(2,1)S(1)} %get-tuple-element.40), channel_id=1, source_target_pairs={{0,8},{1,9},{2,10},{3,11},{4,12},{5,13},{6,14},{7,15},{8,0},{9,1},... | collective-permute-start | bytes 258056 | tf_op jit(solution)/shard_map/ppermute | solution.py:23
  48.8 6.4 %collective-permute-start.16 = (s16[336,128]{1,0:T(8,128)(2,1)S(1)}, s16[336,128]{1,0:T(8,128)(2,1)S(1)}, u32[]{:S(2)}, u32[]{:S(2)}) collective-permute-start(s16[336,128]{1,0:T(8,128)(2,1)S(1)} %get-tuple-element.41), channel_id=1, source_target_pairs={{0,12},{1,13},{2,14},{3,15},{4,8},{5,9},{6,10},{7,11},{8,4},{9,5},... | collective-permute-start | bytes 258056 | tf_op jit(solution)/shard_map/ppermute | solution.py:23
  49.8 5.8 %collective-permute-start.14 = (s16[336,128]{1,0:T(8,128)(2,1)S(1)}, s16[336,128]{1,0:T(8,128)(2,1)S(1)}, u32[]{:S(2)}, u32[]{:S(2)}) collective-permute-start(s16[336,128]{1,0:T(8,128)(2,1)S(1)} %get-tuple-element.39.rest_0_), channel_id=1, source_target_pairs={{0,4},{1,5},{2,6},{3,7},{4,0},{5,1},{6,2},{7,3},{8,12},{9,13},{10,... | collective-permute-start | bytes 258056 | tf_op jit(solution)/shard_map/ppermute | solution.py:23
  55.6 1.5 %collective-permute-start.17 = (f32[64,128]{1,0:T(8,128)S(1)}, f32[64,128]{1,0:T(8,128)S(1)}, u32[]{:S(2)}, u32[]{:S(2)}) collective-permute-start(f32[64,128]{1,0:T(8,128)S(1)} %far_kernel.1), channel_id=1, source_target_pairs={{0,16},{16,0},{1,17},{17,1},{2,18},{18,2},{3,19},{19,3},{4,20},{20... | collective-permute-start | bytes 98312 | tf_op jit(solution)/shard_map/ppermute | solution.py:23
  57.1 0.6 %copy-start.3 = (f32[2,64,128]{2,1,0:T(8,128)}, f32[2,64,128]{2,1,0:T(8,128)S(1)}, u32[]{:S(2)}) copy-start(f32[2,64,128]{2,1,0:T(8,128)S(1)} %bitcast_dynamic-update-slice_fusion) | copy-start | bytes 196612

commit v7 on v6

--- a/solution.py
+++ b/solution.py
@@ -271,17 +271,19 @@
     owned_ref[...] = total / jnp.sqrt(F32(root))
 
 
-def place_kernel(low, high, size, me_ref, *rest):
+def place_kernel(low, size, first, me_ref, *rest):
     parts, (out_ref, block_ref, sems) = rest[:-3], rest[-3:]
+    if first > 0:
+        parts = parts[1:]
     far = me_ref[0] // low
     copies = []
-    for d in range(high):
-        tile = parts[d].shape[0] - scale_rows(low + 1)
-        code = parts[d][tile:, :].astype(jnp.int32)
+    for d, part in enumerate(parts):
+        tile = part.shape[0] - scale_rows(low + 1)
+        code = part[tile:, :].astype(jnp.int32)
         for b in range(low):
             span = slice(b * size, (b + 1) * size)
-            block_ref[d, span, :] = decode(parts[d][span, :], code[b : b + 1, :])
-        at = pl.multiple_of(jnp.bitwise_xor(far, d) * (low * size), low * size)
+            block_ref[d, span, :] = decode(part[span, :], code[b : b + 1, :])
+        at = pl.multiple_of(jnp.bitwise_xor(far, d + first) * (low * size), low * size)
         copies.append(
             pltpu.make_async_copy(
                 block_ref.at[d], out_ref.at[pl.ds(at, low * size), :], sems.at[d]
@@ -422,19 +424,25 @@
         grad_factors = lax.dynamic_update_index_in_dim(grad_factors, piece, here ^ h, 0)
     grad_factors = grad_factors.reshape(rows, rank)
 
-    grad_cores = pl.pallas_call(
-        functools.partial(place_kernel, low, high, size),
-        in_specs=[pl.BlockSpec(memory_space=pltpu.SMEM)]
-        + [pl.BlockSpec(memory_space=pltpu.VMEM)] * high,
-        out_specs=pl.BlockSpec(memory_space=pl.ANY),
-        out_shape=shape((relations * rank, rank), F32),
-        scratch_shapes=[
-            pltpu.VMEM((high, low * size, rank), F32),
-            pltpu.SemaphoreType.DMA((high,)),
-        ],
-        compiler_params=pltpu.CompilerParams(vmem_limit_bytes=4 * MIB),
-        name="place_kernel",
-    )(me, *parts)
+    def place(start, blocks, out):
+        return pl.pallas_call(
+            functools.partial(place_kernel, low, size, start),
+            in_specs=[pl.BlockSpec(memory_space=pltpu.SMEM)]
+            + [pl.BlockSpec(memory_space=pl.ANY)] * len(out)
+            + [pl.BlockSpec(memory_space=pltpu.VMEM)] * len(blocks),
+            out_specs=pl.BlockSpec(memory_space=pl.ANY),
+            out_shape=shape((relations * rank, rank), F32),
+            scratch_shapes=[
+                pltpu.VMEM((len(blocks), low * size, rank), F32),
+                pltpu.SemaphoreType.DMA((len(blocks),)),
+            ],
+            input_output_aliases={1: 0} if out else {},
+            compiler_params=pltpu.CompilerParams(vmem_limit_bytes=4 * MIB),
+            name="place_kernel",
+        )(me, *out, *blocks)
+
+    grad_cores = place(0, parts[:1], [])
+    grad_cores = place(1, parts[1:], [grad_cores])
     return grad_factors, grad_cores.reshape(relations, rank, rank)
 
 

time: 57.9 us -> 57.9 us (level)
  waiting for transfers between devices: 17.8 us -> 16.5 us
  Pallas kernels: 11.2 us -> 12.4 us
    ppermute x18, waiting for transfers between devices: 17.8 us -> 16.5 us  [swap(): return lax.ppermute(x, axis, [(i, i ^ distance) for i in range(size)])]
    pallas_call x1 -> x2, Pallas kernels: 1.38 us -> 2.56 us  [place(): pl.pallas_call(functools.partial(place_kernel, low, size, start), in_spec...]
  transfers between devices with their start and end apart: 18 -> 18, of which waited for: 11 -> 11; matrix products, arithmetic and copies ran while one was open for 4% -> 4% of each run, Pallas kernels for 8% -> 10%
where the time goes in v7:
time: 57.9 us; the launch traced here: 57.7 us
  starting transfers between devices  22.6 us (39%)
  waiting for transfers between devices  16.5 us (28%)
  Pallas kernels  12.4 us (21%)
  local copies, waits for them, and re-layouts  5.15 us (9%)
  between operations  0.85 us (1%)
    ppermute x18, starting transfers between devices, swap(): return lax.ppermute(x, axis, [(i, i ^ distance) for i in range(size)])  22.6 us
    ppermute x18, waiting for transfers between devices, swap(): return lax.ppermute(x, axis, [(i, i ^ distance) for i in range(size)])  16.5 us
    unnamed x13, local copies, waits for them, and re-layouts  3.55 us
    pallas_call x1, Pallas kernels, gradients(): late_shares = rows_call(pairs - first)(me, late_err, left, stacked, *nears)  3.29 us
    pallas_call x1, Pallas kernels, gradients(): late_err, *pulls = late_call(me, packed, facts, left, part, *nears)  2.75 us
    pallas_call x2, Pallas kernels, place(): pl.pallas_call(functools.partial(place_kernel, low, size, start), in_spec...  2.56 us
    pallas_call x1, Pallas kernels, gradients(): early_shares = rows_call(first)(me, early_err, left, stacked, column)  1.56 us
    slice x1, local copies, waits for them, and re-layouts, gradients(): packed = observed[:, :half] | jnp.left_shift(observed[:, half:], 16)  1.53 us
  transfers between devices with their start and end apart: 18, of which 11 were waited for; matrix products, arithmetic and copies ran while one was open for 4% of the time, Pallas kernels for 10%

profile of v7, /device:TPU:0, one launch (start us, length us, event | category | flops | bytes accessed | tf_op | source)
XLA Modules:
  0.0 57.7 jit_solution(6986378625504337421)
XLA Ops:
  0.7 5.1 %collective-permute-start.2 = (bf16[128,128]{1,0:T(8,128)(2,1)}, bf16[128,128]{1,0:T(8,128)(2,1)S(1)}, u32[]{:S(2)}, u32[]{:S(2)}) collective-permute-start(bf16[128,128]{1,0:T(8,128)(2,1)} %own_ref.1), channel_id=1, source_target_pairs={{0,12},{1,13},{2,14},{3,15},{4,8},{5,9},{6,10},{7,11},{8,4},{9,5},... | collective-permute-start | bytes 98312 | tf_op jit(solution)/shard_map/ppermute | solution.py:23
  5.8 0.0 collective-permute-start.1
  5.8 0.6 %collective-permute-start = (bf16[128,128]{1,0:T(8,128)(2,1)}, bf16[128,128]{1,0:T(8,128)(2,1)S(1)}, u32[]{:S(2)}, u32[]{:S(2)}) collective-permute-start(bf16[128,128]{1,0:T(8,128)(2,1)} %own_ref.1), channel_id=1, source_target_pairs={{0,4},{1,5},{2,6},{3,7},{4,0},{5,1},{6,2},{7,3},{8,12},{9,13},{10,... | collective-permute-start | bytes 98312 | tf_op jit(solution)/shard_map/ppermute | solution.py:23
  6.4 1.5 %fusion = (s32[8,64,158]{1,0,2:T(8,128)S(1)}, s32[8,64,158]{1,0,2:T(8,128)S(1)}) fusion(s32[8,128,158]{1,0,2:T(8,128)} %param.5), kind=kLoop, calls=%fused_computation.8 | loop fusion | bytes 1294336 | tf_op jit(solution)/shard_map/slice | solution.py:317
  8.0 0.4 copy.10
  8.3 0.3 copy.9
  8.7 0.1 shift-left_or_fusion
  8.9 1.1 %collective-permute-done = bf16[128,128]{1,0:T(8,128)(2,1)S(1)} collective-permute-done((bf16[128,128]{1,0:T(8,128)(2,1)}, bf16[128,128]{1,0:T(8,128)(2,1)S(1)}, u32[]{:S(2)}, u32[]{:S(2)}) %collective-permute-start) | collective-permute-done | bytes 32800 | tf_op jit(solution)/shard_map/ppermute | solution.py:23
  9.9 0.9 %collective-permute-done.1 = bf16[128,128]{1,0:T(8,128)(2,1)S(1)} collective-permute-done((bf16[128,128]{1,0:T(8,128)(2,1)}, bf16[128,128]{1,0:T(8,128)(2,1)S(1)}, u32[]{:S(2)}, u32[]{:S(2)}) %collective-permute-start.1) | collective-permute-done | bytes 32800 | tf_op jit(solution)/shard_map/ppermute | solution.py:23
  10.8 2.5 %collective-permute-start.5 = (bf16[512,128]{1,0:T(8,128)(2,1)S(1)}, bf16[512,128]{1,0:T(8,128)(2,1)S(1)}, u32[]{:S(2)}, u32[]{:S(2)}) collective-permute-start(bf16[512,128]{1,0:T(8,128)(2,1)S(1)} %constant_dynamic-update-slice_fusion.column_ref.rest_0_), channel_id=1, source_target_pairs={{0,3},{1,2},{2,1},{3,0},{4,7},{5,6},{6,5},{7,4},{8,11},{9,10},{10,... | collective-permute-start | bytes 393224 | tf_op jit(solution)/shard_map/ppermute | solution.py:23
  13.4 0.5 collective-permute-start.4
  13.9 0.5 collective-permute-start.3
  14.4 0.1 pad_add_fusion.me_ref
  14.5 2.2 %copy-done = bf16[8,128,2048]{2,1,0:T(8,128)(2,1)S(1)} copy-done((bf16[8,128,2048]{2,1,0:T(8,128)(2,1)S(1)}, bf16[8,128,2048]{2,1,0:T(8,128)(2,1)}, u32[]{:S(2)}) %copy-start) | copy-done | bytes 4194328
  16.7 1.5 %early_kernel.1 = (bf16[2,1024,256]{2,1,0:T(8,128)(2,1)S(1)}, bf16[1024,128]{1,0:T(8,128)(2,1)S(1)}, f32[1024,128]{1,0:T(8,128)S(1)}) custom-call(s32[2]{0:T(128)S(1)} %pad_add_fusion.me_ref, s32[8,64,256]{2,1,0:T(8,128)S(1)} %pad.4.words_ref, bf16[8,128,2048]{2,1,0:T(8,128)(2,1)S(1)} %copy-done, bf16[128,128]{1,0:T(8,128)(2,1)S(1)} %copy-done.2, ...), custom_call_target="tpu_custom_call" | custom-call | flops 268435456 | bytes 2097152 | tf_op jit(solution)/shard_map/early_kernel/pallas_call | solution.py:347
  18.2 0.0 collective-permute-done.5.rest_2_
  18.2 0.8 %collective-permute-done.4.rest_1_ = bf16[512,128]{1,0:T(8,128)(2,1)S(1)} collective-permute-done((bf16[512,128]{1,0:T(8,128)(2,1)S(1)}, bf16[512,128]{1,0:T(8,128)(2,1)S(1)}, u32[]{:S(2)}, u32[]{:S(2)}) %collective-permute-start.4) | collective-permute-done | bytes 131104 | tf_op jit(solution)/shard_map/ppermute | solution.py:23
  19.0 2.7 %late_kernel.1 = (bf16[6,1024,256]{2,1,0:T(8,128)(2,1)S(1)}, bf16[256,128]{1,0:T(8,128)(2,1)S(1)}, bf16[256,128]{1,0:T(8,128)(2,1)S(1)}, bf16[256,128]{1,0:T(8,128)(2,1)S(1)}, bf16[256,128]{1,0:T(8,128)(2,1)S(1)}) custom-call(s32[2]{0:T(128)S(1)} %pad_add_fusion.me_ref, s32[8,64,256]{2,1,0:T(8,128)S(1)} %pad.4.words_ref, bf16[8,128,2048]{2,1,0:T(8,128)(2,1)S(1)} %copy-done, ...), custom_call_target="tpu_custom_call" | custom-call | flops 805306368 | bytes 6291456 | tf_op jit(solution)/shard_map/late_kernel/pallas_call | solution.py:377
  21.7 3.3 %rows_kernel.3 = (f32[832,128]{1,0:T(8,128)S(1)}, f32[832,128]{1,0:T(8,128)S(1)}) custom-call(s32[2]{0:T(128)S(1)} %pad_add_fusion.me_ref, bf16[6,1024,256]{2,1,0:T(8,128)(2,1)S(1)} %get-tuple-element.31.err_ref, bf16[1024,128]{1,0:T(8,128)(2,1)S(1)} %get-tuple-element.22.left_ref, bf16[1024,128]{1,0:T(8,128)(2,1)S(1)} %bitcast.9, ...), custom_call_target="tpu_custom_call" | custom-call | flops 1207959552 | bytes 9437184 | tf_op jit(solution)/shard_map/rows_kernel/pallas_call | solution.py:380
  25.0 0.1 collective-permute-start.10
  25.1 1.6 %rows_kernel.2 = (f32[320,128]{1,0:T(8,128)S(1)}, f32[320,128]{1,0:T(8,128)S(1)}) custom-call(s32[2]{0:T(128)S(1)} %pad_add_fusion.me_ref, bf16[2,1024,256]{2,1,0:T(8,128)(2,1)S(1)} %get-tuple-element.28.err_ref, bf16[1024,128]{1,0:T(8,128)(2,1)S(1)} %get-tuple-element.22.left_ref, bf16[1024,128]{1,0:T(8,128)(2,1)S(1)} %bitcast.10, ...), custom_call_target="tpu_custom_call" | custom-call | flops 402653184 | bytes 3145728 | tf_op jit(solution)/shard_map/rows_kernel/pallas_call | solution.py:364
  26.7 0.6 collective-permute-start.9
  27.2 0.0 collective-permute-start.6
  27.2 2.5 %collective-permute-start.7 = (bf16[256,128]{1,0:T(8,128)(2,1)S(1)}, bf16[256,128]{1,0:T(8,128)(2,1)S(1)}, u32[]{:S(2)}, u32[]{:S(2)}) collective-permute-start(bf16[256,128]{1,0:T(8,128)(2,1)S(1)} %get-tuple-element.26), channel_id=1, source_target_pairs={{0,8},{1,9},{2,10},{3,11},{4,12},{5,13},{6,14},{7,15},{8,0},{9,1},... | collective-permute-start | bytes 196616 | tf_op jit(solution)/shard_map/ppermute | solution.py:23
  29.8 1.8 %collective-permute-start.8 = (bf16[256,128]{1,0:T(8,128)(2,1)S(1)}, bf16[256,128]{1,0:T(8,128)(2,1)S(1)}, u32[]{:S(2)}, u32[]{:S(2)}) collective-permute-start(bf16[256,128]{1,0:T(8,128)(2,1)S(1)} %get-tuple-element.27), channel_id=1, source_target_pairs={{0,12},{1,13},{2,14},{3,15},{4,8},{5,9},{6,10},{7,11},{8,4},{9,5},... | collective-permute-start | bytes 196616 | tf_op jit(solution)/shard_map/ppermute | solution.py:23
  31.6 1.3 %collective-permute-done.6.rest_1_ = bf16[256,128]{1,0:T(8,128)(2,1)S(1)} collective-permute-done((bf16[256,128]{1,0:T(8,128)(2,1)S(1)}, bf16[256,128]{1,0:T(8,128)(2,1)S(1)}, u32[]{:S(2)}, u32[]{:S(2)}) %collective-permute-start.6) | collective-permute-done | bytes 65568 | tf_op jit(solution)/shard_map/ppermute | solution.py:23
  32.9 0.0 collective-permute-done.7.rest_2_
  32.9 2.9 %collective-permute-done.8.rest_3_ = bf16[256,128]{1,0:T(8,128)(2,1)S(1)} collective-permute-done((bf16[256,128]{1,0:T(8,128)(2,1)S(1)}, bf16[256,128]{1,0:T(8,128)(2,1)S(1)}, u32[]{:S(2)}, u32[]{:S(2)}) %collective-permute-start.8) | collective-permute-done | bytes 65568 | tf_op jit(solution)/shard_map/ppermute | solution.py:23
  35.8 0.3 core_kernel.1.core_ref
  36.2 0.2 merge_kernel.1
  36.4 1.5 %collective-permute-start.12 = (s16[528,128]{1,0:T(8,128)(2,1)S(1)}, s16[528,128]{1,0:T(8,128)(2,1)S(1)}, u32[]{:S(2)}, u32[]{:S(2)}) collective-permute-start(s16[528,128]{1,0:T(8,128)(2,1)S(1)} %get-tuple-element.36), channel_id=1, source_target_pairs={{0,2},{1,3},{2,0},{3,1},{4,6},{5,7},{6,4},{7,5},{8,10},{9,11},{10,... | collective-permute-start | bytes 405512 | tf_op jit(solution)/shard_map/ppermute | solution.py:23
  37.9 1.6 %collective-permute-start.13 = (s16[528,128]{1,0:T(8,128)(2,1)S(1)}, s16[528,128]{1,0:T(8,128)(2,1)S(1)}, u32[]{:S(2)}, u32[]{:S(2)}) collective-permute-start(s16[528,128]{1,0:T(8,128)(2,1)S(1)} %get-tuple-element.37), channel_id=1, source_target_pairs={{0,3},{1,2},{2,1},{3,0},{4,7},{5,6},{6,5},{7,4},{8,11},{9,10},{10,... | collective-permute-start | bytes 405512 | tf_op jit(solution)/shard_map/ppermute | solution.py:23
  39.5 0.4 collective-permute-start.11
  39.9 3.4 %collective-permute-done.12.rest_3_ = s16[528,128]{1,0:T(8,128)(2,1)S(1)} collective-permute-done((s16[528,128]{1,0:T(8,128)(2,1)S(1)}, s16[528,128]{1,0:T(8,128)(2,1)S(1)}, u32[]{:S(2)}, u32[]{:S(2)}) %collective-permute-start.12) | collective-permute-done | bytes 135200 | tf_op jit(solution)/shard_map/ppermute | solution.py:23
  43.4 0.9 %collective-permute-done.13.rest_4_ = s16[528,128]{1,0:T(8,128)(2,1)S(1)} collective-permute-done((s16[528,128]{1,0:T(8,128)(2,1)S(1)}, s16[528,128]{1,0:T(8,128)(2,1)S(1)}, u32[]{:S(2)}, u32[]{:S(2)}) %collective-permute-start.13) | collective-permute-done | bytes 135200 | tf_op jit(solution)/shard_map/ppermute | solution.py:23
  44.3 0.6 %collective-permute-done.11.rest_2_ = s16[528,128]{1,0:T(8,128)(2,1)S(1)} collective-permute-done((s16[528,128]{1,0:T(8,128)(2,1)S(1)}, s16[528,128]{1,0:T(8,128)(2,1)S(1)}, u32[]{:S(2)}, u32[]{:S(2)}) %collective-permute-start.11) | collective-permute-done | bytes 135200 | tf_op jit(solution)/shard_map/ppermute | solution.py:23
  44.9 0.2 near_kernel.1
  45.2 3.7 %collective-permute-start.15 = (s16[336,128]{1,0:T(8,128)(2,1)S(1)}, s16[336,128]{1,0:T(8,128)(2,1)S(1)}, u32[]{:S(2)}, u32[]{:S(2)}) collective-permute-start(s16[336,128]{1,0:T(8,128)(2,1)S(1)} %get-tuple-element.40), channel_id=1, source_target_pairs={{0,8},{1,9},{2,10},{3,11},{4,12},{5,13},{6,14},{7,15},{8,0},{9,1},... | collective-permute-start | bytes 258056 | tf_op jit(solution)/shard_map/ppermute | solution.py:23
  48.8 0.9 %collective-permute-start.16 = (s16[336,128]{1,0:T(8,128)(2,1)S(1)}, s16[336,128]{1,0:T(8,128)(2,1)S(1)}, u32[]{:S(2)}, u32[]{:S(2)}) collective-permute-start(s16[336,128]{1,0:T(8,128)(2,1)S(1)} %get-tuple-element.41), channel_id=1, source_target_pairs={{0,12},{1,13},{2,14},{3,15},{4,8},{5,9},{6,10},{7,11},{8,4},{9,5},... | collective-permute-start | bytes 258056 | tf_op jit(solution)/shard_map/ppermute | solution.py:23
  49.8 0.0 collective-permute-start.14
  49.8 1.2 %place_kernel.2.rest_0_ = f32[1024,128]{1,0:T(8,128)} custom-call(s32[2]{0:T(128)S(1)} %pad_add_fusion.me_ref, s16[336,128]{1,0:T(8,128)(2,1)S(1)} %get-tuple-element.39.rest_0_), custom_call_target="tpu_custom_call" | custom-call | tf_op jit(solution)/shard_map/place_kernel/pallas_call | solution.py:428
  51.0 2.9 %collective-permute-done.15.rest_1_.rest_2_ = s16[336,128]{1,0:T(8,128)(2,1)S(1)} collective-permute-done((s16[336,128]{1,0:T(8,128)(2,1)S(1)}, s16[336,128]{1,0:T(8,128)(2,1)S(1)}, u32[]{:S(2)}, u32[]{:S(2)}) %collective-permute-start.15) | collective-permute-done | bytes 86048 | tf_op jit(solution)/shard_map/ppermute | solution.py:23
  53.9 1.3 %collective-permute-done.16.rest_2_.rest_3_ = s16[336,128]{1,0:T(8,128)(2,1)S(1)} collective-permute-done((s16[336,128]{1,0:T(8,128)(2,1)S(1)}, s16[336,128]{1,0:T(8,128)(2,1)S(1)}, u32[]{:S(2)}, u32[]{:S(2)}) %collective-permute-start.16) | collective-permute-done | bytes 86048 | tf_op jit(solution)/shard_map/ppermute | solution.py:23
  55.2 0.3 collective-permute-done.14.rest_0_.rest_1_
  55.6 0.1 collective-permute-start.17
  55.7 1.3 %place_kernel.3 = f32[1024,128]{1,0:T(8,128)} custom-call(s32[2]{0:T(128)S(1)} %pad_add_fusion.me_ref, f32[1024,128]{1,0:T(8,128)} %place_kernel.2.rest_0_, s16[336,128]{1,0:T(8,128)(2,1)S(1)} %collective-permute-done.14.rest_0_.rest_1_, s16[336,128]{1,0:T(8,128)(2,1)S(1)} %collective-permute-done.15.rest_1_.rest_2_, ...), custom_call_target="tpu_custom_call", output_to_operand_aliasing={{}: (1, {})} | custom-call | tf_op jit(solution)/shard_map/place_kernel/pallas_call | solution.py:428
  57.0 0.0 copy-start.3
  57.1 0.6 %copy-done.3 = f32[2,64,128]{2,1,0:T(8,128)} copy-done((f32[2,64,128]{2,1,0:T(8,128)}, f32[2,64,128]{2,1,0:T(8,128)S(1)}, u32[]{:S(2)}) %copy-start.3) | copy-done | bytes 65560
  (19 shorter events, 0.1 us)
Async XLA Ops:
  0.6 8.2 %copy-start.2 = (bf16[128,128]{1,0:T(8,128)(2,1)S(1)}, bf16[128,128]{1,0:T(8,128)(2,1)}, u32[]{:S(2)}) copy-start(bf16[128,128]{1,0:T(8,128)(2,1)} %own_ref.1) | copy-start | bytes 98308
  0.6 13.8 %copy-start.1 = (bf16[8,128,128]{2,1,0:T(8,128)(2,1)S(1)}, bf16[8,128,128]{2,1,0:T(8,128)(2,1)}, u32[]{:S(2)}) copy-start(bf16[8,128,128]{2,1,0:T(8,128)(2,1)} %cores_ref.1) | copy-start | bytes 786436
  0.7 10.2 %collective-permute-start.2 = (bf16[128,128]{1,0:T(8,128)(2,1)}, bf16[128,128]{1,0:T(8,128)(2,1)S(1)}, u32[]{:S(2)}, u32[]{:S(2)}) collective-permute-start(bf16[128,128]{1,0:T(8,128)(2,1)} %own_ref.1), channel_id=1, source_target_pairs={{0,12},{1,13},{2,14},{3,15},{4,8},{5,9},{6,10},{7,11},{8,4},{9,5},... | collective-permute-start | bytes 98312 | tf_op jit(solution)/shard_map/ppermute | solution.py:23
  5.8 5.0 %collective-permute-start.1 = (bf16[128,128]{1,0:T(8,128)(2,1)}, bf16[128,128]{1,0:T(8,128)(2,1)S(1)}, u32[]{:S(2)}, u32[]{:S(2)}) collective-permute-start(bf16[128,128]{1,0:T(8,128)(2,1)} %own_ref.1), channel_id=1, source_target_pairs={{0,8},{1,9},{2,10},{3,11},{4,12},{5,13},{6,14},{7,15},{8,0},{9,1},... | collective-permute-start | bytes 98312 | tf_op jit(solution)/shard_map/ppermute | solution.py:23
  5.8 4.1 %collective-permute-start = (bf16[128,128]{1,0:T(8,128)(2,1)}, bf16[128,128]{1,0:T(8,128)(2,1)S(1)}, u32[]{:S(2)}, u32[]{:S(2)}) collective-permute-start(bf16[128,128]{1,0:T(8,128)(2,1)} %own_ref.1), channel_id=1, source_target_pairs={{0,4},{1,5},{2,6},{3,7},{4,0},{5,1},{6,2},{7,3},{8,12},{9,13},{10,... | collective-permute-start | bytes 98312 | tf_op jit(solution)/shard_map/ppermute | solution.py:23
  10.8 7.3 %collective-permute-start.5 = (bf16[512,128]{1,0:T(8,128)(2,1)S(1)}, bf16[512,128]{1,0:T(8,128)(2,1)S(1)}, u32[]{:S(2)}, u32[]{:S(2)}) collective-permute-start(bf16[512,128]{1,0:T(8,128)(2,1)S(1)} %constant_dynamic-update-slice_fusion.column_ref.rest_0_), channel_id=1, source_target_pairs={{0,3},{1,2},{2,1},{3,0},{4,7},{5,6},{6,5},{7,4},{8,11},{9,10},{10,... | collective-permute-start | bytes 393224 | tf_op jit(solution)/shard_map/ppermute | solution.py:23
  13.4 5.6 %collective-permute-start.4 = (bf16[512,128]{1,0:T(8,128)(2,1)S(1)}, bf16[512,128]{1,0:T(8,128)(2,1)S(1)}, u32[]{:S(2)}, u32[]{:S(2)}) collective-permute-start(bf16[512,128]{1,0:T(8,128)(2,1)S(1)} %constant_dynamic-update-slice_fusion.column_ref.rest_0_), channel_id=1, source_target_pairs={{0,2},{1,3},{2,0},{3,1},{4,6},{5,7},{6,4},{7,5},{8,10},{9,11},{10,... | collective-permute-start | bytes 393224 | tf_op jit(solution)/shard_map/ppermute | solution.py:23
  13.9 5.1 %collective-permute-start.3 = (bf16[512,128]{1,0:T(8,128)(2,1)S(1)}, bf16[512,128]{1,0:T(8,128)(2,1)S(1)}, u32[]{:S(2)}, u32[]{:S(2)}) collective-permute-start(bf16[512,128]{1,0:T(8,128)(2,1)S(1)} %constant_dynamic-update-slice_fusion.column_ref.rest_0_), channel_id=1, source_target_pairs={{0,1},{1,0},{2,3},{3,2},{4,5},{5,4},{6,7},{7,6},{8,9},{9,8},{10,11... | collective-permute-start | bytes 393224 | tf_op jit(solution)/shard_map/ppermute | solution.py:23
  14.5 2.2 %copy-start = (bf16[8,128,2048]{2,1,0:T(8,128)(2,1)S(1)}, bf16[8,128,2048]{2,1,0:T(8,128)(2,1)}, u32[]{:S(2)}) copy-start(bf16[8,128,2048]{2,1,0:T(8,128)(2,1)} %facts_ref.3) | copy-start | bytes 12582916
  25.0 11.2 %collective-permute-start.10 = (f32[832,128]{1,0:T(8,128)S(1)}, f32[832,128]{1,0:T(8,128)S(1)}, u32[]{:S(2)}, u32[]{:S(2)}) collective-permute-start(f32[832,128]{1,0:T(8,128)S(1)} %get-tuple-element.33), channel_id=1, source_target_pairs={{0,16},{16,0},{1,17},{17,1},{2,18},{18,2},{3,19},{19,3},{4,20},{20... | collective-permute-start | bytes 1277960 | tf_op jit(solution)/shard_map/ppermute | solution.py:23
  26.7 9.5 %collective-permute-start.9 = (f32[320,128]{1,0:T(8,128)S(1)}, f32[320,128]{1,0:T(8,128)S(1)}, u32[]{:S(2)}, u32[]{:S(2)}) collective-permute-start(f32[320,128]{1,0:T(8,128)S(1)} %get-tuple-element.30), channel_id=1, source_target_pairs={{0,16},{16,0},{1,17},{17,1},{2,18},{18,2},{3,19},{19,3},{4,20},{20... | collective-permute-start | bytes 491528 | tf_op jit(solution)/shard_map/ppermute | solution.py:23
  27.2 5.7 %collective-permute-start.6 = (bf16[256,128]{1,0:T(8,128)(2,1)S(1)}, bf16[256,128]{1,0:T(8,128)(2,1)S(1)}, u32[]{:S(2)}, u32[]{:S(2)}) collective-permute-start(bf16[256,128]{1,0:T(8,128)(2,1)S(1)} %get-tuple-element.25), channel_id=1, source_target_pairs={{0,4},{1,5},{2,6},{3,7},{4,0},{5,1},{6,2},{7,3},{8,12},{9,13},{10,... | collective-permute-start | bytes 196616 | tf_op jit(solution)/shard_map/ppermute | solution.py:23
  27.2 5.7 %collective-permute-start.7 = (bf16[256,128]{1,0:T(8,128)(2,1)S(1)}, bf16[256,128]{1,0:T(8,128)(2,1)S(1)}, u32[]{:S(2)}, u32[]{:S(2)}) collective-permute-start(bf16[256,128]{1,0:T(8,128)(2,1)S(1)} %get-tuple-element.26), channel_id=1, source_target_pairs={{0,8},{1,9},{2,10},{3,11},{4,12},{5,13},{6,14},{7,15},{8,0},{9,1},... | collective-permute-start | bytes 196616 | tf_op jit(solution)/shard_map/ppermute | solution.py:23
  29.8 6.1 %collective-permute-start.8 = (bf16[256,128]{1,0:T(8,128)(2,1)S(1)}, bf16[256,128]{1,0:T(8,128)(2,1)S(1)}, u32[]{:S(2)}, u32[]{:S(2)}) collective-permute-start(bf16[256,128]{1,0:T(8,128)(2,1)S(1)} %get-tuple-element.27), channel_id=1, source_target_pairs={{0,12},{1,13},{2,14},{3,15},{4,8},{5,9},{6,10},{7,11},{8,4},{9,5},... | collective-permute-start | bytes 196616 | tf_op jit(solution)/shard_map/ppermute | solution.py:23
  36.4 7.0 %collective-permute-start.12 = (s16[528,128]{1,0:T(8,128)(2,1)S(1)}, s16[528,128]{1,0:T(8,128)(2,1)S(1)}, u32[]{:S(2)}, u32[]{:S(2)}) collective-permute-start(s16[528,128]{1,0:T(8,128)(2,1)S(1)} %get-tuple-element.36), channel_id=1, source_target_pairs={{0,2},{1,3},{2,0},{3,1},{4,6},{5,7},{6,4},{7,5},{8,10},{9,11},{10,... | collective-permute-start | bytes 405512 | tf_op jit(solution)/shard_map/ppermute | solution.py:23
  37.9 6.4 %collective-permute-start.13 = (s16[528,128]{1,0:T(8,128)(2,1)S(1)}, s16[528,128]{1,0:T(8,128)(2,1)S(1)}, u32[]{:S(2)}, u32[]{:S(2)}) collective-permute-start(s16[528,128]{1,0:T(8,128)(2,1)S(1)} %get-tuple-element.37), channel_id=1, source_target_pairs={{0,3},{1,2},{2,1},{3,0},{4,7},{5,6},{6,5},{7,4},{8,11},{9,10},{10,... | collective-permute-start | bytes 405512 | tf_op jit(solution)/shard_map/ppermute | solution.py:23
  39.5 5.4 %collective-permute-start.11 = (s16[528,128]{1,0:T(8,128)(2,1)S(1)}, s16[528,128]{1,0:T(8,128)(2,1)S(1)}, u32[]{:S(2)}, u32[]{:S(2)}) collective-permute-start(s16[528,128]{1,0:T(8,128)(2,1)S(1)} %get-tuple-element.35.rest_1_), channel_id=1, source_target_pairs={{0,1},{1,0},{2,3},{3,2},{4,5},{5,4},{6,7},{7,6},{8,9},{9,8},{10,11... | collective-permute-start | bytes 405512 | tf_op jit(solution)/shard_map/ppermute | solution.py:23
  45.2 8.7 %collective-permute-start.15 = (s16[336,128]{1,0:T(8,128)(2,1)S(1)}, s16[336,128]{1,0:T(8,128)(2,1)S(1)}, u32[]{:S(2)}, u32[]{:S(2)}) collective-permute-start(s16[336,128]{1,0:T(8,128)(2,1)S(1)} %get-tuple-element.40), channel_id=1, source_target_pairs={{0,8},{1,9},{2,10},{3,11},{4,12},{5,13},{6,14},{7,15},{8,0},{9,1},... | collective-permute-start | bytes 258056 | tf_op jit(solution)/shard_map/ppermute | solution.py:23
  48.8 6.4 %collective-permute-start.16 = (s16[336,128]{1,0:T(8,128)(2,1)S(1)}, s16[336,128]{1,0:T(8,128)(2,1)S(1)}, u32[]{:S(2)}, u32[]{:S(2)}) collective-permute-start(s16[336,128]{1,0:T(8,128)(2,1)S(1)} %get-tuple-element.41), channel_id=1, source_target_pairs={{0,12},{1,13},{2,14},{3,15},{4,8},{5,9},{6,10},{7,11},{8,4},{9,5},... | collective-permute-start | bytes 258056 | tf_op jit(solution)/shard_map/ppermute | solution.py:23
  49.8 5.8 %collective-permute-start.14 = (s16[336,128]{1,0:T(8,128)(2,1)S(1)}, s16[336,128]{1,0:T(8,128)(2,1)S(1)}, u32[]{:S(2)}, u32[]{:S(2)}) collective-permute-start(s16[336,128]{1,0:T(8,128)(2,1)S(1)} %get-tuple-element.39.rest_0_), channel_id=1, source_target_pairs={{0,4},{1,5},{2,6},{3,7},{4,0},{5,1},{6,2},{7,3},{8,12},{9,13},{10,... | collective-permute-start | bytes 258056 | tf_op jit(solution)/shard_map/ppermute | solution.py:23
  55.6 1.5 %collective-permute-start.17 = (f32[64,128]{1,0:T(8,128)S(1)}, f32[64,128]{1,0:T(8,128)S(1)}, u32[]{:S(2)}, u32[]{:S(2)}) collective-permute-start(f32[64,128]{1,0:T(8,128)S(1)} %far_kernel.1), channel_id=1, source_target_pairs={{0,16},{16,0},{1,17},{17,1},{2,18},{18,2},{3,19},{19,3},{4,20},{20... | collective-permute-start | bytes 98312 | tf_op jit(solution)/shard_map/ppermute | solution.py:23
  57.0 0.6 %copy-start.3 = (f32[2,64,128]{2,1,0:T(8,128)}, f32[2,64,128]{2,1,0:T(8,128)S(1)}, u32[]{:S(2)}) copy-start(f32[2,64,128]{2,1,0:T(8,128)S(1)} %bitcast_dynamic-update-slice_fusion) | copy-start | bytes 196612
